TPU v7x, 256 devices: a whole 4x4x8 slice. The times are simulated.
256 devices in a mesh: expert: 64 (over z, y, core), etp: 4 (over x).
Axes of the slice: x: 4, y: 4, z: 8, core: 2. Of those that a mesh axis runs over, the one named last changes fastest.
Arguments:
- tokens: bfloat16 [32768, 2560], P(('expert', 'etp')), may hold values from -6 to 6
- hidden_grad: bfloat16 [32768, 4096], P(('expert', 'etp')), may hold values from -6 to 6
- routes: int32 [32768, 1], P(('expert', 'etp')), may hold values from 0 to 63; in each aligned block of 512 rows (0 to 511, 512 to 1023, ...) at most 10 rows name the same one
- exponents: int32 [32768], P(('expert', 'etp')), may hold values from -2 to 2
- gate_weight: bfloat16 [64, 2560, 4096], P('expert', None, 'etp'), may hold values from -0.125 to 0.125
- up_weight: bfloat16 [64, 2560, 4096], P('expert', None, 'etp'), may hold values from -0.125 to 0.125
Outputs:
- input_grad: bfloat16 [32768, 2560], P(('expert', 'etp'))
Inputs may be any that keep to these rules, and one draw needn't show every extreme that they name: `routes`: in each aligned block of 512 rows (the tokens of one group of devices along etp) no expert is named by more than 10 rows, and in every draw some expert is named by exactly 10 rows of some block.
All inputs are finite; a program needn't handle non-finite values.
Results may differ from a plain program's by a relative error of at most 0.0095.
Values may be sent and summed in bfloat16 or wider, within the bound.
No kernel may reach another device: no remote copies, remote signals or barrier semaphores. Data moves between devices by JAX's collectives and lax.ppermute only.
A program may use at most 128 MiB of HBM per device.

v0:
```python
import jax
import jax.numpy as jnp
from jax import lax
from jax.sharding import PartitionSpec as P


def on_device(tokens, hidden_grad, routes, exponents, gate_weight, up_weight):
    feature_count = tokens.shape[1]
    local_experts = gate_weight.shape[0]
    experts = local_experts * lax.axis_size("expert")
    group_tokens, group_routes, group_expo = (
        lax.all_gather(tokens, "etp", axis=0, tiled=True),
        lax.all_gather(routes[:, 0], "etp", axis=0, tiled=True),
        lax.all_gather(exponents, "etp", axis=0, tiled=True),
    )
    group_hidden = lax.all_to_all(hidden_grad, "etp", split_axis=1, concat_axis=0, tiled=True)
    group_size = group_tokens.shape[0]
    hidden_local = group_hidden.shape[1]
    capacity = max(2, 5 * group_size // (4 * experts))
    onehot = (group_routes[:, None] == jnp.arange(experts, dtype=jnp.int32)[None, :]).astype(
        jnp.int32
    )
    ranking = jnp.sum((jnp.cumsum(onehot, axis=0) - 1) * onehot, axis=1)
    slot_index = (group_routes * capacity + ranking).astype(jnp.int32)
    slot_owner = (
        jnp.full((experts * capacity,), group_size, jnp.int32)
        .at[slot_index]
        .set(jnp.arange(group_size, dtype=jnp.int32))
    )
    padded_tokens = jnp.concatenate(
        [group_tokens, jnp.zeros((1, feature_count), jnp.bfloat16)], axis=0
    )
    padded_hidden = jnp.concatenate(
        [group_hidden, jnp.zeros((1, hidden_local), jnp.bfloat16)], axis=0
    )
    padded_expo = jnp.concatenate([group_expo, jnp.zeros((1,), jnp.int32)], axis=0)
    packed_tokens = padded_tokens[slot_owner].reshape(experts, capacity, feature_count)
    packed_hidden = padded_hidden[slot_owner].reshape(experts, capacity, hidden_local)
    packed_expo = padded_expo[slot_owner].reshape(experts, capacity)
    arrived_tokens = lax.all_to_all(
        packed_tokens, "expert", split_axis=0, concat_axis=0, tiled=True
    )
    arrived_hidden = lax.all_to_all(
        packed_hidden, "expert", split_axis=0, concat_axis=0, tiled=True
    )
    arrived_expo = lax.all_to_all(packed_expo, "expert", split_axis=0, concat_axis=0, tiled=True)
    sources = arrived_tokens.shape[0] // local_experts
    slot_count = arrived_tokens.shape[1]
    tokens_split = arrived_tokens.reshape(sources, local_experts, slot_count, feature_count)
    hidden_split = arrived_hidden.reshape(sources, local_experts, slot_count, hidden_local)
    expo_split = arrived_expo.reshape(sources, local_experts, slot_count)
    gate_pre = jnp.einsum(
        "slmd,ldf->slmf", tokens_split, gate_weight, preferred_element_type=jnp.float32
    )
    up_pre = jnp.einsum(
        "slmd,ldf->slmf", tokens_split, up_weight, preferred_element_type=jnp.float32
    )
    scaled_grad = (
        hidden_split.astype(jnp.float32) * jnp.exp2(expo_split.astype(jnp.float32))[..., None]
    )
    sigmoid_gate = jax.nn.sigmoid(gate_pre)
    grad_gate = (
        scaled_grad * up_pre * sigmoid_gate * (1.0 + gate_pre * (1.0 - sigmoid_gate))
    ).astype(jnp.bfloat16)
    grad_up = (scaled_grad * gate_pre * sigmoid_gate).astype(jnp.bfloat16)
    partial_value = jnp.einsum(
        "slmf,ldf->slmd", grad_gate, gate_weight, preferred_element_type=jnp.float32
    )
    partial_value = partial_value + jnp.einsum(
        "slmf,ldf->slmd", grad_up, up_weight, preferred_element_type=jnp.float32
    )
    partial_value = partial_value.reshape(sources * local_experts, slot_count, feature_count)
    returned = lax.all_to_all(
        partial_value.astype(jnp.bfloat16), "expert", split_axis=0, concat_axis=0, tiled=True
    )
    token_rows = returned.reshape(experts * capacity, feature_count)[slot_index]
    result = lax.psum_scatter(
        token_rows.astype(jnp.float32).astype(jnp.bfloat16), "etp", scatter_dimension=0, tiled=True
    )
    return result


def solution(mesh):
    placed = (
        P(("expert", "etp"), None),
        P(("expert", "etp"), None),
        P(("expert", "etp"), None),
        P(("expert", "etp")),
        P("expert", None, "etp"),
        P("expert", None, "etp"),
    )
    return jax.shard_map(
        on_device, mesh=mesh, in_specs=placed, out_specs=P(("expert", "etp"), None), check_vma=False
    )
```

profile of v0, /device:TPU:8, one launch (start us, length us, event | category | flops | bytes accessed | tf_op | source)
XLA Modules:
  0.0 454.6 jit_solution(6448953205632328921)
XLA Ops:
  6.5 0.0 all-gather.4.cloned.1.call-start
  6.5 0.7 all-gather.4.cloned.1.call-update
  7.3 0.0 copy-start
  7.3 10.0 %all-gather = s32[512,1]{0,1:T(1,128)S(1)} all-gather(s32[128,1]{0,1:T(1,128)} %param.8), channel_id=2, replica_groups=mesh['expert'=64,'etp'=4] {'etp'}, dimensions={0}, use_global_device_ids=true | all-gather | bytes 2560 | tf_op jit(solution)/shard_map/all_gather | solution.py:13
  17.3 1.2 reduce-window.6
  18.5 0.2 slice_reduce_fusion
  18.7 0.1 fusion.35
  18.9 2.4 scatter_custom_fusion
  21.3 7.2 %all-gather.1 = s32[4,1,128]{2,1,0:T(1,128)S(1)} all-gather(s32[1,1,128]{2,1,0:T(1,128)} %bitcast.111), channel_id=1, replica_groups=mesh['expert'=64,'etp'=4] {'etp'}, dimensions={0}, use_global_device_ids=true | all-gather | bytes 2560 | tf_op jit(solution)/shard_map/all_gather | solution.py:14
  28.5 2.8 gather_fusion.1
  31.3 0.7 all_to_all.34
  32.1 12.1 %all-to-all-start.2 = ((s32[64,1,10]{2,1,0:T(1,128)}), s32[64,1,10]{2,1,0:T(1,128)S(1)}, u32[]{:S(2)}, u32[]{:S(2)}) async-start(s32[64,1,10]{2,1,0:T(1,128)} %bitcast.7), calls=%async_computation.2 | async-start | bytes 65536 | tf_op jit(solution)/shard_map/all_to_all | solution.py:46
  44.2 0.0 copy-done
  44.2 1.1 copy.39
  45.3 7.4 %all-to-all-done.2 = s32[64,1,10]{2,1,0:T(1,128)S(1)} async-done(((s32[64,1,10]{2,1,0:T(1,128)}), s32[64,1,10]{2,1,0:T(1,128)S(1)}, u32[]{:S(2)}, u32[]{:S(2)}) %all-to-all-start.2) | async-done | bytes 2592 | tf_op jit(solution)/shard_map/all_to_all | solution.py:46
  52.7 4.3 all-to-all-start
  57.0 0.0 all-gather.4.cloned.1.call-done
  57.0 1.9 concatenate.11
  58.9 4.3 gather_fusion.2
  63.2 6.9 %reshape.73 = bf16[64,10,2560]{2,1,0:T(8,128)(2,1)} reshape(bf16[640,2560]{1,0:T(8,128)(2,1)} %gather_fusion.2) | data formatting | bytes 6553600 | tf_op jit(solution)/shard_map/reshape | solution.py:37
  70.1 2.3 all-to-all-done
  72.4 6.5 %all-to-all-start.3 = ((bf16[64,10,2560]{2,1,0:T(8,128)(2,1)}), bf16[64,10,2560]{2,1,0:T(8,128)(2,1)}, u32[]{:S(2)}, u32[]{:S(2)}) async-start(bf16[64,10,2560]{2,1,0:T(8,128)(2,1)} %reshape.73), calls=%async_computation.3 | async-start | bytes 10485760 | tf_op jit(solution)/shard_map/all_to_all | solution.py:40
  78.9 1.3 concatenate.9
  80.2 2.8 gather_fusion
  83.1 1.5 reshape.72
  84.6 113.1 %all-to-all-done.3 = bf16[64,10,2560]{2,1,0:T(8,128)(2,1)} async-done(((bf16[64,10,2560]{2,1,0:T(8,128)(2,1)}), bf16[64,10,2560]{2,1,0:T(8,128)(2,1)}, u32[]{:S(2)}, u32[]{:S(2)}) %all-to-all-start.3) | async-done | bytes 3276832 | tf_op jit(solution)/shard_map/all_to_all | solution.py:40
  197.7 5.5 %all-to-all-start.1 = ((bf16[64,10,1024]{2,1,0:T(8,128)(2,1)}), bf16[64,10,1024]{2,1,0:T(8,128)(2,1)S(1)}, u32[]{:S(2)}, u32[]{:S(2)}) async-start(bf16[64,10,1024]{2,1,0:T(8,128)(2,1)} %reshape.72), calls=%async_computation.1 | async-start | bytes 4194304 | tf_op jit(solution)/shard_map/all_to_all | solution.py:43
  203.2 0.1 multiply_exponential_fusion
  203.2 0.1 copy.18
  203.3 9.9 %fusion.2 = f32[64,10,1024]{2,0,1:T(8,128)} fusion(bf16[1,2560,1024]{2,1,0:T(8,128)(2,1)} %param.10, bf16[64,10,2560]{2,1,0:T(8,128)(2,1)} %all-to-all-done.3), kind=kOutput, calls=%fused_computation.8 | convolution fusion | flops 3355443200 | bytes 11141120 | tf_op jit(solution)/shard_map/slmd,ldf->slmf/dot_general | solution.py:52
  213.2 41.2 %all-to-all-done.1 = bf16[64,10,1024]{2,1,0:T(8,128)(2,1)S(1)} async-done(((bf16[64,10,1024]{2,1,0:T(8,128)(2,1)}), bf16[64,10,1024]{2,1,0:T(8,128)(2,1)S(1)}, u32[]{:S(2)}, u32[]{:S(2)}) %all-to-all-start.1) | async-done | bytes 1310752 | tf_op jit(solution)/shard_map/all_to_all | solution.py:43
  254.4 10.7 %fusion.25 = bf16[64,10,1024]{2,0,1:T(8,128)(2,1)S(1)} fusion(f32[64,10,1024]{2,0,1:T(8,128)} %fusion.2, bf16[1,2560,1024]{2,1,0:T(8,128)(2,1)} %param.11, bf16[64,10,2560]{2,1,0:T(8,128)(2,1)} %all-to-all-done.3, f32[64,10]{0,1:T(8,128)S(1)} %copy.18, bf16[64,10,1024]{2,1,0:T(8,128)(2,1)S(1)} %all-to-all-done.1), kind=kOutput, calls=%fused_computation.30 | convolution fusion | flops 3363307520 | bytes 13765120 | tf_op jit(solution)/shard_map/slmd,ldf->slmf/dot_general | solution.py:55
  265.1 0.0 copy-start.1
  265.2 5.8 %fusion = f32[64,10,2560]{2,0,1:T(8,128)S(1)} fusion(bf16[64,10,1024]{2,0,1:T(8,128)(2,1)S(1)} %fusion.25, bf16[1,2560,1024]{2,1,0:T(8,128)(2,1)} %param.10), kind=kOutput, calls=%fused_computation.6 | convolution fusion | flops 3355443200 | bytes 13107200 | tf_op jit(solution)/shard_map/slmf,ldf->slmd/dot_general | solution.py:66
  270.9 0.0 copy-done.1
  270.9 8.0 %add_convert_fusion = bf16[64,10,2560]{2,0,1:T(8,128)(2,1)S(1)} fusion(f32[64,10,2560]{2,0,1:T(8,128)S(1)} %fusion, bf16[1,2560,1024]{2,1,0:T(8,128)(2,1)} %param.11, f32[64,10,1024]{2,0,1:T(8,128)S(1)} %copy-done.1, f32[64,10]{0,1:T(8,128)S(1)} %copy.18, bf16[64,10,1024]{2,1,0:T(8,128)(2,1)S(1)} %all-to-all-done.1), kind=kOutput, calls=%fused_computation.5 | convolution fusion | flops 3363962880 | bytes 19008000 | tf_op jit(solution)/shard_map/slmf,ldf->slmd/dot_general | solution.py:69
  279.0 4.3 copy.21
  283.3 5.6 %all-to-all-start.4 = ((bf16[64,10,2560]{2,1,0:T(8,128)(2,1)}), bf16[64,10,2560]{2,1,0:T(8,128)(2,1)}, u32[]{:S(2)}, u32[]{:S(2)}) async-start(bf16[64,10,2560]{2,1,0:T(8,128)(2,1)} %copy.21), calls=%async_computation.4 | async-start | bytes 10485760 | tf_op jit(solution)/shard_map/all_to_all | solution.py:73
  288.9 0.0 reduce-scatter.2.cloned.1.call-start
  289.0 118.7 %all-to-all-done.4 = bf16[64,10,2560]{2,1,0:T(8,128)(2,1)} async-done(((bf16[64,10,2560]{2,1,0:T(8,128)(2,1)}), bf16[64,10,2560]{2,1,0:T(8,128)(2,1)}, u32[]{:S(2)}, u32[]{:S(2)}) %all-to-all-start.4) | async-done | bytes 3276832 | tf_op jit(solution)/shard_map/all_to_all | solution.py:73
  407.6 5.3 %reshape.78 = bf16[640,2560]{1,0:T(8,128)(2,1)S(1)} reshape(bf16[64,10,2560]{2,1,0:T(8,128)(2,1)} %all-to-all-done.4) | data formatting | bytes 6553600 | tf_op jit(solution)/shard_map/reshape | solution.py:76
  412.9 3.5 gather_fusion.3
  416.5 0.0 reduce-scatter.2.cloned.1.call-update
  416.5 31.2 %reduce-scatter.2.cloned.1.call-done = bf16[128,2560]{1,0:T(8,128)(2,1)} async-done(((bf16[512,2560]{1,0:T(8,128)(2,1)}), bf16[128,2560]{1,0:T(8,128)(2,1)}) %reduce-scatter.2.cloned.1.call-update) | async-done | bytes 655376 | tf_op jit(solution)/shard_map/reduce_scatter | solution.py:77
  (9 shorter events, 0.1 us)
Async XLA Ops:
  6.5 50.5 %all-gather.4.cloned.1.call-start = ((), (), s32[]{:S(2)}) async-start(), calls=%async_computation.6 | async-start | bytes 3276800 | tf_op jit(solution)/shard_map/all_gather | solution.py:12
  7.3 36.9 %copy-start = (bf16[128,4096]{1,0:T(8,128)(2,1)S(1)}, bf16[128,4096]{1,0:T(8,128)(2,1)}, u32[]{:S(2)}) copy-start(bf16[128,4096]{1,0:T(8,128)(2,1)} %param.7) | copy-start | bytes 3145732
  32.1 20.6 %all-to-all-start.2 = ((s32[64,1,10]{2,1,0:T(1,128)}), s32[64,1,10]{2,1,0:T(1,128)S(1)}, u32[]{:S(2)}, u32[]{:S(2)}) async-start(s32[64,1,10]{2,1,0:T(1,128)} %bitcast.7), calls=%async_computation.2 | async-start | bytes 65536 | tf_op jit(solution)/shard_map/all_to_all | solution.py:46
  52.7 19.7 %all-to-all-start = ((bf16[128,4,1024]{2,0,1:T(8,128)(2,1)}), bf16[128,4,1024]{2,0,1:T(8,128)(2,1)}, u32[]{:S(2)}, u32[]{:S(2)}) async-start(bf16[128,4,1024]{2,0,1:T(8,128)(2,1)} %bitcast.104), calls=%async_computation | async-start | bytes 2097152 | tf_op jit(solution)/shard_map/all_to_all | solution.py:16
  72.4 125.2 %all-to-all-start.3 = ((bf16[64,10,2560]{2,1,0:T(8,128)(2,1)}), bf16[64,10,2560]{2,1,0:T(8,128)(2,1)}, u32[]{:S(2)}, u32[]{:S(2)}) async-start(bf16[64,10,2560]{2,1,0:T(8,128)(2,1)} %reshape.73), calls=%async_computation.3 | async-start | bytes 10485760 | tf_op jit(solution)/shard_map/all_to_all | solution.py:40
  197.7 56.8 %all-to-all-start.1 = ((bf16[64,10,1024]{2,1,0:T(8,128)(2,1)}), bf16[64,10,1024]{2,1,0:T(8,128)(2,1)S(1)}, u32[]{:S(2)}, u32[]{:S(2)}) async-start(bf16[64,10,1024]{2,1,0:T(8,128)(2,1)} %reshape.72), calls=%async_computation.1 | async-start | bytes 4194304 | tf_op jit(solution)/shard_map/all_to_all | solution.py:43
  265.1 5.8 %copy-start.1 = (f32[64,10,1024]{2,0,1:T(8,128)S(1)}, f32[64,10,1024]{2,0,1:T(8,128)}, u32[]{:S(2)}) copy-start(f32[64,10,1024]{2,0,1:T(8,128)} %fusion.2) | copy-start | bytes 7864324
  283.3 124.4 %all-to-all-start.4 = ((bf16[64,10,2560]{2,1,0:T(8,128)(2,1)}), bf16[64,10,2560]{2,1,0:T(8,128)(2,1)}, u32[]{:S(2)}, u32[]{:S(2)}) async-start(bf16[64,10,2560]{2,1,0:T(8,128)(2,1)} %copy.21), calls=%async_computation.4 | async-start | bytes 10485760 | tf_op jit(solution)/shard_map/all_to_all | solution.py:73
  288.9 158.8 %reduce-scatter.2.cloned.1.call-start = ((), (), s32[]{:S(2)}) async-start(), calls=%async_computation.7 | async-start | bytes 3276800 | tf_op jit(solution)/shard_map/reduce_scatter | solution.py:77
Sparse Core Ops, SparseCore 0:
  9.2 40.5 all-gather.3
  416.6 31.0 reduce-scatter.1
where the time goes:
time: 456 us; the launch traced here: 455 us
  waiting for transfers between devices  315 us (69%)
  local copies, waits for them, and re-layouts  39.3 us (9%)
  matrix products  34.4 us (8%)
  starting transfers between devices  34 us (7%)
  blocking collectives  17.1 us (4%)
  between operations  13.6 us (3%)
    all_to_all x1, waiting for transfers between devices, on_device(): lax.all_to_all(partial_value.astype(jnp.bfloat16), 'expert', split_axis=0...  119 us
    all_to_all x1, waiting for transfers between devices, on_device(): lax.all_to_all(packed_tokens, 'expert', split_axis=0, concat_axis=0, tile...  113 us
    all_to_all x1, waiting for transfers between devices, on_device(): lax.all_to_all(packed_hidden, 'expert', split_axis=0, concat_axis=0, tile...  41.2 us
    reduce_scatter x1, waiting for transfers between devices, on_device(): lax.psum_scatter(token_rows.astype(jnp.float32).astype(jnp.bfloat16), 'et...  31.2 us
    all_to_all x1, starting transfers between devices, on_device(): lax.all_to_all(packed_expo, 'expert', split_axis=0, concat_axis=0, tiled=...  12.1 us
    dot_general x1, matrix products, on_device(): jnp.einsum('slmd,ldf->slmf', tokens_split, up_weight, preferred_element_t...  10.7 us
    all_gather x1, blocking collectives, on_device(): lax.all_gather(routes[:, 0], 'etp', axis=0, tiled=True)  9.97 us
    dot_general x1, matrix products, on_device(): jnp.einsum('slmd,ldf->slmf', tokens_split, gate_weight, preferred_element...  9.87 us
  transfers between devices with their start and end apart: 7, of which 6 were waited for; matrix products, arithmetic and copies ran while one was open for 8% of the time, Pallas kernels for 0%

commit v1 on v0

v1 whole, which is shorter than its diff:
```python
import jax
import jax.numpy as jnp
from jax import lax
from jax.experimental import pallas as pl
from jax.experimental.pallas import tpu as pltpu
from jax.sharding import PartitionSpec as P

BF = jnp.bfloat16
F32 = jnp.float32
VMEM_LIMIT = 48 * 1024 * 1024


def cost(flops, nbytes, trans=0):
    return pl.CostEstimate(flops=flops, bytes_accessed=nbytes, transcendentals=trans)


def params(grid_rank=1):
    return pltpu.CompilerParams(
        dimension_semantics=("arbitrary",) * grid_rank, vmem_limit_bytes=VMEM_LIMIT
    )


def split_columns(array, quarters, scale=None):
    rows, columns = array.shape
    width = columns // 4

    def kernel(q_ref, *refs):
        scale_refs = refs[4:-4]
        for source, target in zip(refs[:4], refs[-4:]):
            if scale_refs:
                target[...] = (source[...].astype(F32) * scale_refs[0][...]).astype(BF)
            else:
                target[...] = source[...]

    def block(r):
        return pl.BlockSpec((rows, width), lambda i, q: (0, q[r]))

    extra = [] if scale is None else [scale]
    return pl.pallas_call(
        kernel,
        grid_spec=pltpu.PrefetchScalarGridSpec(
            num_scalar_prefetch=1,
            grid=(1,),
            in_specs=[block(r) for r in range(4)]
            + [pl.BlockSpec((rows, 1), lambda i, q: (0, 0)) for _ in extra],
            out_specs=[pl.BlockSpec((rows, width), lambda i, q: (0, 0))] * 4,
        ),
        out_shape=[jax.ShapeDtypeStruct((rows, width), BF)] * 4,
        compiler_params=params(),
        cost_estimate=cost(rows * columns, 4 * rows * columns),
        name="split_columns",
    )(quarters, array, array, array, array, *extra)


def join_columns(blocks, quarters):
    rows, width = blocks[0].shape

    def kernel(q_ref, b0, b1, b2, b3, out):
        for r, block in enumerate((b0, b1, b2, b3)):
            start = pl.multiple_of(q_ref[r] * width, 128)
            out[:, pl.ds(start, width)] = block[...]

    return pl.pallas_call(
        kernel,
        grid_spec=pltpu.PrefetchScalarGridSpec(
            num_scalar_prefetch=1,
            grid=(1,),
            in_specs=[pl.BlockSpec((rows, width), lambda i, q: (0, 0))] * 4,
            out_specs=pl.BlockSpec((rows, 4 * width), lambda i, q: (0, 0)),
        ),
        out_shape=jax.ShapeDtypeStruct((rows, 4 * width), BF),
        compiler_params=params(),
        cost_estimate=cost(0, 16 * rows * width),
        name="join_columns",
    )(quarters, *blocks)


def up_three(blocks, gate_weight, up_weight, quarters):
    rows, depth = blocks[0].shape
    hidden = gate_weight.shape[1]
    tile = 256

    def kernel(q_ref, t0, t1, t2, g0, g1, g2, u0, u1, u2, gate, up):
        for out, weights in ((gate, (g0, g1, g2)), (up, (u0, u1, u2))):
            total = jnp.dot(t0[...], weights[0][...], preferred_element_type=F32)
            total += jnp.dot(t1[...], weights[1][...], preferred_element_type=F32)
            total += jnp.dot(t2[...], weights[2][...], preferred_element_type=F32)
            out[...] = total

    def weight(r):
        return pl.BlockSpec((depth, tile), lambda j, q: (q[r], j))

    whole = pl.BlockSpec((rows, depth), lambda j, q: (0, 0))
    out = pl.BlockSpec((rows, tile), lambda j, q: (0, j))
    return pl.pallas_call(
        kernel,
        grid_spec=pltpu.PrefetchScalarGridSpec(
            num_scalar_prefetch=1,
            grid=(hidden // tile,),
            in_specs=[whole] * 3 + [weight(r) for r in range(3)] * 2,
            out_specs=[out, out],
        ),
        out_shape=[jax.ShapeDtypeStruct((rows, hidden), F32)] * 2,
        compiler_params=params(),
        cost_estimate=cost(12 * rows * depth * hidden, 12 * depth * hidden + 8 * rows * hidden),
        name="up_three",
    )(quarters, *blocks, *([gate_weight] * 3), *([up_weight] * 3))


def up_last(block, gate, up, gate_weight, up_weight, quarters):
    rows, depth = block.shape
    hidden = gate_weight.shape[1]
    tile = 256

    def kernel(q_ref, t, g_in, u_in, wg, wu, for_gate, for_up):
        g = g_in[...] + jnp.dot(t[...], wg[...], preferred_element_type=F32)
        u = u_in[...] + jnp.dot(t[...], wu[...], preferred_element_type=F32)
        s = 1.0 / (1.0 + jnp.exp(-g))
        for_gate[...] = u * s * (1.0 + g * (1.0 - s))
        for_up[...] = g * s

    weight = pl.BlockSpec((depth, tile), lambda j, q: (q[3], j))
    tiled = pl.BlockSpec((rows, tile), lambda j, q: (0, j))
    return pl.pallas_call(
        kernel,
        grid_spec=pltpu.PrefetchScalarGridSpec(
            num_scalar_prefetch=1,
            grid=(hidden // tile,),
            in_specs=[pl.BlockSpec((rows, depth), lambda j, q: (0, 0)), tiled, tiled, weight, weight],
            out_specs=[tiled, tiled],
        ),
        out_shape=[jax.ShapeDtypeStruct((rows, hidden), F32)] * 2,
        compiler_params=params(),
        cost_estimate=cost(
            4 * rows * depth * hidden, 4 * depth * hidden + 16 * rows * hidden, rows * hidden
        ),
        name="up_last",
    )(quarters, block, gate, up, gate_weight, up_weight)


CONTRACT_LAST = (((1,), (1,)), ((), ()))


def down_first(scaled, for_gate, for_up, gate_weight, up_weight, quarters):
    rows, hidden = scaled.shape
    depth = gate_weight.shape[0] // 4
    tile = 160

    def kernel(q_ref, h, a, b, wg, wu, gg_out, gu_out, out):
        scaled_rows = h[...].astype(F32)
        gg = (scaled_rows * a[...]).astype(BF)
        gu = (scaled_rows * b[...]).astype(BF)
        gg_out[...] = gg
        gu_out[...] = gu
        total = lax.dot_general(gg, wg[...], CONTRACT_LAST, preferred_element_type=F32)
        total += lax.dot_general(gu, wu[...], CONTRACT_LAST, preferred_element_type=F32)
        out[...] = total.astype(BF)

    weight = pl.BlockSpec((depth, hidden), lambda i, q: (q[0], 0))
    tiled = pl.BlockSpec((tile, hidden), lambda i, q: (i, 0))
    return pl.pallas_call(
        kernel,
        grid_spec=pltpu.PrefetchScalarGridSpec(
            num_scalar_prefetch=1,
            grid=(rows // tile,),
            in_specs=[tiled, tiled, tiled, weight, weight],
            out_specs=[tiled, tiled, pl.BlockSpec((tile, depth), lambda i, q: (i, 0))],
        ),
        out_shape=[jax.ShapeDtypeStruct((rows, hidden), BF)] * 2
        + [jax.ShapeDtypeStruct((rows, depth), BF)],
        compiler_params=params(),
        cost_estimate=cost(4 * rows * depth * hidden, 4 * depth * hidden + 14 * rows * hidden),
        name="down_first",
    )(quarters, scaled, for_gate, for_up, gate_weight, up_weight)


def down_more(grad_gate, grad_up, gate_weight, up_weight, quarters, count):
    rows, hidden = grad_gate.shape
    depth = gate_weight.shape[0] // 4
    tile = 160

    def kernel(q_ref, gg, gu, *refs):
        for r in range(count):
            wg, wu, out = refs[r], refs[count + r], refs[2 * count + r]
            total = lax.dot_general(gg[...], wg[...], CONTRACT_LAST, preferred_element_type=F32)
            total += lax.dot_general(gu[...], wu[...], CONTRACT_LAST, preferred_element_type=F32)
            out[...] = total.astype(BF)

    def weight(r):
        return pl.BlockSpec((depth, hidden), lambda i, q: (q[r], 0))

    tiled = pl.BlockSpec((tile, hidden), lambda i, q: (i, 0))
    return pl.pallas_call(
        kernel,
        grid_spec=pltpu.PrefetchScalarGridSpec(
            num_scalar_prefetch=1,
            grid=(rows // tile,),
            in_specs=[tiled, tiled] + [weight(r) for r in range(count)] * 2,
            out_specs=[pl.BlockSpec((tile, depth), lambda i, q: (i, 0))] * count,
        ),
        out_shape=[jax.ShapeDtypeStruct((rows, depth), BF)] * count,
        compiler_params=params(),
        cost_estimate=cost(
            4 * count * rows * depth * hidden, 4 * count * depth * hidden + 4 * rows * hidden
        ),
        name="down_more",
    )(quarters, grad_gate, grad_up, *([gate_weight] * count), *([up_weight] * count))


def on_device(tokens, hidden_grad, routes, exponents, gate_weight, up_weight):
    etp = lax.axis_size("etp")
    experts = lax.axis_size("expert")
    own_rows, features = tokens.shape
    group_size = own_rows * etp
    capacity = 5 * group_size // (4 * experts)
    slots = experts * capacity
    x = lax.axis_index("etp").astype(jnp.int32)
    steps = jnp.arange(4, dtype=jnp.int32)
    ahead = (x + steps) % 4
    behind = (x - steps) % 4
    gate_w, up_w = gate_weight[0], up_weight[0]

    def back(array, r):
        return lax.ppermute(array, "etp", [(i, (i - r) % etp) for i in range(etp)])

    def forward(array, r):
        return lax.ppermute(array, "etp", [(i, (i + r) % etp) for i in range(etp)])

    with jax.named_scope("group_exchange"):
        own_routes = routes[:, 0]
        group_routes = jnp.concatenate([own_routes] + [back(own_routes, r) for r in (1, 2, 3)])
        token_parts = split_columns(tokens, behind)
        scales = jnp.exp2(exponents.astype(F32))[:, None]
        hidden_parts = split_columns(hidden_grad, behind, scales)
        group_tokens = jnp.concatenate(
            [token_parts[0]] + [back(token_parts[r], r) for r in (1, 2, 3)]
        )
        group_hidden = jnp.concatenate(
            [hidden_parts[0]] + [back(hidden_parts[r], r) for r in (1, 2, 3)]
        )

    with jax.named_scope("slots"):
        place = (ahead[:, None] * own_rows + jnp.arange(own_rows, dtype=jnp.int32)[None, :]).reshape(-1)
        earlier = (group_routes[:, None] == group_routes[None, :]) & (place[:, None] < place[None, :])
        rank = jnp.sum(earlier.astype(jnp.int32), axis=0)
        slot_index = group_routes * capacity + rank
        select = (jnp.arange(slots, dtype=jnp.int32)[:, None] == slot_index[None, :]).astype(BF)

    def pick(rows):
        return jnp.dot(select, rows, preferred_element_type=F32).astype(BF)

    def to_experts(array):
        return lax.all_to_all(array, "expert", split_axis=0, concat_axis=0, tiled=True)

    quarter = features // 4
    hidden = hidden_grad.shape[1] // 4
    with jax.named_scope("send_tokens"):
        packed_tokens = pick(group_tokens).reshape(experts, capacity // 2, 2, quarter)
        own_block = to_experts(packed_tokens).reshape(slots, quarter)
    with jax.named_scope("send_hidden"):
        packed_hidden = pick(group_hidden).reshape(experts, capacity * hidden // 128, 128)
        scaled = to_experts(packed_hidden).reshape(slots, hidden)

    with jax.named_scope("gather_width"):
        block1, block3, block2 = back(own_block, 1), back(own_block, 3), back(own_block, 2)
    with jax.named_scope("pre_activations"):
        order = jnp.stack([ahead[0], ahead[1], ahead[3], ahead[2]])
        gate, up = up_three((own_block, block1, block3), gate_w, up_w, order)
        for_gate, for_up = up_last(block2, gate, up, gate_w, up_w, order)
    with jax.named_scope("input_partials"):
        grad_gate, grad_up, part2 = down_first(scaled, for_gate, for_up, gate_w, up_w, ahead[2:3])
        part1, part3 = down_more(
            grad_gate, grad_up, gate_w, up_w, jnp.stack([ahead[1], ahead[3]]), 2
        )
        (part0,) = down_more(grad_gate, grad_up, gate_w, up_w, ahead[0:1], 1)
    with jax.named_scope("sum_quarters"):
        from2, from1, from3 = forward(part2, 2), forward(part1, 1), forward(part3, 3)
        summed = (
            part0.astype(F32) + from1.astype(F32) + from2.astype(F32) + from3.astype(F32)
        ).astype(BF)
    with jax.named_scope("return_tokens"):
        returned = to_experts(summed.reshape(experts, capacity // 2, 2, quarter))
        rows = returned.reshape(slots, quarter)
        group_rows = lax.dot_general(
            select, rows, (((0,), (0,)), ((), ())), preferred_element_type=F32
        ).astype(BF)
        parts = [group_rows[r * own_rows : (r + 1) * own_rows] for r in range(4)]
        blocks = [parts[0]] + [forward(parts[r], r) for r in (1, 2, 3)]
        return join_columns(blocks, behind)


def solution(mesh):
    placed = (
        P(("expert", "etp"), None),
        P(("expert", "etp"), None),
        P(("expert", "etp"), None),
        P(("expert", "etp")),
        P("expert", None, "etp"),
        P("expert", None, "etp"),
    )
    return jax.shard_map(
        on_device, mesh=mesh, in_specs=placed, out_specs=P(("expert", "etp"), None), check_vma=False
    )
```

time: 456 us -> 221 us (0.48)
  waiting for transfers between devices: 315 us -> 87.2 us
  Pallas kernels: 0 us -> 42.6 us
  matrix products: 34.4 us -> 2.37 us
  local copies, waits for them, and re-layouts: 39.3 us -> 10.7 us
  blocking collectives: 17.1 us -> 34 us
  between operations: 13.6 us -> 0.26 us
  starting transfers between devices: 34 us -> 39.8 us
    all_to_all x5 -> x2, waiting for transfers between devices: 283 us -> 4.83 us  [to_experts(): lax.all_to_all(array, 'expert', split_axis=0, concat_axis=0, tiled=True)]
    ppermute x0 -> x18, waiting for transfers between devices: none -> 82.4 us  [the longest x12 53.2 us: back(): return lax.ppermute(array, 'etp', [(i, (i - r) % etp) for i in range(etp)])]
    pallas_call x0 -> x8, Pallas kernels: none -> 42.6 us  [the longest x2 16.2 us: down_more(): pl.pallas_call(kernel, grid_spec=pltpu.PrefetchScalarGridSpec(num_scalar_...]
    all_to_all x0 -> x1, blocking collectives: none -> 34 us  [to_experts(): lax.all_to_all(array, 'expert', split_axis=0, concat_axis=0, tiled=True)]
    dot_general x4 -> x3, matrix products: 34.4 us -> 2.37 us  [the longest x2 1.55 us: pick(): return jnp.dot(select, rows, preferred_element_type=F32).astype(BF)]
    reduce_scatter x1 -> x0, waiting for transfers between devices: 31.2 us -> none  [on_device(): lax.psum_scatter(token_rows.astype(jnp.float32).astype(jnp.bfloat16), 'et...]
    ppermute x0 -> x18, starting transfers between devices: none -> 21.8 us  [the longest x12 15.2 us: back(): return lax.ppermute(array, 'etp', [(i, (i - r) % etp) for i in range(etp)])]
    all_gather x2 -> x0, blocking collectives: 17.1 us -> none  [the longest x1 9.97 us: on_device(): lax.all_gather(routes[:, 0], 'etp', axis=0, tiled=True)]
  transfers between devices with their start and end apart: 7 -> 20, of which waited for: 6 -> 12; matrix products, arithmetic and copies ran while one was open for 8% -> 3% of each run, Pallas kernels for 0% -> 11%
where the time goes in v1:
time: 221 us; the launch traced here: 220 us
  waiting for transfers between devices  87.2 us (39%)
  Pallas kernels  42.6 us (19%)
  starting transfers between devices  39.8 us (18%)
  blocking collectives  34 us (15%)
  local copies, waits for them, and re-layouts  10.7 us (5%)
  other arithmetic  3.41 us (2%)
  matrix products  2.37 us (1%)
    ppermute x12, waiting for transfers between devices, back(): return lax.ppermute(array, 'etp', [(i, (i - r) % etp) for i in range(etp)])  53.2 us
    all_to_all x1, blocking collectives, to_experts(): lax.all_to_all(array, 'expert', split_axis=0, concat_axis=0, tiled=True)  34 us
    ppermute x6, waiting for transfers between devices, forward(): return lax.ppermute(array, 'etp', [(i, (i + r) % etp) for i in range(etp)])  29.2 us
    all_to_all x2, starting transfers between devices, to_experts(): lax.all_to_all(array, 'expert', split_axis=0, concat_axis=0, tiled=True)  17.9 us
    pallas_call x2, Pallas kernels, down_more(): pl.pallas_call(kernel, grid_spec=pltpu.PrefetchScalarGridSpec(num_scalar_...  16.2 us
    ppermute x12, starting transfers between devices, back(): return lax.ppermute(array, 'etp', [(i, (i - r) % etp) for i in range(etp)])  15.2 us
    pallas_call x1, Pallas kernels, up_three(): pl.pallas_call(kernel, grid_spec=pltpu.PrefetchScalarGridSpec(num_scalar_...  10.1 us
    pallas_call x1, Pallas kernels, down_first(): pl.pallas_call(kernel, grid_spec=pltpu.PrefetchScalarGridSpec(num_scalar_...  7 us
  transfers between devices with their start and end apart: 20, of which 12 were waited for; matrix products, arithmetic and copies ran while one was open for 3% of the time, Pallas kernels for 11%

profile of v1, /device:TPU:8, one launch (start us, length us, event | category | flops | bytes accessed | tf_op | source)
XLA Modules:
  0.0 220.2 jit_solution(17635362155180565265)
XLA Ops:
  0.0 2.8 %collective-permute-start = (s32[128]{0:T(128)}, s32[128]{0:T(128)S(1)}, u32[]{:S(2)}, u32[]{:S(2)}) collective-permute-start(s32[128]{0:T(128)} %bitcast.26), channel_id=1, source_target_pairs={{0,3},{1,0},{2,1},{3,2},{4,7},{5,4},{6,5},{7,6},{8,11},{9,8},{10,9... | collective-permute-start | bytes 1544 | tf_op jit(solution)/shard_map/group_exchange/ppermute | solution.py:224
  2.8 0.8 collective-permute-start.1
  3.6 0.9 collective-permute-start.2
  4.5 0.0 copy-start.1
  4.5 1.1 copy-done.1
  5.6 0.6 split_columns.3
  6.2 2.4 %collective-permute-start.6 = (bf16[128,640]{1,0:T(8,128)(2,1)S(1)}, bf16[128,640]{1,0:T(8,128)(2,1)S(1)}, u32[]{:S(2)}, u32[]{:S(2)}) collective-permute-start(bf16[128,640]{1,0:T(8,128)(2,1)S(1)} %get-tuple-element.27), channel_id=1, source_target_pairs={{0,3},{1,0},{2,1},{3,2},{4,7},{5,4},{6,5},{7,6},{8,11},{9,8},{10,9... | collective-permute-start | bytes 491528 | tf_op jit(solution)/shard_map/group_exchange/ppermute | solution.py:224
  8.6 1.5 collective-permute-start.7
  10.1 0.1 add_bitcast_fusion
  10.2 0.0 collective-permute-start.8
  10.3 0.2 convert_reduce_fusion
  10.6 4.2 %collective-permute-done.6 = bf16[128,640]{1,0:T(8,128)(2,1)S(1)} collective-permute-done((bf16[128,640]{1,0:T(8,128)(2,1)S(1)}, bf16[128,640]{1,0:T(8,128)(2,1)S(1)}, u32[]{:S(2)}, u32[]{:S(2)}) %collective-permute-start.6) | collective-permute-done | bytes 163872 | tf_op jit(solution)/shard_map/group_exchange/ppermute | solution.py:224
  14.8 2.0 collective-permute-done.7
  16.7 1.7 collective-permute-done.8
  18.4 0.7 convolution_convert_fusion.1
  19.1 0.0 copy-start.6
  19.2 0.0 copy-start
  19.2 1.2 reshape.101
  20.4 12.1 %all-to-all-start.1 = ((bf16[64,5,2,640]{3,2,1,0:T(2,128)(2,1)}), bf16[64,5,2,640]{3,2,1,0:T(2,128)(2,1)S(1)}, u32[]{:S(2)}, u32[]{:S(2)}) async-start(bf16[64,5,2,640]{3,2,1,0:T(2,128)(2,1)} %reshape.101), calls=%async_computation.1 | async-start | bytes 1638400 | tf_op jit(solution)/shard_map/send_tokens/all_to_all | solution.py:253
  32.5 0.1 copy.8.refs_4_
  32.6 0.8 split_columns.2
  33.4 0.6 collective-permute-start.3
  34.1 1.5 collective-permute-start.4
  35.6 0.9 collective-permute-start.5
  36.4 6.2 %collective-permute-done.3 = bf16[128,1024]{1,0:T(8,128)(2,1)S(1)} collective-permute-done((bf16[128,1024]{1,0:T(8,128)(2,1)S(1)}, bf16[128,1024]{1,0:T(8,128)(2,1)S(1)}, u32[]{:S(2)}, u32[]{:S(2)}) %collective-permute-start.3) | collective-permute-done | bytes 262176 | tf_op jit(solution)/shard_map/group_exchange/ppermute | solution.py:224
  42.6 2.1 collective-permute-done.4
  44.8 4.5 %collective-permute-done.5 = bf16[128,1024]{1,0:T(8,128)(2,1)S(1)} collective-permute-done((bf16[128,1024]{1,0:T(8,128)(2,1)S(1)}, bf16[128,1024]{1,0:T(8,128)(2,1)S(1)}, u32[]{:S(2)}, u32[]{:S(2)}) %collective-permute-start.5) | collective-permute-done | bytes 262176 | tf_op jit(solution)/shard_map/group_exchange/ppermute | solution.py:224
  49.3 0.8 convolution_convert_fusion
  50.1 1.4 reshape.99
  51.5 4.8 %all-to-all-done.1 = bf16[64,5,2,640]{3,2,1,0:T(2,128)(2,1)S(1)} async-done(((bf16[64,5,2,640]{3,2,1,0:T(2,128)(2,1)}), bf16[64,5,2,640]{3,2,1,0:T(2,128)(2,1)S(1)}, u32[]{:S(2)}, u32[]{:S(2)}) %all-to-all-start.1) | async-done | bytes 819232 | tf_op jit(solution)/shard_map/send_tokens/all_to_all | solution.py:253
  56.4 5.8 %all-to-all-start = ((bf16[64,80,128]{2,1,0:T(8,128)(2,1)}), bf16[64,80,128]{2,1,0:T(8,128)(2,1)S(1)}, u32[]{:S(2)}, u32[]{:S(2)}) async-start(bf16[64,80,128]{2,1,0:T(8,128)(2,1)} %reshape.99), calls=%async_computation | async-start | bytes 2621440 | tf_op jit(solution)/shard_map/send_hidden/all_to_all | solution.py:253
  62.2 0.3 reshape.102.t0
  62.5 0.8 collective-permute-start.10
  63.3 1.5 collective-permute-start.11
  64.8 1.5 collective-permute-start.9
  66.3 0.7 fusion.22
  67.0 1.3 pad_add_fusion.2.q_ref
  68.3 1.3 pad_add_fusion.1.q_ref
  69.6 14.2 %collective-permute-done.10.t1 = bf16[640,640]{1,0:T(8,128)(2,1)S(1)} collective-permute-done((bf16[640,640]{1,0:T(8,128)(2,1)S(1)}, bf16[640,640]{1,0:T(8,128)(2,1)S(1)}, u32[]{:S(2)}, u32[]{:S(2)}) %collective-permute-start.10) | collective-permute-done | bytes 819232 | tf_op jit(solution)/shard_map/gather_width/ppermute | solution.py:224
  83.8 18.3 %collective-permute-done.11.t2 = bf16[640,640]{1,0:T(8,128)(2,1)S(1)} collective-permute-done((bf16[640,640]{1,0:T(8,128)(2,1)S(1)}, bf16[640,640]{1,0:T(8,128)(2,1)S(1)}, u32[]{:S(2)}, u32[]{:S(2)}) %collective-permute-start.11) | collective-permute-done | bytes 819232 | tf_op jit(solution)/shard_map/gather_width/ppermute | solution.py:224
  102.1 10.1 %up_three.1 = (f32[640,1024]{1,0:T(8,128)S(1)}, f32[640,1024]{1,0:T(8,128)}) custom-call(s32[4]{0:T(128)S(1)} %pad_add_fusion.1.q_ref, bf16[640,640]{1,0:T(8,128)(2,1)S(1)} %reshape.102.t0, bf16[640,640]{1,0:T(8,128)(2,1)S(1)} %collective-permute-done.10.t1, bf16[640,640]{1,0:T(8,128)(2,1)S(1)} %collective-permute-done.11.t2, bf16[2560,1024]{1,0:T(8,128)(2,1)} %bitcast.9, ...), custom_call_target="tpu_custom_call" | custom-call | flops 5033164800 | bytes 13107200 | tf_op jit(solution)/shard_map/pre_activations/up_three/pallas_call | solution.py:95
  112.2 1.5 copy-done.4
  113.8 6.4 %up_last.1 = (f32[640,1024]{1,0:T(8,128)S(1)}, f32[640,1024]{1,0:T(8,128)S(1)}) custom-call(s32[4]{0:T(128)S(1)} %pad_add_fusion.1.q_ref, bf16[640,640]{1,0:T(8,128)(2,1)S(1)} %collective-permute-done.9.t, f32[640,1024]{1,0:T(8,128)} %copy-done.4, f32[640,1024]{1,0:T(8,128)} %get-tuple-element.31.u_in, bf16[2560,1024]{1,0:T(8,128)(2,1)} %bitcast.12, ...), custom_call_target="tpu_custom_call" | custom-call | flops 1677721600 | bytes 13107200 | tf_op jit(solution)/shard_map/pre_activations/up_last/pallas_call | solution.py:124
  120.2 1.5 copy-done.2
  121.7 1.5 copy-done.3
  123.3 0.6 reshape.100.h
  123.8 7.0 %down_first.1 = (bf16[640,1024]{1,0:T(8,128)(2,1)S(1)}, bf16[640,1024]{1,0:T(8,128)(2,1)S(1)}, bf16[640,640]{1,0:T(8,128)(2,1)S(1)}) custom-call(s32[1]{0:T(128)} %get-tuple-element.45.q_ref, bf16[640,1024]{1,0:T(8,128)(2,1)S(1)} %reshape.100.h, f32[640,1024]{1,0:T(8,128)} %copy-done.2, f32[640,1024]{1,0:T(8,128)} %copy-done.3, bf16[2560,1024]{1,0:T(8,128)(2,1)} %bitcast.13, ...), custom_call_target="tpu_custom_call" | custom-call | flops 1677721600 | bytes 11796480 | tf_op jit(solution)/shard_map/input_partials/down_first/pallas_call | solution.py:161
  130.9 10.1 %down_more.3 = (bf16[640,640]{1,0:T(8,128)(2,1)S(1)}, bf16[640,640]{1,0:T(8,128)(2,1)S(1)}) custom-call(s32[2]{0:T(128)S(1)} %pad_add_fusion.2.q_ref, bf16[640,1024]{1,0:T(8,128)(2,1)S(1)} %get-tuple-element.34.gg, bf16[640,1024]{1,0:T(8,128)(2,1)S(1)} %get-tuple-element.35.gu, bf16[2560,1024]{1,0:T(8,128)(2,1)} %bitcast.14, bf16[2560,1024]{1,0:T(8,128)(2,1)} %bitcast.15, ...), custom_call_target="tpu_custom_call" | custom-call | flops 3355443200 | bytes 7864320 | tf_op jit(solution)/shard_map/input_partials/down_more/pallas_call | solution.py:193
  141.0 0.1 collective-permute-start.12
  141.1 3.2 %collective-permute-start.14 = (bf16[640,640]{1,0:T(8,128)(2,1)S(1)}, bf16[640,640]{1,0:T(8,128)(2,1)S(1)}, u32[]{:S(2)}, u32[]{:S(2)}) collective-permute-start(bf16[640,640]{1,0:T(8,128)(2,1)S(1)} %get-tuple-element.38), channel_id=1, source_target_pairs={{0,3},{1,0},{2,1},{3,2},{4,7},{5,4},{6,5},{7,6},{8,11},{9,8},{10,9... | collective-permute-start | bytes 2457608 | tf_op jit(solution)/shard_map/sum_quarters/ppermute | solution.py:227
  144.3 6.1 %down_more.2 = bf16[640,640]{1,0:T(8,128)(2,1)S(1)} custom-call(s32[1]{0:T(128)} %get-tuple-element.43.q_ref, bf16[640,1024]{1,0:T(8,128)(2,1)S(1)} %get-tuple-element.34.gg, bf16[640,1024]{1,0:T(8,128)(2,1)S(1)} %get-tuple-element.35.gu, bf16[2560,1024]{1,0:T(8,128)(2,1)} %bitcast.16, bf16[2560,1024]{1,0:T(8,128)(2,1)} %bitcast.24), custom_call_target="tpu_custom_call" | custom-call | flops 1677721600 | bytes 5242880 | tf_op jit(solution)/shard_map/input_partials/down_more/pallas_call | solution.py:193
  150.4 21.8 %collective-permute-done.12 = bf16[640,640]{1,0:T(8,128)(2,1)S(1)} collective-permute-done((bf16[640,640]{1,0:T(8,128)(2,1)S(1)}, bf16[640,640]{1,0:T(8,128)(2,1)S(1)}, u32[]{:S(2)}, u32[]{:S(2)}) %collective-permute-start.12) | collective-permute-done | bytes 819232 | tf_op jit(solution)/shard_map/sum_quarters/ppermute | solution.py:227
  172.2 0.4 add_convert_fusion
  172.6 0.3 reshape.103
  172.9 34.0 %all_to_all.15 = bf16[64,5,2,640]{3,2,1,0:T(2,128)(2,1)S(1)} all-to-all(bf16[64,5,2,640]{3,2,1,0:T(2,128)(2,1)S(1)} %reshape.103), channel_id=1, replica_groups=mesh['expert'=64,'etp'=4] {'expert'}, dimensions={0} | all-to-all | bytes 1638400 | tf_op jit(solution)/shard_map/return_tokens/all_to_all | solution.py:253
  206.9 0.3 reshape.104
  207.2 0.8 convolution_convert_fusion.2
  208.0 0.1 fusion.21
  208.1 0.1 collective-permute-start.15
  208.2 1.0 collective-permute-start.16
  209.2 2.2 %collective-permute-start.17 = (bf16[128,640]{1,0:T(8,128)(2,1)S(1)}, bf16[128,640]{1,0:T(8,128)(2,1)S(1)}, u32[]{:S(2)}, u32[]{:S(2)}) collective-permute-start(bf16[128,640]{1,0:T(8,128)(2,1)S(1)} %get-tuple-element.39), channel_id=1, source_target_pairs={{0,3},{1,0},{2,1},{3,2},{4,7},{5,4},{6,5},{7,6},{8,11},{9,8},{10,9... | collective-permute-start | bytes 491528 | tf_op jit(solution)/shard_map/return_tokens/ppermute | solution.py:227
  211.4 6.8 %collective-permute-done.15.b1 = bf16[128,640]{1,0:T(8,128)(2,1)S(1)} collective-permute-done((bf16[128,640]{1,0:T(8,128)(2,1)S(1)}, bf16[128,640]{1,0:T(8,128)(2,1)S(1)}, u32[]{:S(2)}, u32[]{:S(2)}) %collective-permute-start.15) | collective-permute-done | bytes 163872 | tf_op jit(solution)/shard_map/return_tokens/ppermute | solution.py:227
  218.2 0.6 collective-permute-done.17.b3
  218.8 1.4 join_columns.1
  (21 shorter events, 0.1 us)
Async XLA Ops:
  0.0 10.3 %copy-start.5 = (s32[128,1]{0,1:T(1,128)S(1)}, s32[128,1]{0,1:T(1,128)}, u32[]{:S(2)}) copy-start(s32[128,1]{0,1:T(1,128)} %param.8) | copy-start | bytes 1540
  0.0 10.2 %collective-permute-start = (s32[128]{0:T(128)}, s32[128]{0:T(128)S(1)}, u32[]{:S(2)}, u32[]{:S(2)}) collective-permute-start(s32[128]{0:T(128)} %bitcast.26), channel_id=1, source_target_pairs={{0,3},{1,0},{2,1},{3,2},{4,7},{5,4},{6,5},{7,6},{8,11},{9,8},{10,9... | collective-permute-start | bytes 1544 | tf_op jit(solution)/shard_map/group_exchange/ppermute | solution.py:224
  2.8 7.5 %collective-permute-start.1 = (s32[128]{0:T(128)}, s32[128]{0:T(128)S(1)}, u32[]{:S(2)}, u32[]{:S(2)}) collective-permute-start(s32[128]{0:T(128)} %bitcast.27), channel_id=1, source_target_pairs={{0,2},{1,3},{2,0},{3,1},{4,6},{5,7},{6,4},{7,5},{8,10},{9,11},{10,... | collective-permute-start | bytes 1544 | tf_op jit(solution)/shard_map/group_exchange/ppermute | solution.py:224
  3.6 6.7 %collective-permute-start.2 = (s32[128]{0:T(128)}, s32[128]{0:T(128)S(1)}, u32[]{:S(2)}, u32[]{:S(2)}) collective-permute-start(s32[128]{0:T(128)} %bitcast.28), channel_id=1, source_target_pairs={{0,1},{1,2},{2,3},{3,0},{4,5},{5,6},{6,7},{7,4},{8,9},{9,10},{10,1... | collective-permute-start | bytes 1544 | tf_op jit(solution)/shard_map/group_exchange/ppermute | solution.py:224
  4.5 1.1 copy-start.1
  6.2 8.6 %collective-permute-start.6 = (bf16[128,640]{1,0:T(8,128)(2,1)S(1)}, bf16[128,640]{1,0:T(8,128)(2,1)S(1)}, u32[]{:S(2)}, u32[]{:S(2)}) collective-permute-start(bf16[128,640]{1,0:T(8,128)(2,1)S(1)} %get-tuple-element.27), channel_id=1, source_target_pairs={{0,3},{1,0},{2,1},{3,2},{4,7},{5,4},{6,5},{7,6},{8,11},{9,8},{10,9... | collective-permute-start | bytes 491528 | tf_op jit(solution)/shard_map/group_exchange/ppermute | solution.py:224
  8.6 8.1 %collective-permute-start.7 = (bf16[128,640]{1,0:T(8,128)(2,1)S(1)}, bf16[128,640]{1,0:T(8,128)(2,1)S(1)}, u32[]{:S(2)}, u32[]{:S(2)}) collective-permute-start(bf16[128,640]{1,0:T(8,128)(2,1)S(1)} %get-tuple-element.28), channel_id=1, source_target_pairs={{0,2},{1,3},{2,0},{3,1},{4,6},{5,7},{6,4},{7,5},{8,10},{9,11},{10,... | collective-permute-start | bytes 491528 | tf_op jit(solution)/shard_map/group_exchange/ppermute | solution.py:224
  10.2 8.2 %collective-permute-start.8 = (bf16[128,640]{1,0:T(8,128)(2,1)S(1)}, bf16[128,640]{1,0:T(8,128)(2,1)S(1)}, u32[]{:S(2)}, u32[]{:S(2)}) collective-permute-start(bf16[128,640]{1,0:T(8,128)(2,1)S(1)} %get-tuple-element.29), channel_id=1, source_target_pairs={{0,1},{1,2},{2,3},{3,0},{4,5},{5,6},{6,7},{7,4},{8,9},{9,10},{10,1... | collective-permute-start | bytes 491528 | tf_op jit(solution)/shard_map/group_exchange/ppermute | solution.py:224
  19.1 13.3 %copy-start.6 = (s32[128]{0:T(128)S(1)}, s32[128]{0:T(128)}, u32[]{:S(2)}) copy-start(s32[128]{0:T(128)} %param.9) | copy-start | bytes 1540
  19.2 13.5 %copy-start = (bf16[128,4096]{1,0:T(8,128)(2,1)S(1)}, bf16[128,4096]{1,0:T(8,128)(2,1)}, u32[]{:S(2)}) copy-start(bf16[128,4096]{1,0:T(8,128)(2,1)} %refs_3_.2) | copy-start | bytes 3145732
  20.4 36.0 %all-to-all-start.1 = ((bf16[64,5,2,640]{3,2,1,0:T(2,128)(2,1)}), bf16[64,5,2,640]{3,2,1,0:T(2,128)(2,1)S(1)}, u32[]{:S(2)}, u32[]{:S(2)}) async-start(bf16[64,5,2,640]{3,2,1,0:T(2,128)(2,1)} %reshape.101), calls=%async_computation.1 | async-start | bytes 1638400 | tf_op jit(solution)/shard_map/send_tokens/all_to_all | solution.py:253
  33.4 9.2 %collective-permute-start.3 = (bf16[128,1024]{1,0:T(8,128)(2,1)S(1)}, bf16[128,1024]{1,0:T(8,128)(2,1)S(1)}, u32[]{:S(2)}, u32[]{:S(2)}) collective-permute-start(bf16[128,1024]{1,0:T(8,128)(2,1)S(1)} %get-tuple-element.23), channel_id=1, source_target_pairs={{0,3},{1,0},{2,1},{3,2},{4,7},{5,4},{6,5},{7,6},{8,11},{9,8},{10,9... | collective-permute-start | bytes 786440 | tf_op jit(solution)/shard_map/group_exchange/ppermute | solution.py:224
  34.1 10.7 %collective-permute-start.4 = (bf16[128,1024]{1,0:T(8,128)(2,1)S(1)}, bf16[128,1024]{1,0:T(8,128)(2,1)S(1)}, u32[]{:S(2)}, u32[]{:S(2)}) collective-permute-start(bf16[128,1024]{1,0:T(8,128)(2,1)S(1)} %get-tuple-element.24), channel_id=1, source_target_pairs={{0,2},{1,3},{2,0},{3,1},{4,6},{5,7},{6,4},{7,5},{8,10},{9,11},{10,... | collective-permute-start | bytes 786440 | tf_op jit(solution)/shard_map/group_exchange/ppermute | solution.py:224
  35.6 13.7 %collective-permute-start.5 = (bf16[128,1024]{1,0:T(8,128)(2,1)S(1)}, bf16[128,1024]{1,0:T(8,128)(2,1)S(1)}, u32[]{:S(2)}, u32[]{:S(2)}) collective-permute-start(bf16[128,1024]{1,0:T(8,128)(2,1)S(1)} %get-tuple-element.25), channel_id=1, source_target_pairs={{0,1},{1,2},{2,3},{3,0},{4,5},{5,6},{6,7},{7,4},{8,9},{9,10},{10,1... | collective-permute-start | bytes 786440 | tf_op jit(solution)/shard_map/group_exchange/ppermute | solution.py:224
  56.4 66.9 %all-to-all-start = ((bf16[64,80,128]{2,1,0:T(8,128)(2,1)}), bf16[64,80,128]{2,1,0:T(8,128)(2,1)S(1)}, u32[]{:S(2)}, u32[]{:S(2)}) async-start(bf16[64,80,128]{2,1,0:T(8,128)(2,1)} %reshape.99), calls=%async_computation | async-start | bytes 2621440 | tf_op jit(solution)/shard_map/send_hidden/all_to_all | solution.py:253
  62.5 21.3 %collective-permute-start.10 = (bf16[640,640]{1,0:T(8,128)(2,1)S(1)}, bf16[640,640]{1,0:T(8,128)(2,1)S(1)}, u32[]{:S(2)}, u32[]{:S(2)}) collective-permute-start(bf16[640,640]{1,0:T(8,128)(2,1)S(1)} %reshape.102.t0), channel_id=1, source_target_pairs={{0,3},{1,0},{2,1},{3,2},{4,7},{5,4},{6,5},{7,6},{8,11},{9,8},{10,9... | collective-permute-start | bytes 2457608 | tf_op jit(solution)/shard_map/gather_width/ppermute | solution.py:224
  63.3 38.8 %collective-permute-start.11 = (bf16[640,640]{1,0:T(8,128)(2,1)S(1)}, bf16[640,640]{1,0:T(8,128)(2,1)S(1)}, u32[]{:S(2)}, u32[]{:S(2)}) collective-permute-start(bf16[640,640]{1,0:T(8,128)(2,1)S(1)} %reshape.102.t0), channel_id=1, source_target_pairs={{0,1},{1,2},{2,3},{3,0},{4,5},{5,6},{6,7},{7,4},{8,9},{9,10},{10,1... | collective-permute-start | bytes 2457608 | tf_op jit(solution)/shard_map/gather_width/ppermute | solution.py:224
  64.8 49.0 %collective-permute-start.9 = (bf16[640,640]{1,0:T(8,128)(2,1)S(1)}, bf16[640,640]{1,0:T(8,128)(2,1)S(1)}, u32[]{:S(2)}, u32[]{:S(2)}) collective-permute-start(bf16[640,640]{1,0:T(8,128)(2,1)S(1)} %reshape.102.t0), channel_id=1, source_target_pairs={{0,2},{1,3},{2,0},{3,1},{4,6},{5,7},{6,4},{7,5},{8,10},{9,11},{10,... | collective-permute-start | bytes 2457608 | tf_op jit(solution)/shard_map/gather_width/ppermute | solution.py:224
  112.2 1.6 copy-start.4
  120.2 1.5 copy-start.2
  121.7 1.6 copy-start.3
  141.0 31.2 %collective-permute-start.12 = (bf16[640,640]{1,0:T(8,128)(2,1)S(1)}, bf16[640,640]{1,0:T(8,128)(2,1)S(1)}, u32[]{:S(2)}, u32[]{:S(2)}) collective-permute-start(bf16[640,640]{1,0:T(8,128)(2,1)S(1)} %get-tuple-element.36), channel_id=1, source_target_pairs={{0,1},{1,2},{2,3},{3,0},{4,5},{5,6},{6,7},{7,4},{8,9},{9,10},{10,1... | collective-permute-start | bytes 2457608 | tf_op jit(solution)/shard_map/sum_quarters/ppermute | solution.py:227
  141.1 31.1 %collective-permute-start.14 = (bf16[640,640]{1,0:T(8,128)(2,1)S(1)}, bf16[640,640]{1,0:T(8,128)(2,1)S(1)}, u32[]{:S(2)}, u32[]{:S(2)}) collective-permute-start(bf16[640,640]{1,0:T(8,128)(2,1)S(1)} %get-tuple-element.38), channel_id=1, source_target_pairs={{0,3},{1,0},{2,1},{3,2},{4,7},{5,4},{6,5},{7,6},{8,11},{9,8},{10,9... | collective-permute-start | bytes 2457608 | tf_op jit(solution)/shard_map/sum_quarters/ppermute | solution.py:227
  144.3 27.9 %collective-permute-start.13 = (bf16[640,640]{1,0:T(8,128)(2,1)S(1)}, bf16[640,640]{1,0:T(8,128)(2,1)S(1)}, u32[]{:S(2)}, u32[]{:S(2)}) collective-permute-start(bf16[640,640]{1,0:T(8,128)(2,1)S(1)} %get-tuple-element.37), channel_id=1, source_target_pairs={{0,2},{1,3},{2,0},{3,1},{4,6},{5,7},{6,4},{7,5},{8,10},{9,11},{10,... | collective-permute-start | bytes 2457608 | tf_op jit(solution)/shard_map/sum_quarters/ppermute | solution.py:227
  208.1 10.1 %collective-permute-start.15 = (bf16[128,640]{1,0:T(8,128)(2,1)S(1)}, bf16[128,640]{1,0:T(8,128)(2,1)S(1)}, u32[]{:S(2)}, u32[]{:S(2)}) collective-permute-start(bf16[128,640]{1,0:T(8,128)(2,1)S(1)} %get-tuple-element.41), channel_id=1, source_target_pairs={{0,1},{1,2},{2,3},{3,0},{4,5},{5,6},{6,7},{7,4},{8,9},{9,10},{10,1... | collective-permute-start | bytes 491528 | tf_op jit(solution)/shard_map/return_tokens/ppermute | solution.py:227
  208.2 10.0 %collective-permute-start.16 = (bf16[128,640]{1,0:T(8,128)(2,1)S(1)}, bf16[128,640]{1,0:T(8,128)(2,1)S(1)}, u32[]{:S(2)}, u32[]{:S(2)}) collective-permute-start(bf16[128,640]{1,0:T(8,128)(2,1)S(1)} %get-tuple-element.40), channel_id=1, source_target_pairs={{0,2},{1,3},{2,0},{3,1},{4,6},{5,7},{6,4},{7,5},{8,10},{9,11},{10,... | collective-permute-start | bytes 491528 | tf_op jit(solution)/shard_map/return_tokens/ppermute | solution.py:227
  209.2 9.6 %collective-permute-start.17 = (bf16[128,640]{1,0:T(8,128)(2,1)S(1)}, bf16[128,640]{1,0:T(8,128)(2,1)S(1)}, u32[]{:S(2)}, u32[]{:S(2)}) collective-permute-start(bf16[128,640]{1,0:T(8,128)(2,1)S(1)} %get-tuple-element.39), channel_id=1, source_target_pairs={{0,3},{1,0},{2,1},{3,2},{4,7},{5,4},{6,5},{7,6},{8,11},{9,8},{10,9... | collective-permute-start | bytes 491528 | tf_op jit(solution)/shard_map/return_tokens/ppermute | solution.py:227

commit v2 on v1

v2 whole, which is shorter than its diff:
```python
import jax
import jax.numpy as jnp
from jax import lax
from jax.experimental import pallas as pl
from jax.experimental.pallas import tpu as pltpu
from jax.sharding import PartitionSpec as P

BF = jnp.bfloat16
F32 = jnp.float32
VMEM_LIMIT = 20 * 1024 * 1024


def cost(flops, nbytes, trans=0):
    return pl.CostEstimate(flops=flops, bytes_accessed=nbytes, transcendentals=trans)


def params(grid_rank=1):
    return pltpu.CompilerParams(
        dimension_semantics=("arbitrary",) * grid_rank, vmem_limit_bytes=VMEM_LIMIT
    )


def in_hbm(array):
    return pltpu.with_memory_space_constraint(array, pltpu.HBM)


def quarter_at(x_ref, ahead):
    return (x_ref[0] + ahead) & 3


def split_columns(array, x, offsets, scale=None):
    rows, columns = array.shape
    width = columns // 4

    def kernel(x_ref, *refs):
        scale_refs = refs[4:-4]
        for source, target in zip(refs[:4], refs[-4:]):
            if scale_refs:
                target[...] = (source[...].astype(F32) * scale_refs[0][...]).astype(BF)
            else:
                target[...] = source[...]

    def block(offset):
        return pl.BlockSpec((rows, width), lambda i, x_ref: (0, quarter_at(x_ref, offset)))

    extra = [] if scale is None else [scale]
    return pl.pallas_call(
        kernel,
        grid_spec=pltpu.PrefetchScalarGridSpec(
            num_scalar_prefetch=1,
            grid=(1,),
            in_specs=[block(offset) for offset in offsets]
            + [pl.BlockSpec((rows, 1), lambda i, x_ref: (0, 0)) for _ in extra],
            out_specs=[pl.BlockSpec((rows, width), lambda i, x_ref: (0, 0))] * 4,
        ),
        out_shape=[jax.ShapeDtypeStruct((rows, width), BF)] * 4,
        compiler_params=params(),
        cost_estimate=cost(rows * columns, 4 * rows * columns),
        name="split_columns",
    )(x, array, array, array, array, *extra)


def join_columns(blocks, x, offsets):
    rows, width = blocks[0].shape

    def kernel(x_ref, b0, b1, b2, b3, out):
        for offset, block in zip(offsets, (b0, b1, b2, b3)):
            start = pl.multiple_of(quarter_at(x_ref, offset) * width, 128)
            out[:, pl.ds(start, width)] = block[...]

    return pl.pallas_call(
        kernel,
        grid_spec=pltpu.PrefetchScalarGridSpec(
            num_scalar_prefetch=1,
            grid=(1,),
            in_specs=[pl.BlockSpec((rows, width), lambda i, x_ref: (0, 0))] * 4,
            out_specs=pl.BlockSpec((rows, 4 * width), lambda i, x_ref: (0, 0)),
        ),
        out_shape=jax.ShapeDtypeStruct((rows, 4 * width), BF),
        compiler_params=params(),
        cost_estimate=cost(0, 16 * rows * width),
        name="join_columns",
    )(x, *blocks)


HIDDEN_TILE = 512


def up_three(blocks, offsets, gate_weight, up_weight, x):
    rows, depth = blocks[0].shape
    hidden = gate_weight.shape[1]

    def kernel(x_ref, t0, t1, t2, g0, g1, g2, u0, u1, u2, gate, up):
        for out, weights in ((gate, (g0, g1, g2)), (up, (u0, u1, u2))):
            total = jnp.dot(t0[...], weights[0][...], preferred_element_type=F32)
            total += jnp.dot(t1[...], weights[1][...], preferred_element_type=F32)
            total += jnp.dot(t2[...], weights[2][...], preferred_element_type=F32)
            out[...] = total

    def weight(offset):
        return pl.BlockSpec((depth, HIDDEN_TILE), lambda j, x_ref: (quarter_at(x_ref, offset), j))

    whole = pl.BlockSpec((rows, depth), lambda j, x_ref: (0, 0))
    out = pl.BlockSpec((rows, HIDDEN_TILE), lambda j, x_ref: (0, j))
    return pl.pallas_call(
        kernel,
        grid_spec=pltpu.PrefetchScalarGridSpec(
            num_scalar_prefetch=1,
            grid=(hidden // HIDDEN_TILE,),
            in_specs=[whole] * 3 + [weight(offset) for offset in offsets] * 2,
            out_specs=[out, out],
        ),
        out_shape=[pltpu.HBM((rows, hidden), F32)] * 2,
        compiler_params=params(),
        cost_estimate=cost(12 * rows * depth * hidden, 12 * depth * hidden + 8 * rows * hidden),
        name="up_three",
    )(x, *blocks, *([gate_weight] * 3), *([up_weight] * 3))


CONTRACT_LAST = (((1,), (1,)), ((), ()))


def down_dot(gg, gu, wg, wu):
    total = lax.dot_general(gg, wg, CONTRACT_LAST, preferred_element_type=F32)
    return total + lax.dot_general(gu, wu, CONTRACT_LAST, preferred_element_type=F32)


def middle(upper, lower, gate, up, scaled, offset, gate_weight, up_weight, x):
    half, depth = upper.shape
    rows, hidden = gate.shape
    steps = hidden // HIDDEN_TILE

    def kernel(x_ref, top, bottom, g_in, u_in, h, wg, wu, gg_out, gu_out, out_top, out_bottom, total):
        step = pl.program_id(0)
        for k, (t, out) in enumerate(((top, out_top), (bottom, out_bottom))):
            part = slice(k * half, (k + 1) * half)
            g = g_in[part, :] + jnp.dot(t[...], wg[...], preferred_element_type=F32)
            u = u_in[part, :] + jnp.dot(t[...], wu[...], preferred_element_type=F32)
            s = 1.0 / (1.0 + jnp.exp(-g))
            hs = h[part, :].astype(F32) * s
            gg = (hs * u * (1.0 + g * (1.0 - s))).astype(BF)
            gu = (hs * g).astype(BF)
            gg_out[part, :] = gg
            gu_out[part, :] = gu
            value = down_dot(gg, gu, wg[...], wu[...])

            @pl.when(step == 0)
            def _():
                total[part, :] = value

            @pl.when((step > 0) & (step < steps - 1))
            def _():
                total[part, :] += value

            @pl.when(step == steps - 1)
            def _():
                out[...] = (total[part, :] + value).astype(BF)

    weight = pl.BlockSpec((depth, HIDDEN_TILE), lambda j, x_ref: (quarter_at(x_ref, offset), j))
    tiled = pl.BlockSpec((rows, HIDDEN_TILE), lambda j, x_ref: (0, j))
    halves = [pl.BlockSpec((half, depth), lambda j, x_ref: (0, 0))] * 2
    return pl.pallas_call(
        kernel,
        grid_spec=pltpu.PrefetchScalarGridSpec(
            num_scalar_prefetch=1,
            grid=(steps,),
            in_specs=halves + [tiled] * 3 + [weight] * 2,
            out_specs=[tiled] * 2 + halves,
            scratch_shapes=[pltpu.VMEM((rows, depth), F32)],
        ),
        out_shape=[jax.ShapeDtypeStruct((rows, hidden), BF)] * 2
        + [jax.ShapeDtypeStruct((half, depth), BF)] * 2,
        compiler_params=params(),
        cost_estimate=cost(
            8 * rows * depth * hidden, 4 * depth * hidden + 14 * rows * hidden, rows * hidden
        ),
        name="middle",
    )(x, upper, lower, in_hbm(gate), in_hbm(up), scaled, gate_weight, up_weight)


def down_halves(grad_gate, grad_up, gate_weight, up_weight, x, pieces, dtype):
    rows, hidden = grad_gate.shape
    depth = gate_weight.shape[0] // 4
    half = rows // 2
    count = len(pieces)

    def at_step(j, values):
        chosen = values[0]
        for k in range(1, count):
            chosen = jnp.where(j == k, values[k], chosen)
        return chosen

    def kernel(x_ref, gg, gu, wg, wu, *outs):
        for k in range(count):

            @pl.when(pl.program_id(0) == k)
            def _():
                outs[k][...] = down_dot(gg[...], gu[...], wg[...], wu[...]).astype(dtype)

    weight = pl.BlockSpec(
        (depth, hidden),
        lambda j, x_ref: (quarter_at(x_ref, at_step(j, [offset for offset, _ in pieces])), 0),
    )
    grads = pl.BlockSpec((half, hidden), lambda j, x_ref: (at_step(j, [k for _, k in pieces]), 0))
    return pl.pallas_call(
        kernel,
        grid_spec=pltpu.PrefetchScalarGridSpec(
            num_scalar_prefetch=1,
            grid=(count,),
            in_specs=[grads] * 2 + [weight] * 2,
            out_specs=[pl.BlockSpec((half, depth), lambda j, x_ref: (0, 0))] * count,
        ),
        out_shape=[jax.ShapeDtypeStruct((half, depth), dtype)] * count,
        compiler_params=params(),
        cost_estimate=cost(
            4 * count * half * depth * hidden, 4 * count * depth * hidden + 4 * count * half * hidden
        ),
        name="down_halves",
    )(x, grad_gate, grad_up, gate_weight, up_weight)


def sum_halves(upper, lower):
    rows, width = upper[0].shape
    count = len(upper)

    def kernel(*refs):
        out = refs[-1]
        for k, half in enumerate((refs[:count], refs[count : 2 * count])):
            total = half[0][...].astype(F32)
            for ref in half[1:]:
                total = total + ref[...].astype(F32)
            out[k * rows : (k + 1) * rows, :] = total.astype(BF)

    return pl.pallas_call(
        kernel,
        out_shape=jax.ShapeDtypeStruct((2 * rows, width), BF),
        compiler_params=pltpu.CompilerParams(vmem_limit_bytes=VMEM_LIMIT),
        cost_estimate=cost(4 * rows * width, 16 * rows * width),
        name="sum_halves",
    )(*upper, *lower)


def on_device(tokens, hidden_grad, routes, exponents, gate_weight, up_weight):
    etp = lax.axis_size("etp")
    experts = lax.axis_size("expert")
    own_rows, features = tokens.shape
    group_size = own_rows * etp
    capacity = 5 * group_size // (4 * experts)
    slots = experts * capacity
    quarter, hidden = features // 4, hidden_grad.shape[1] // 4
    place_x = lax.axis_index("etp").astype(jnp.int32)
    x = place_x.reshape(1)
    gate_w, up_w = in_hbm(gate_weight[0]), in_hbm(up_weight[0])
    tokens, hidden_grad = in_hbm(tokens), in_hbm(hidden_grad)

    def back(array, r):
        return lax.ppermute(array, "etp", [(i, (i - r) % etp) for i in range(etp)])

    def forward(array, r):
        return lax.ppermute(array, "etp", [(i, (i + r) % etp) for i in range(etp)])

    ahead = (0, 2, 1, 3)
    with jax.named_scope("group_exchange"):
        token_parts = split_columns(tokens, x, [-r for r in ahead])
        group_tokens = jnp.concatenate(
            [token_parts[0]] + [back(token_parts[k], ahead[k]) for k in (1, 2, 3)]
        )
        own_routes = routes[:, 0]
        group_routes = jnp.concatenate([own_routes] + [back(own_routes, r) for r in ahead[1:]])
        scales = jnp.exp2(exponents.astype(F32))[:, None]
        hidden_parts = split_columns(hidden_grad, x, [-r for r in ahead], scales)
        group_hidden = jnp.concatenate(
            [hidden_parts[0]] + [back(hidden_parts[k], ahead[k]) for k in (1, 2, 3)]
        )

    with jax.named_scope("slots"):
        row = jnp.arange(group_size, dtype=jnp.int32)
        block = row // own_rows
        offset = jnp.where(block == 1, 2, jnp.where(block == 2, 1, block))
        place = ((place_x + offset) & 3) * own_rows + row % own_rows
        earlier = (group_routes[:, None] == group_routes[None, :]) & (place[:, None] < place[None, :])
        rank = jnp.sum(earlier.astype(jnp.int32), axis=0)
        slot_index = group_routes * capacity + rank
        select = (jnp.arange(slots, dtype=jnp.int32)[:, None] == slot_index[None, :]).astype(BF)

    def pick(rows):
        return jnp.dot(select, rows, preferred_element_type=F32).astype(BF)

    def to_experts(array):
        return lax.all_to_all(array, "expert", split_axis=0, concat_axis=0, tiled=True)

    with jax.named_scope("send_tokens"):
        packed_tokens = pick(group_tokens).reshape(experts, capacity // 2, 2, quarter)
        own_block = to_experts(packed_tokens).reshape(slots, quarter)
    with jax.named_scope("send_hidden"):
        packed_hidden = pick(group_hidden).reshape(experts, capacity * hidden // 128, 128)
        scaled = to_experts(packed_hidden).reshape(slots, hidden)

    half = slots // 2
    with jax.named_scope("gather_width"):
        left_block, right_block = forward(own_block, 1), back(own_block, 1)
        far_upper, far_lower = forward(left_block[:half], 1), back(right_block[half:], 1)
    with jax.named_scope("pre_activations"):
        gate, up = up_three((own_block, right_block, left_block), (0, 1, 3), gate_w, up_w, x)
    with jax.named_scope("input_partials"):
        grad_gate, grad_up, far_top, far_bottom = middle(
            far_upper, far_lower, gate, up, scaled, 2, gate_w, up_w, x
        )
        right_bottom, left_top = down_halves(
            grad_gate, grad_up, gate_w, up_w, x, ((1, 1), (3, 0)), BF
        )
        right_top, left_bottom = down_halves(
            grad_gate, grad_up, gate_w, up_w, x, ((1, 0), (3, 1)), F32
        )
        own_top, own_bottom = down_halves(
            grad_gate, grad_up, gate_w, up_w, x, ((0, 0), (0, 1)), F32
        )
    with jax.named_scope("sum_quarters"):
        passed_top, passed_bottom = forward(far_top, 1), back(far_bottom, 1)
        from_left_bottom, from_right_top = forward(right_bottom, 1), back(left_top, 1)
        from_left_top = forward((right_top + passed_top.astype(F32)).astype(BF), 1)
        from_right_bottom = back((left_bottom + passed_bottom.astype(F32)).astype(BF), 1)
        summed = sum_halves(
            (own_top, from_left_top, from_right_top),
            (own_bottom, from_left_bottom, from_right_bottom),
        )
    with jax.named_scope("return_tokens"):
        returned = to_experts(summed.reshape(experts, capacity // 2, 2, quarter))
        rows = returned.reshape(slots, quarter)
        group_rows = lax.dot_general(
            select, rows, (((0,), (0,)), ((), ())), preferred_element_type=F32
        ).astype(BF)
        parts = [group_rows[k * own_rows : (k + 1) * own_rows] for k in range(4)]
        blocks = [parts[0]] + [forward(parts[k], ahead[k]) for k in (1, 2, 3)]
        return join_columns(blocks, x, [-r for r in ahead])


def solution(mesh):
    placed = (
        P(("expert", "etp"), None),
        P(("expert", "etp"), None),
        P(("expert", "etp"), None),
        P(("expert", "etp")),
        P("expert", None, "etp"),
        P("expert", None, "etp"),
    )
    return jax.shard_map(
        on_device, mesh=mesh, in_specs=placed, out_specs=P(("expert", "etp"), None), check_vma=False
    )
```

time: 221 us -> 183 us (0.83)
  waiting for transfers between devices: 87.2 us -> 59.9 us
  Pallas kernels: 42.6 us -> 34.3 us
  starting transfers between devices: 39.8 us -> 45.3 us
  local copies, waits for them, and re-layouts: 10.7 us -> 5.92 us
  other arithmetic: 3.41 us -> 0.49 us
    ppermute x6 -> x8, waiting for transfers between devices: 29.2 us -> 14.6 us  [forward(): return lax.ppermute(array, 'etp', [(i, (i + r) % etp) for i in range(etp)])]
    ppermute x12 -> x14, waiting for transfers between devices: 53.2 us -> 40.7 us  [back(): return lax.ppermute(array, 'etp', [(i, (i - r) % etp) for i in range(etp)])]
    pallas_call x4 -> x5, Pallas kernels: 29.6 us -> 21 us  [the longest x3 12.7 us: down_halves(): pl.pallas_call(kernel, grid_spec=pltpu.PrefetchScalarGridSpec(num_scalar_...]
    ppermute x12 -> x14, starting transfers between devices: 15.2 us -> 23.4 us  [back(): return lax.ppermute(array, 'etp', [(i, (i - r) % etp) for i in range(etp)])]
    unnamed x14 -> x4, local copies, waits for them, and re-layouts: 5.68 us -> 0.01 us
    ppermute x6 -> x8, starting transfers between devices: 6.62 us -> 3.92 us  [forward(): return lax.ppermute(array, 'etp', [(i, (i + r) % etp) for i in range(etp)])]
    another operation x2 -> x0, other arithmetic: 2.62 us -> none  [the longest x1 1.32 us: on_device(): order = jnp.stack([ahead[0], ahead[1], ahead[3], ahead[2]])]
  transfers between devices with their start and end apart: 20 -> 24, of which waited for: 12 -> 15; matrix products, arithmetic and copies ran while one was open for 3% -> 3% of each run, Pallas kernels for 11% -> 14%
where the time goes in v2:
time: 183 us; the launch traced here: 182 us
  waiting for transfers between devices  59.9 us (33%)
  starting transfers between devices  45.3 us (25%)
  Pallas kernels  34.3 us (19%)
  blocking collectives  34 us (19%)
  local copies, waits for them, and re-layouts  5.92 us (3%)
  matrix products  2.37 us (1%)
    ppermute x14, waiting for transfers between devices, back(): return lax.ppermute(array, 'etp', [(i, (i - r) % etp) for i in range(etp)])  40.7 us
    all_to_all x1, blocking collectives, to_experts(): lax.all_to_all(array, 'expert', split_axis=0, concat_axis=0, tiled=True)  34 us
    ppermute x14, starting transfers between devices, back(): return lax.ppermute(array, 'etp', [(i, (i - r) % etp) for i in range(etp)])  23.4 us
    all_to_all x2, starting transfers between devices, to_experts(): lax.all_to_all(array, 'expert', split_axis=0, concat_axis=0, tiled=True)  18 us
    ppermute x8, waiting for transfers between devices, forward(): return lax.ppermute(array, 'etp', [(i, (i + r) % etp) for i in range(etp)])  14.6 us
    pallas_call x3, Pallas kernels, down_halves(): pl.pallas_call(kernel, grid_spec=pltpu.PrefetchScalarGridSpec(num_scalar_...  12.7 us
    pallas_call x1, Pallas kernels, up_three(): pl.pallas_call(kernel, grid_spec=pltpu.PrefetchScalarGridSpec(num_scalar_...  9.75 us
    pallas_call x1, Pallas kernels, middle(): pl.pallas_call(kernel, grid_spec=pltpu.PrefetchScalarGridSpec(num_scalar_...  8 us
  transfers between devices with their start and end apart: 24, of which 15 were waited for; matrix products, arithmetic and copies ran while one was open for 3% of the time, Pallas kernels for 14%

profile of v2, /device:TPU:8, one launch (start us, length us, event | category | flops | bytes accessed | tf_op | source)
XLA Modules:
  0.0 182.4 jit_solution(8590191467672516050)
XLA Ops:
  0.0 1.5 collective-permute-start.2
  1.5 1.7 collective-permute-start.1
  3.2 1.8 collective-permute-start
  5.1 1.2 split_columns.2
  6.3 1.8 collective-permute-start.3
  8.1 1.5 collective-permute-start.4
  9.6 0.6 collective-permute-start.5
  10.2 0.2 convert_reduce_fusion
  10.5 4.3 %collective-permute-done.3 = bf16[128,640]{1,0:T(8,128)(2,1)S(1)} collective-permute-done((bf16[128,640]{1,0:T(8,128)(2,1)S(1)}, bf16[128,640]{1,0:T(8,128)(2,1)S(1)}, u32[]{:S(2)}, u32[]{:S(2)}) %collective-permute-start.3) | collective-permute-done | bytes 163872 | tf_op jit(solution)/shard_map/group_exchange/ppermute | solution.py:257
  14.8 0.1 collective-permute-done.4
  14.9 2.0 %collective-permute-done.5 = bf16[128,640]{1,0:T(8,128)(2,1)S(1)} collective-permute-done((bf16[128,640]{1,0:T(8,128)(2,1)S(1)}, bf16[128,640]{1,0:T(8,128)(2,1)S(1)}, u32[]{:S(2)}, u32[]{:S(2)}) %collective-permute-start.5) | collective-permute-done | bytes 163872 | tf_op jit(solution)/shard_map/group_exchange/ppermute | solution.py:257
  17.0 0.7 convolution_convert_fusion.1
  17.7 0.0 copy-start.1
  17.7 1.2 reshape.113
  18.9 12.1 %all-to-all-start = ((bf16[64,5,2,640]{3,2,1,0:T(2,128)(2,1)}), bf16[64,5,2,640]{3,2,1,0:T(2,128)(2,1)S(1)}, u32[]{:S(2)}, u32[]{:S(2)}) async-start(bf16[64,5,2,640]{3,2,1,0:T(2,128)(2,1)} %reshape.113), calls=%async_computation | async-start | bytes 1638400 | tf_op jit(solution)/shard_map/send_tokens/all_to_all | solution.py:290
  31.1 0.1 copy.8.refs_4_
  31.2 1.4 split_columns.3
  32.6 1.3 collective-permute-start.10
  33.9 1.2 collective-permute-start.11
  35.1 0.9 collective-permute-start.12
  35.9 7.5 %collective-permute-done.10 = bf16[128,1024]{1,0:T(8,128)(2,1)S(1)} collective-permute-done((bf16[128,1024]{1,0:T(8,128)(2,1)S(1)}, bf16[128,1024]{1,0:T(8,128)(2,1)S(1)}, u32[]{:S(2)}, u32[]{:S(2)}) %collective-permute-start.10) | collective-permute-done | bytes 262176 | tf_op jit(solution)/shard_map/group_exchange/ppermute | solution.py:257
  43.4 2.8 %collective-permute-done.11 = bf16[128,1024]{1,0:T(8,128)(2,1)S(1)} collective-permute-done((bf16[128,1024]{1,0:T(8,128)(2,1)S(1)}, bf16[128,1024]{1,0:T(8,128)(2,1)S(1)}, u32[]{:S(2)}, u32[]{:S(2)}) %collective-permute-start.11) | collective-permute-done | bytes 262176 | tf_op jit(solution)/shard_map/group_exchange/ppermute | solution.py:257
  46.2 2.0 %collective-permute-done.12 = bf16[128,1024]{1,0:T(8,128)(2,1)S(1)} collective-permute-done((bf16[128,1024]{1,0:T(8,128)(2,1)S(1)}, bf16[128,1024]{1,0:T(8,128)(2,1)S(1)}, u32[]{:S(2)}, u32[]{:S(2)}) %collective-permute-start.12) | collective-permute-done | bytes 262176 | tf_op jit(solution)/shard_map/group_exchange/ppermute | solution.py:257
  48.2 0.8 convolution_convert_fusion
  49.0 1.4 reshape.115
  50.5 4.4 %all-to-all-done = bf16[64,5,2,640]{3,2,1,0:T(2,128)(2,1)S(1)} async-done(((bf16[64,5,2,640]{3,2,1,0:T(2,128)(2,1)}), bf16[64,5,2,640]{3,2,1,0:T(2,128)(2,1)S(1)}, u32[]{:S(2)}, u32[]{:S(2)}) %all-to-all-start) | async-done | bytes 819232 | tf_op jit(solution)/shard_map/send_tokens/all_to_all | solution.py:290
  54.9 5.8 %all-to-all-start.1 = ((bf16[64,80,128]{2,1,0:T(8,128)(2,1)}), bf16[64,80,128]{2,1,0:T(8,128)(2,1)S(1)}, u32[]{:S(2)}, u32[]{:S(2)}) async-start(bf16[64,80,128]{2,1,0:T(8,128)(2,1)} %reshape.115), calls=%async_computation.1 | async-start | bytes 2621440 | tf_op jit(solution)/shard_map/send_hidden/all_to_all | solution.py:290
  60.8 0.3 reshape.114.t0
  61.1 0.9 collective-permute-start.8
  62.0 1.4 collective-permute-start.6
  63.4 18.3 %collective-permute-done.8.t1 = bf16[640,640]{1,0:T(8,128)(2,1)S(1)} collective-permute-done((bf16[640,640]{1,0:T(8,128)(2,1)S(1)}, bf16[640,640]{1,0:T(8,128)(2,1)S(1)}, u32[]{:S(2)}, u32[]{:S(2)}) %collective-permute-start.8) | collective-permute-done | bytes 819232 | tf_op jit(solution)/shard_map/gather_width/ppermute | solution.py:257
  81.6 0.8 slice.25
  82.4 1.8 %collective-permute-start.9 = (bf16[320,640]{1,0:T(8,128)(2,1)}, bf16[320,640]{1,0:T(8,128)(2,1)S(1)}, u32[]{:S(2)}, u32[]{:S(2)}) collective-permute-start(bf16[320,640]{1,0:T(8,128)(2,1)} %slice.25), channel_id=1, source_target_pairs={{0,3},{1,0},{2,1},{3,2},{4,7},{5,4},{6,5},{7,6},{8,11},{9,8},{10,9... | collective-permute-start | bytes 1228808 | tf_op jit(solution)/shard_map/gather_width/ppermute | solution.py:257
  84.3 0.8 slice.24
  85.1 0.2 collective-permute-start.7
  85.3 9.8 %up_three.1 = (f32[640,1024]{1,0:T(8,128)}, f32[640,1024]{1,0:T(8,128)}) custom-call(s32[1]{0:T(128)} %bitcast.x_ref, bf16[640,640]{1,0:T(8,128)(2,1)S(1)} %reshape.114.t0, bf16[640,640]{1,0:T(8,128)(2,1)S(1)} %collective-permute-done.8.t1, bf16[640,640]{1,0:T(8,128)(2,1)S(1)} %collective-permute-done.6.t2, bf16[2560,1024]{1,0:T(8,128)(2,1)} %bitcast.7, ...), custom_call_target="tpu_custom_call" | custom-call | flops 5033164800 | bytes 13107200 | tf_op jit(solution)/shard_map/pre_activations/up_three/pallas_call | solution.py:105
  95.0 0.2 all-to-all-done.1
  95.2 0.6 reshape.116.h
  95.8 1.1 collective-permute-done.7.top
  96.9 8.0 %middle.1 = (bf16[640,1024]{1,0:T(8,128)(2,1)S(1)}, bf16[640,1024]{1,0:T(8,128)(2,1)S(1)}, bf16[320,640]{1,0:T(8,128)(2,1)S(1)}, bf16[320,640]{1,0:T(8,128)(2,1)S(1)}) custom-call(s32[1]{0:T(128)} %bitcast.x_ref, bf16[320,640]{1,0:T(8,128)(2,1)S(1)} %collective-permute-done.7.top, bf16[320,640]{1,0:T(8,128)(2,1)S(1)} %collective-permute-done.9.bottom, ...), custom_call_target="tpu_custom_call" | custom-call | flops 3355443200 | bytes 11796480 | tf_op jit(solution)/shard_map/input_partials/middle/pallas_call | solution.py:162
  104.9 2.0 %collective-permute-start.17 = (bf16[320,640]{1,0:T(8,128)(2,1)S(1)}, bf16[320,640]{1,0:T(8,128)(2,1)S(1)}, u32[]{:S(2)}, u32[]{:S(2)}) collective-permute-start(bf16[320,640]{1,0:T(8,128)(2,1)S(1)} %get-tuple-element.44), channel_id=1, source_target_pairs={{0,3},{1,0},{2,1},{3,2},{4,7},{5,4},{6,5},{7,6},{8,11},{9,8},{10,9... | collective-permute-start | bytes 1228808 | tf_op jit(solution)/shard_map/sum_quarters/ppermute | solution.py:257
  106.9 0.2 collective-permute-start.13
  107.0 4.2 %down_halves.5 = (bf16[320,640]{1,0:T(8,128)(2,1)S(1)}, bf16[320,640]{1,0:T(8,128)(2,1)S(1)}) custom-call(s32[1]{0:T(128)} %bitcast.x_ref, bf16[640,1024]{1,0:T(8,128)(2,1)S(1)} %get-tuple-element.35.gg, bf16[640,1024]{1,0:T(8,128)(2,1)S(1)} %get-tuple-element.36.gu, bf16[2560,1024]{1,0:T(8,128)(2,1)} %bitcast.11, bf16[2560,1024]{1,0:T(8,128)(2,1)} %bitcast.18), custom_call_target="tpu_custom_call" | custom-call | flops 1677721600 | bytes 7864320 | tf_op jit(solution)/shard_map/input_partials/down_halves/pallas_call | solution.py:205
  111.2 3.2 %collective-permute-start.15 = (bf16[320,640]{1,0:T(8,128)(2,1)S(1)}, bf16[320,640]{1,0:T(8,128)(2,1)S(1)}, u32[]{:S(2)}, u32[]{:S(2)}) collective-permute-start(bf16[320,640]{1,0:T(8,128)(2,1)S(1)} %get-tuple-element.40), channel_id=1, source_target_pairs={{0,3},{1,0},{2,1},{3,2},{4,7},{5,4},{6,5},{7,6},{8,11},{9,8},{10,9... | collective-permute-start | bytes 1228808 | tf_op jit(solution)/shard_map/sum_quarters/ppermute | solution.py:257
  114.4 4.2 %down_halves.4 = (f32[320,640]{1,0:T(8,128)S(1)}, f32[320,640]{1,0:T(8,128)S(1)}) custom-call(s32[1]{0:T(128)} %bitcast.x_ref, bf16[640,1024]{1,0:T(8,128)(2,1)S(1)} %get-tuple-element.35.gg, bf16[640,1024]{1,0:T(8,128)(2,1)S(1)} %get-tuple-element.36.gu, bf16[2560,1024]{1,0:T(8,128)(2,1)} %bitcast.12, bf16[2560,1024]{1,0:T(8,128)(2,1)} %bitcast.19), custom_call_target="tpu_custom_call" | custom-call | flops 1677721600 | bytes 7864320 | tf_op jit(solution)/shard_map/input_partials/down_halves/pallas_call | solution.py:205
  118.7 0.1 add_convert_fusion
  118.8 3.3 %collective-permute-start.18 = (bf16[320,640]{1,0:T(8,128)(2,1)S(1)}, bf16[320,640]{1,0:T(8,128)(2,1)S(1)}, u32[]{:S(2)}, u32[]{:S(2)}) collective-permute-start(bf16[320,640]{1,0:T(8,128)(2,1)S(1)} %add_convert_fusion), channel_id=1, source_target_pairs={{0,3},{1,0},{2,1},{3,2},{4,7},{5,4},{6,5},{7,6},{8,11},{9,8},{10,9... | collective-permute-start | bytes 1228808 | tf_op jit(solution)/shard_map/sum_quarters/ppermute | solution.py:257
  122.1 0.1 add_convert_fusion.1
  122.2 0.1 collective-permute-start.14
  122.3 4.2 %down_halves.3 = (f32[320,640]{1,0:T(8,128)S(1)}, f32[320,640]{1,0:T(8,128)S(1)}) custom-call(s32[1]{0:T(128)} %bitcast.x_ref, bf16[640,1024]{1,0:T(8,128)(2,1)S(1)} %get-tuple-element.35.gg, bf16[640,1024]{1,0:T(8,128)(2,1)S(1)} %get-tuple-element.36.gu, bf16[2560,1024]{1,0:T(8,128)(2,1)} %bitcast.13, bf16[2560,1024]{1,0:T(8,128)(2,1)} %bitcast.20), custom_call_target="tpu_custom_call" | custom-call | flops 1677721600 | bytes 7864320 | tf_op jit(solution)/shard_map/input_partials/down_halves/pallas_call | solution.py:205
  126.5 1.9 %collective-permute-done.16.refs_4_ = bf16[320,640]{1,0:T(8,128)(2,1)S(1)} collective-permute-done((bf16[320,640]{1,0:T(8,128)(2,1)S(1)}, bf16[320,640]{1,0:T(8,128)(2,1)S(1)}, u32[]{:S(2)}, u32[]{:S(2)}) %collective-permute-start.16) | collective-permute-done | bytes 409632 | tf_op jit(solution)/shard_map/sum_quarters/ppermute | solution.py:260
  128.4 3.6 %collective-permute-done.18.refs_5_ = bf16[320,640]{1,0:T(8,128)(2,1)S(1)} collective-permute-done((bf16[320,640]{1,0:T(8,128)(2,1)S(1)}, bf16[320,640]{1,0:T(8,128)(2,1)S(1)}, u32[]{:S(2)}, u32[]{:S(2)}) %collective-permute-start.18) | collective-permute-done | bytes 409632 | tf_op jit(solution)/shard_map/sum_quarters/ppermute | solution.py:257
  132.1 3.4 %collective-permute-done.14.refs_1_ = bf16[320,640]{1,0:T(8,128)(2,1)S(1)} collective-permute-done((bf16[320,640]{1,0:T(8,128)(2,1)S(1)}, bf16[320,640]{1,0:T(8,128)(2,1)S(1)}, u32[]{:S(2)}, u32[]{:S(2)}) %collective-permute-start.14) | collective-permute-done | bytes 409632 | tf_op jit(solution)/shard_map/sum_quarters/ppermute | solution.py:260
  135.5 0.3 sum_halves.1
  135.8 0.3 reshape.117
  136.1 34.0 %all_to_all.15 = bf16[64,5,2,640]{3,2,1,0:T(2,128)(2,1)S(1)} all-to-all(bf16[64,5,2,640]{3,2,1,0:T(2,128)(2,1)S(1)} %reshape.117), channel_id=1, replica_groups=mesh['expert'=64,'etp'=4] {'expert'}, dimensions={0} | all-to-all | bytes 1638400 | tf_op jit(solution)/shard_map/return_tokens/all_to_all | solution.py:290
  170.0 0.3 reshape.118
  170.4 0.8 convolution_convert_fusion.2
  171.2 0.1 fusion.32
  171.3 0.4 collective-permute-start.21
  171.6 1.7 collective-permute-start.20
  173.4 5.0 %collective-permute-done.21.b3 = bf16[128,640]{1,0:T(8,128)(2,1)S(1)} collective-permute-done((bf16[128,640]{1,0:T(8,128)(2,1)S(1)}, bf16[128,640]{1,0:T(8,128)(2,1)S(1)}, u32[]{:S(2)}, u32[]{:S(2)}) %collective-permute-start.21) | collective-permute-done | bytes 163872 | tf_op jit(solution)/shard_map/return_tokens/ppermute | solution.py:260
  178.3 3.2 %collective-permute-done.20.b2 = bf16[128,640]{1,0:T(8,128)(2,1)S(1)} collective-permute-done((bf16[128,640]{1,0:T(8,128)(2,1)S(1)}, bf16[128,640]{1,0:T(8,128)(2,1)S(1)}, u32[]{:S(2)}, u32[]{:S(2)}) %collective-permute-start.20) | collective-permute-done | bytes 163872 | tf_op jit(solution)/shard_map/return_tokens/ppermute | solution.py:260
  181.5 0.9 join_columns.1
  (18 shorter events, 0.1 us)
Async XLA Ops:
  0.0 9.6 %collective-permute-start.2 = (s32[128]{0:T(128)}, s32[128]{0:T(128)S(1)}, u32[]{:S(2)}, u32[]{:S(2)}) collective-permute-start(s32[128]{0:T(128)} %bitcast.21), channel_id=1, source_target_pairs={{0,1},{1,2},{2,3},{3,0},{4,5},{5,6},{6,7},{7,4},{8,9},{9,10},{10,1... | collective-permute-start | bytes 1544 | tf_op jit(solution)/shard_map/group_exchange/ppermute | solution.py:257
  1.5 8.7 %collective-permute-start.1 = (s32[128]{0:T(128)}, s32[128]{0:T(128)S(1)}, u32[]{:S(2)}, u32[]{:S(2)}) collective-permute-start(s32[128]{0:T(128)} %bitcast.22), channel_id=1, source_target_pairs={{0,3},{1,0},{2,1},{3,2},{4,7},{5,4},{6,5},{7,6},{8,11},{9,8},{10,9... | collective-permute-start | bytes 1544 | tf_op jit(solution)/shard_map/group_exchange/ppermute | solution.py:257
  3.2 7.0 %collective-permute-start = (s32[128]{0:T(128)}, s32[128]{0:T(128)S(1)}, u32[]{:S(2)}, u32[]{:S(2)}) collective-permute-start(s32[128]{0:T(128)} %bitcast.23), channel_id=1, source_target_pairs={{0,2},{1,3},{2,0},{3,1},{4,6},{5,7},{6,4},{7,5},{8,10},{9,11},{10,... | collective-permute-start | bytes 1544 | tf_op jit(solution)/shard_map/group_exchange/ppermute | solution.py:257
  5.1 5.2 %copy-start = (s32[128,1]{0,1:T(1,128)S(1)}, s32[128,1]{0,1:T(1,128)}, u32[]{:S(2)}) copy-start(s32[128,1]{0,1:T(1,128)} %param.8) | copy-start | bytes 1540
  6.3 8.6 %collective-permute-start.3 = (bf16[128,640]{1,0:T(8,128)(2,1)S(1)}, bf16[128,640]{1,0:T(8,128)(2,1)S(1)}, u32[]{:S(2)}, u32[]{:S(2)}) collective-permute-start(bf16[128,640]{1,0:T(8,128)(2,1)S(1)} %get-tuple-element.26), channel_id=1, source_target_pairs={{0,2},{1,3},{2,0},{3,1},{4,6},{5,7},{6,4},{7,5},{8,10},{9,11},{10,... | collective-permute-start | bytes 491528 | tf_op jit(solution)/shard_map/group_exchange/ppermute | solution.py:257
  8.1 6.9 %collective-permute-start.4 = (bf16[128,640]{1,0:T(8,128)(2,1)S(1)}, bf16[128,640]{1,0:T(8,128)(2,1)S(1)}, u32[]{:S(2)}, u32[]{:S(2)}) collective-permute-start(bf16[128,640]{1,0:T(8,128)(2,1)S(1)} %get-tuple-element.27), channel_id=1, source_target_pairs={{0,3},{1,0},{2,1},{3,2},{4,7},{5,4},{6,5},{7,6},{8,11},{9,8},{10,9... | collective-permute-start | bytes 491528 | tf_op jit(solution)/shard_map/group_exchange/ppermute | solution.py:257
  9.6 7.4 %collective-permute-start.5 = (bf16[128,640]{1,0:T(8,128)(2,1)S(1)}, bf16[128,640]{1,0:T(8,128)(2,1)S(1)}, u32[]{:S(2)}, u32[]{:S(2)}) collective-permute-start(bf16[128,640]{1,0:T(8,128)(2,1)S(1)} %get-tuple-element.28), channel_id=1, source_target_pairs={{0,1},{1,2},{2,3},{3,0},{4,5},{5,6},{6,7},{7,4},{8,9},{9,10},{10,1... | collective-permute-start | bytes 491528 | tf_op jit(solution)/shard_map/group_exchange/ppermute | solution.py:257
  17.7 13.3 %copy-start.1 = (s32[128]{0:T(128)S(1)}, s32[128]{0:T(128)}, u32[]{:S(2)}) copy-start(s32[128]{0:T(128)} %param.9) | copy-start | bytes 1540
  18.9 36.0 %all-to-all-start = ((bf16[64,5,2,640]{3,2,1,0:T(2,128)(2,1)}), bf16[64,5,2,640]{3,2,1,0:T(2,128)(2,1)S(1)}, u32[]{:S(2)}, u32[]{:S(2)}) async-start(bf16[64,5,2,640]{3,2,1,0:T(2,128)(2,1)} %reshape.113), calls=%async_computation | async-start | bytes 1638400 | tf_op jit(solution)/shard_map/send_tokens/all_to_all | solution.py:290
  32.6 10.8 %collective-permute-start.10 = (bf16[128,1024]{1,0:T(8,128)(2,1)S(1)}, bf16[128,1024]{1,0:T(8,128)(2,1)S(1)}, u32[]{:S(2)}, u32[]{:S(2)}) collective-permute-start(bf16[128,1024]{1,0:T(8,128)(2,1)S(1)} %get-tuple-element.32), channel_id=1, source_target_pairs={{0,2},{1,3},{2,0},{3,1},{4,6},{5,7},{6,4},{7,5},{8,10},{9,11},{10,... | collective-permute-start | bytes 786440 | tf_op jit(solution)/shard_map/group_exchange/ppermute | solution.py:257
  33.9 12.3 %collective-permute-start.11 = (bf16[128,1024]{1,0:T(8,128)(2,1)S(1)}, bf16[128,1024]{1,0:T(8,128)(2,1)S(1)}, u32[]{:S(2)}, u32[]{:S(2)}) collective-permute-start(bf16[128,1024]{1,0:T(8,128)(2,1)S(1)} %get-tuple-element.33), channel_id=1, source_target_pairs={{0,3},{1,0},{2,1},{3,2},{4,7},{5,4},{6,5},{7,6},{8,11},{9,8},{10,9... | collective-permute-start | bytes 786440 | tf_op jit(solution)/shard_map/group_exchange/ppermute | solution.py:257
  35.1 13.1 %collective-permute-start.12 = (bf16[128,1024]{1,0:T(8,128)(2,1)S(1)}, bf16[128,1024]{1,0:T(8,128)(2,1)S(1)}, u32[]{:S(2)}, u32[]{:S(2)}) collective-permute-start(bf16[128,1024]{1,0:T(8,128)(2,1)S(1)} %get-tuple-element.34), channel_id=1, source_target_pairs={{0,1},{1,2},{2,3},{3,0},{4,5},{5,6},{6,7},{7,4},{8,9},{9,10},{10,1... | collective-permute-start | bytes 786440 | tf_op jit(solution)/shard_map/group_exchange/ppermute | solution.py:257
  54.9 40.3 %all-to-all-start.1 = ((bf16[64,80,128]{2,1,0:T(8,128)(2,1)}), bf16[64,80,128]{2,1,0:T(8,128)(2,1)S(1)}, u32[]{:S(2)}, u32[]{:S(2)}) async-start(bf16[64,80,128]{2,1,0:T(8,128)(2,1)} %reshape.115), calls=%async_computation.1 | async-start | bytes 2621440 | tf_op jit(solution)/shard_map/send_hidden/all_to_all | solution.py:290
  61.1 20.6 %collective-permute-start.8 = (bf16[640,640]{1,0:T(8,128)(2,1)S(1)}, bf16[640,640]{1,0:T(8,128)(2,1)S(1)}, u32[]{:S(2)}, u32[]{:S(2)}) collective-permute-start(bf16[640,640]{1,0:T(8,128)(2,1)S(1)} %reshape.114.t0), channel_id=1, source_target_pairs={{0,3},{1,0},{2,1},{3,2},{4,7},{5,4},{6,5},{7,6},{8,11},{9,8},{10,9... | collective-permute-start | bytes 2457608 | tf_op jit(solution)/shard_map/gather_width/ppermute | solution.py:257
  62.0 22.3 %collective-permute-start.6 = (bf16[640,640]{1,0:T(8,128)(2,1)S(1)}, bf16[640,640]{1,0:T(8,128)(2,1)S(1)}, u32[]{:S(2)}, u32[]{:S(2)}) collective-permute-start(bf16[640,640]{1,0:T(8,128)(2,1)S(1)} %reshape.114.t0), channel_id=1, source_target_pairs={{0,1},{1,2},{2,3},{3,0},{4,5},{5,6},{6,7},{7,4},{8,9},{9,10},{10,1... | collective-permute-start | bytes 2457608 | tf_op jit(solution)/shard_map/gather_width/ppermute | solution.py:260
  82.4 13.3 %collective-permute-start.9 = (bf16[320,640]{1,0:T(8,128)(2,1)}, bf16[320,640]{1,0:T(8,128)(2,1)S(1)}, u32[]{:S(2)}, u32[]{:S(2)}) collective-permute-start(bf16[320,640]{1,0:T(8,128)(2,1)} %slice.25), channel_id=1, source_target_pairs={{0,3},{1,0},{2,1},{3,2},{4,7},{5,4},{6,5},{7,6},{8,11},{9,8},{10,9... | collective-permute-start | bytes 1228808 | tf_op jit(solution)/shard_map/gather_width/ppermute | solution.py:257
  85.1 11.8 %collective-permute-start.7 = (bf16[320,640]{1,0:T(8,128)(2,1)}, bf16[320,640]{1,0:T(8,128)(2,1)S(1)}, u32[]{:S(2)}, u32[]{:S(2)}) collective-permute-start(bf16[320,640]{1,0:T(8,128)(2,1)} %slice.24), channel_id=1, source_target_pairs={{0,1},{1,2},{2,3},{3,0},{4,5},{5,6},{6,7},{7,4},{8,9},{9,10},{10,1... | collective-permute-start | bytes 1228808 | tf_op jit(solution)/shard_map/gather_width/ppermute | solution.py:260
  104.9 13.7 %collective-permute-start.17 = (bf16[320,640]{1,0:T(8,128)(2,1)S(1)}, bf16[320,640]{1,0:T(8,128)(2,1)S(1)}, u32[]{:S(2)}, u32[]{:S(2)}) collective-permute-start(bf16[320,640]{1,0:T(8,128)(2,1)S(1)} %get-tuple-element.44), channel_id=1, source_target_pairs={{0,3},{1,0},{2,1},{3,2},{4,7},{5,4},{6,5},{7,6},{8,11},{9,8},{10,9... | collective-permute-start | bytes 1228808 | tf_op jit(solution)/shard_map/sum_quarters/ppermute | solution.py:257
  106.9 15.2 %collective-permute-start.13 = (bf16[320,640]{1,0:T(8,128)(2,1)S(1)}, bf16[320,640]{1,0:T(8,128)(2,1)S(1)}, u32[]{:S(2)}, u32[]{:S(2)}) collective-permute-start(bf16[320,640]{1,0:T(8,128)(2,1)S(1)} %get-tuple-element.39), channel_id=1, source_target_pairs={{0,1},{1,2},{2,3},{3,0},{4,5},{5,6},{6,7},{7,4},{8,9},{9,10},{10,1... | collective-permute-start | bytes 1228808 | tf_op jit(solution)/shard_map/sum_quarters/ppermute | solution.py:260
  111.2 15.3 %collective-permute-start.15 = (bf16[320,640]{1,0:T(8,128)(2,1)S(1)}, bf16[320,640]{1,0:T(8,128)(2,1)S(1)}, u32[]{:S(2)}, u32[]{:S(2)}) collective-permute-start(bf16[320,640]{1,0:T(8,128)(2,1)S(1)} %get-tuple-element.40), channel_id=1, source_target_pairs={{0,3},{1,0},{2,1},{3,2},{4,7},{5,4},{6,5},{7,6},{8,11},{9,8},{10,9... | collective-permute-start | bytes 1228808 | tf_op jit(solution)/shard_map/sum_quarters/ppermute | solution.py:257
  114.4 14.0 %collective-permute-start.16 = (bf16[320,640]{1,0:T(8,128)(2,1)S(1)}, bf16[320,640]{1,0:T(8,128)(2,1)S(1)}, u32[]{:S(2)}, u32[]{:S(2)}) collective-permute-start(bf16[320,640]{1,0:T(8,128)(2,1)S(1)} %get-tuple-element.42), channel_id=1, source_target_pairs={{0,1},{1,2},{2,3},{3,0},{4,5},{5,6},{6,7},{7,4},{8,9},{9,10},{10,1... | collective-permute-start | bytes 1228808 | tf_op jit(solution)/shard_map/sum_quarters/ppermute | solution.py:260
  118.8 13.3 %collective-permute-start.18 = (bf16[320,640]{1,0:T(8,128)(2,1)S(1)}, bf16[320,640]{1,0:T(8,128)(2,1)S(1)}, u32[]{:S(2)}, u32[]{:S(2)}) collective-permute-start(bf16[320,640]{1,0:T(8,128)(2,1)S(1)} %add_convert_fusion), channel_id=1, source_target_pairs={{0,3},{1,0},{2,1},{3,2},{4,7},{5,4},{6,5},{7,6},{8,11},{9,8},{10,9... | collective-permute-start | bytes 1228808 | tf_op jit(solution)/shard_map/sum_quarters/ppermute | solution.py:257
  122.2 13.3 %collective-permute-start.14 = (bf16[320,640]{1,0:T(8,128)(2,1)S(1)}, bf16[320,640]{1,0:T(8,128)(2,1)S(1)}, u32[]{:S(2)}, u32[]{:S(2)}) collective-permute-start(bf16[320,640]{1,0:T(8,128)(2,1)S(1)} %add_convert_fusion.1), channel_id=1, source_target_pairs={{0,1},{1,2},{2,3},{3,0},{4,5},{5,6},{6,7},{7,4},{8,9},{9,10},{10,1... | collective-permute-start | bytes 1228808 | tf_op jit(solution)/shard_map/sum_quarters/ppermute | solution.py:260
  171.3 7.1 %collective-permute-start.21 = (bf16[128,640]{1,0:T(8,128)(2,1)S(1)}, bf16[128,640]{1,0:T(8,128)(2,1)S(1)}, u32[]{:S(2)}, u32[]{:S(2)}) collective-permute-start(bf16[128,640]{1,0:T(8,128)(2,1)S(1)} %get-tuple-element.45), channel_id=1, source_target_pairs={{0,3},{1,0},{2,1},{3,2},{4,7},{5,4},{6,5},{7,6},{8,11},{9,8},{10,9... | collective-permute-start | bytes 491528 | tf_op jit(solution)/shard_map/return_tokens/ppermute | solution.py:260
  171.6 9.9 %collective-permute-start.20 = (bf16[128,640]{1,0:T(8,128)(2,1)S(1)}, bf16[128,640]{1,0:T(8,128)(2,1)S(1)}, u32[]{:S(2)}, u32[]{:S(2)}) collective-permute-start(bf16[128,640]{1,0:T(8,128)(2,1)S(1)} %get-tuple-element.46), channel_id=1, source_target_pairs={{0,1},{1,2},{2,3},{3,0},{4,5},{5,6},{6,7},{7,4},{8,9},{9,10},{10,1... | collective-permute-start | bytes 491528 | tf_op jit(solution)/shard_map/return_tokens/ppermute | solution.py:260
  173.4 8.2 %collective-permute-start.19 = (bf16[128,640]{1,0:T(8,128)(2,1)S(1)}, bf16[128,640]{1,0:T(8,128)(2,1)S(1)}, u32[]{:S(2)}, u32[]{:S(2)}) collective-permute-start(bf16[128,640]{1,0:T(8,128)(2,1)S(1)} %get-tuple-element.47), channel_id=1, source_target_pairs={{0,2},{1,3},{2,0},{3,1},{4,6},{5,7},{6,4},{7,5},{8,10},{9,11},{10,... | collective-permute-start | bytes 491528 | tf_op jit(solution)/shard_map/return_tokens/ppermute | solution.py:260

commit v3 on v2

--- a/solution.py
+++ b/solution.py
@@ -83,38 +83,99 @@
     )(x, *blocks)
 
 
+def slot_matrix(route_blocks, x, offsets, experts, capacity):
+    own_rows = route_blocks[0].shape[1]
+    group = own_rows * len(offsets)
+    slots = experts * capacity
+
+    def kernel(x_ref, r0, r1, r2, r3, out):
+        routes = jnp.concatenate([r[...] for r in (r0, r1, r2, r3)], axis=1)
+
+        def places(axis):
+            row = lax.broadcasted_iota(jnp.int32, (group, group), axis)
+            block = row // own_rows
+            offset = jnp.zeros_like(row)
+            for k, value in enumerate(offsets):
+                offset = jnp.where(block == k, value, offset)
+            return ((x_ref[0] + offset) & 3) * own_rows + row % own_rows
+
+        before = jnp.where(places(0) < places(1), 1.0, 0.0).astype(BF)
+        same = lax.broadcasted_iota(jnp.int32, (experts, group), 0) == routes
+        named = jnp.where(same, 1.0, 0.0)
+        counts = jnp.dot(named.astype(BF), before, preferred_element_type=F32)
+        rank = jnp.sum(named * counts, axis=0, keepdims=True).astype(jnp.int32)
+        slot = routes * capacity + rank
+        filled = lax.broadcasted_iota(jnp.int32, (slots, group), 0) == slot
+        out[...] = jnp.where(filled, 1.0, 0.0).astype(BF)
+
+    block = pl.BlockSpec((1, own_rows), lambda i, x_ref: (0, 0))
+    return pl.pallas_call(
+        kernel,
+        grid_spec=pltpu.PrefetchScalarGridSpec(
+            num_scalar_prefetch=1,
+            grid=(1,),
+            in_specs=[block] * 4,
+            out_specs=pl.BlockSpec((slots, group), lambda i, x_ref: (0, 0)),
+        ),
+        out_shape=jax.ShapeDtypeStruct((slots, group), BF),
+        compiler_params=params(),
+        cost_estimate=cost(0, 0),
+        name="slot_matrix",
+    )(x, *route_blocks)
+
+
 HIDDEN_TILE = 512
 
 
-def up_three(blocks, offsets, gate_weight, up_weight, x):
-    rows, depth = blocks[0].shape
+def up_sums(uppers, lowers, offsets, gate_weight, up_weight, x, so_far=()):
+    half, depth = uppers[0].shape
     hidden = gate_weight.shape[1]
-
-    def kernel(x_ref, t0, t1, t2, g0, g1, g2, u0, u1, u2, gate, up):
-        for out, weights in ((gate, (g0, g1, g2)), (up, (u0, u1, u2))):
-            total = jnp.dot(t0[...], weights[0][...], preferred_element_type=F32)
-            total += jnp.dot(t1[...], weights[1][...], preferred_element_type=F32)
-            total += jnp.dot(t2[...], weights[2][...], preferred_element_type=F32)
-            out[...] = total
+    rows, count = 2 * half, len(offsets)
+    tile = 256
+
+    def kernel(x_ref, *refs):
+        gate, up = refs[-2:]
+        starts = refs[4 * count : -2]
+        for k in range(2):
+            part = slice(k * half, (k + 1) * half)
+            blocks = refs[k * count : (k + 1) * count]
+            for n, out in enumerate((gate, up)):
+                weights = refs[(2 + n) * count : (3 + n) * count]
+                total = jnp.dot(blocks[0][...], weights[0][...], preferred_element_type=F32)
+                for block, w in zip(blocks[1:], weights[1:]):
+                    total += jnp.dot(block[...], w[...], preferred_element_type=F32)
+                if starts:
+                    total += starts[n][part, :]
+                out[part, :] = total
 
     def weight(offset):
-        return pl.BlockSpec((depth, HIDDEN_TILE), lambda j, x_ref: (quarter_at(x_ref, offset), j))
-
-    whole = pl.BlockSpec((rows, depth), lambda j, x_ref: (0, 0))
-    out = pl.BlockSpec((rows, HIDDEN_TILE), lambda j, x_ref: (0, j))
-    return pl.pallas_call(
-        kernel,
-        grid_spec=pltpu.PrefetchScalarGridSpec(
-            num_scalar_prefetch=1,
-            grid=(hidden // HIDDEN_TILE,),
-            in_specs=[whole] * 3 + [weight(offset) for offset in offsets] * 2,
-            out_specs=[out, out],
+        return pl.BlockSpec((depth, tile), lambda j, x_ref: (quarter_at(x_ref, offset), j))
+
+    tiled = pl.BlockSpec((rows, tile), lambda j, x_ref: (0, j))
+    return pl.pallas_call(
+        kernel,
+        grid_spec=pltpu.PrefetchScalarGridSpec(
+            num_scalar_prefetch=1,
+            grid=(hidden // tile,),
+            in_specs=[pl.BlockSpec((half, depth), lambda j, x_ref: (0, 0))] * (2 * count)
+            + [weight(offset) for offset in offsets] * 2
+            + [tiled] * len(so_far),
+            out_specs=[tiled, tiled],
         ),
         out_shape=[pltpu.HBM((rows, hidden), F32)] * 2,
         compiler_params=params(),
-        cost_estimate=cost(12 * rows * depth * hidden, 12 * depth * hidden + 8 * rows * hidden),
-        name="up_three",
-    )(x, *blocks, *([gate_weight] * 3), *([up_weight] * 3))
+        cost_estimate=cost(
+            4 * count * rows * depth * hidden, 4 * count * depth * hidden + 16 * rows * hidden
+        ),
+        name="up_sums",
+    )(
+        x,
+        *uppers,
+        *lowers,
+        *([gate_weight] * count),
+        *([up_weight] * count),
+        *(in_hbm(array) for array in so_far),
+    )
 
 
 CONTRACT_LAST = (((1,), (1,)), ((), ()))
@@ -213,7 +274,7 @@
         out_shape=[jax.ShapeDtypeStruct((half, depth), dtype)] * count,
         compiler_params=params(),
         cost_estimate=cost(
-            4 * count * half * depth * hidden, 4 * count * depth * hidden + 4 * count * half * hidden
+            1 * count * half * depth * hidden, 4 * count * depth * hidden + 4 * count * half * hidden
         ),
         name="down_halves",
     )(x, grad_gate, grad_up, gate_weight, up_weight)
@@ -244,12 +305,10 @@
     etp = lax.axis_size("etp")
     experts = lax.axis_size("expert")
     own_rows, features = tokens.shape
-    group_size = own_rows * etp
-    capacity = 5 * group_size // (4 * experts)
+    capacity = 5 * own_rows * etp // (4 * experts)
     slots = experts * capacity
     quarter, hidden = features // 4, hidden_grad.shape[1] // 4
-    place_x = lax.axis_index("etp").astype(jnp.int32)
-    x = place_x.reshape(1)
+    x = lax.axis_index("etp").astype(jnp.int32).reshape(1)
     gate_w, up_w = in_hbm(gate_weight[0]), in_hbm(up_weight[0])
     tokens, hidden_grad = in_hbm(tokens), in_hbm(hidden_grad)
 
@@ -265,8 +324,8 @@
         group_tokens = jnp.concatenate(
             [token_parts[0]] + [back(token_parts[k], ahead[k]) for k in (1, 2, 3)]
         )
-        own_routes = routes[:, 0]
-        group_routes = jnp.concatenate([own_routes] + [back(own_routes, r) for r in ahead[1:]])
+        own_routes = routes.reshape(1, own_rows)
+        route_blocks = [own_routes] + [back(own_routes, r) for r in ahead[1:]]
         scales = jnp.exp2(exponents.astype(F32))[:, None]
         hidden_parts = split_columns(hidden_grad, x, [-r for r in ahead], scales)
         group_hidden = jnp.concatenate(
@@ -274,14 +333,7 @@
         )
 
     with jax.named_scope("slots"):
-        row = jnp.arange(group_size, dtype=jnp.int32)
-        block = row // own_rows
-        offset = jnp.where(block == 1, 2, jnp.where(block == 2, 1, block))
-        place = ((place_x + offset) & 3) * own_rows + row % own_rows
-        earlier = (group_routes[:, None] == group_routes[None, :]) & (place[:, None] < place[None, :])
-        rank = jnp.sum(earlier.astype(jnp.int32), axis=0)
-        slot_index = group_routes * capacity + rank
-        select = (jnp.arange(slots, dtype=jnp.int32)[:, None] == slot_index[None, :]).astype(BF)
+        select = slot_matrix(route_blocks, x, ahead, experts, capacity)
 
     def pick(rows):
         return jnp.dot(select, rows, preferred_element_type=F32).astype(BF)
@@ -291,17 +343,24 @@
 
     with jax.named_scope("send_tokens"):
         packed_tokens = pick(group_tokens).reshape(experts, capacity // 2, 2, quarter)
-        own_block = to_experts(packed_tokens).reshape(slots, quarter)
+        arrived = to_experts(packed_tokens)
+        top = arrived[: experts // 2].reshape(slots // 2, quarter)
+        bottom = arrived[experts // 2 :].reshape(slots // 2, quarter)
     with jax.named_scope("send_hidden"):
         packed_hidden = pick(group_hidden).reshape(experts, capacity * hidden // 128, 128)
         scaled = to_experts(packed_hidden).reshape(slots, hidden)
 
-    half = slots // 2
     with jax.named_scope("gather_width"):
-        left_block, right_block = forward(own_block, 1), back(own_block, 1)
-        far_upper, far_lower = forward(left_block[:half], 1), back(right_block[half:], 1)
+        own_sums = up_sums((top,), (bottom,), (0,), gate_w, up_w, x)
+        left_top, right_bottom, *own_sums = lax.optimization_barrier(
+            (forward(top, 1), back(bottom, 1), *own_sums)
+        )
+        far_upper, far_lower = forward(left_top, 1), back(right_bottom, 1)
+        left_bottom, right_top = forward(bottom, 1), back(top, 1)
     with jax.named_scope("pre_activations"):
-        gate, up = up_three((own_block, right_block, left_block), (0, 1, 3), gate_w, up_w, x)
+        gate, up = up_sums(
+            (right_top, left_top), (right_bottom, left_bottom), (1, 3), gate_w, up_w, x, own_sums
+        )
     with jax.named_scope("input_partials"):
         grad_gate, grad_up, far_top, far_bottom = middle(
             far_upper, far_lower, gate, up, scaled, 2, gate_w, up_w, x

time: 183 us -> 184 us (level)
  waiting for transfers between devices: 59.9 us -> 47.3 us
  starting transfers between devices: 45.3 us -> 52.8 us
  Pallas kernels: 34.3 us -> 39.9 us
    ppermute x14 -> x15, waiting for transfers between devices: 40.7 us -> 27.2 us  [back(): return lax.ppermute(array, 'etp', [(i, (i - r) % etp) for i in range(etp)])]
    pallas_call x1 -> x3, Pallas kernels: 9.75 us -> 15.2 us  [the longest x2 14.7 us: up_sums(): pl.pallas_call(kernel, grid_spec=pltpu.PrefetchScalarGridSpec(num_scalar_...]
    ppermute x14 -> x15, starting transfers between devices: 23.4 us -> 27.8 us  [back(): return lax.ppermute(array, 'etp', [(i, (i - r) % etp) for i in range(etp)])]
    ppermute x8 -> x9, starting transfers between devices: 3.92 us -> 6.9 us  [forward(): return lax.ppermute(array, 'etp', [(i, (i + r) % etp) for i in range(etp)])]
    all_to_all x2, waiting for transfers between devices: 4.62 us -> 6.49 us  [to_experts(): lax.all_to_all(array, 'expert', split_axis=0, concat_axis=0, tiled=True)]
    ppermute x8 -> x9, waiting for transfers between devices: 14.6 us -> 13.6 us  [forward(): return lax.ppermute(array, 'etp', [(i, (i + r) % etp) for i in range(etp)])]
  transfers between devices with their start and end apart: 24 -> 26, of which waited for: 15 -> 15; matrix products, arithmetic and copies ran while one was open for 3% -> 3% of each run, Pallas kernels for 14% -> 16%
where the time goes in v3:
time: 184 us; the launch traced here: 182 us
  starting transfers between devices  52.8 us (29%)
  waiting for transfers between devices  47.3 us (26%)
  Pallas kernels  39.9 us (22%)
  blocking collectives  33 us (18%)
  local copies, waits for them, and re-layouts  6.67 us (4%)
  matrix products  2.32 us (1%)
    all_to_all x1, blocking collectives, to_experts(): lax.all_to_all(array, 'expert', split_axis=0, concat_axis=0, tiled=True)  33 us
    ppermute x15, starting transfers between devices, back(): return lax.ppermute(array, 'etp', [(i, (i - r) % etp) for i in range(etp)])  27.8 us
    ppermute x15, waiting for transfers between devices, back(): return lax.ppermute(array, 'etp', [(i, (i - r) % etp) for i in range(etp)])  27.2 us
    all_to_all x2, starting transfers between devices, to_experts(): lax.all_to_all(array, 'expert', split_axis=0, concat_axis=0, tiled=True)  18.1 us
    pallas_call x2, Pallas kernels, up_sums(): pl.pallas_call(kernel, grid_spec=pltpu.PrefetchScalarGridSpec(num_scalar_...  14.7 us
    ppermute x9, waiting for transfers between devices, forward(): return lax.ppermute(array, 'etp', [(i, (i + r) % etp) for i in range(etp)])  13.6 us
    pallas_call x3, Pallas kernels, down_halves(): pl.pallas_call(kernel, grid_spec=pltpu.PrefetchScalarGridSpec(num_scalar_...  12.7 us
    pallas_call x1, Pallas kernels, middle(): pl.pallas_call(kernel, grid_spec=pltpu.PrefetchScalarGridSpec(num_scalar_...  8.15 us
  transfers between devices with their start and end apart: 26, of which 15 were waited for; matrix products, arithmetic and copies ran while one was open for 3% of the time, Pallas kernels for 16%

profile of v3, /device:TPU:8, one launch (start us, length us, event | category | flops | bytes accessed | tf_op | source)
XLA Modules:
  0.0 182.3 jit_solution(7636927699502872660)
XLA Ops:
  0.0 1.2 split_columns.2
  1.2 3.1 %collective-permute-start.3 = (bf16[128,640]{1,0:T(8,128)(2,1)S(1)}, bf16[128,640]{1,0:T(8,128)(2,1)S(1)}, u32[]{:S(2)}, u32[]{:S(2)}) collective-permute-start(bf16[128,640]{1,0:T(8,128)(2,1)S(1)} %get-tuple-element.32), channel_id=1, source_target_pairs={{0,2},{1,3},{2,0},{3,1},{4,6},{5,7},{6,4},{7,5},{8,10},{9,11},{10,... | collective-permute-start | bytes 491528 | tf_op jit(solution)/shard_map/group_exchange/ppermute | solution.py:316
  4.3 1.1 collective-permute-start.4
  5.5 0.9 collective-permute-start.5
  6.4 0.6 collective-permute-start
  7.0 2.6 %collective-permute-start.1 = (s32[1,128]{1,0:T(1,128)S(1)}, s32[1,128]{1,0:T(1,128)S(1)}, u32[]{:S(2)}, u32[]{:S(2)}) collective-permute-start(s32[1,128]{1,0:T(1,128)S(1)} %bitcast.11), channel_id=1, source_target_pairs={{0,3},{1,0},{2,1},{3,2},{4,7},{5,4},{6,5},{7,6},{8,11},{9,8},{10,9... | collective-permute-start | bytes 1544 | tf_op jit(solution)/shard_map/group_exchange/ppermute | solution.py:316
  9.6 2.6 %collective-permute-done.r1 = s32[1,128]{1,0:T(1,128)S(1)} collective-permute-done((s32[1,128]{1,0:T(1,128)S(1)}, s32[1,128]{1,0:T(1,128)S(1)}, u32[]{:S(2)}, u32[]{:S(2)}) %collective-permute-start) | collective-permute-done | bytes 544 | tf_op jit(solution)/shard_map/group_exchange/ppermute | solution.py:316
  12.3 1.5 collective-permute-start.2
  13.8 3.2 %collective-permute-done.2.r3 = s32[1,128]{1,0:T(1,128)S(1)} collective-permute-done((s32[1,128]{1,0:T(1,128)S(1)}, s32[1,128]{1,0:T(1,128)S(1)}, u32[]{:S(2)}, u32[]{:S(2)}) %collective-permute-start.2) | collective-permute-done | bytes 544 | tf_op jit(solution)/shard_map/group_exchange/ppermute | solution.py:316
  17.0 0.5 slot_matrix.1
  17.5 0.7 convolution_convert_fusion.1
  18.2 1.2 reshape.29
  19.4 12.1 %all-to-all-start = ((bf16[64,5,2,640]{3,2,1,0:T(2,128)(2,1)}), bf16[64,5,2,640]{3,2,1,0:T(2,128)(2,1)S(1)}, u32[]{:S(2)}, u32[]{:S(2)}) async-start(bf16[64,5,2,640]{3,2,1,0:T(2,128)(2,1)} %reshape.29), calls=%async_computation | async-start | bytes 1638400 | tf_op jit(solution)/shard_map/send_tokens/all_to_all | solution.py:342
  31.6 0.1 copy.7.refs_4_
  31.7 1.4 split_columns.3
  33.1 1.9 %collective-permute-start.12 = (bf16[128,1024]{1,0:T(8,128)(2,1)S(1)}, bf16[128,1024]{1,0:T(8,128)(2,1)S(1)}, u32[]{:S(2)}, u32[]{:S(2)}) collective-permute-start(bf16[128,1024]{1,0:T(8,128)(2,1)S(1)} %get-tuple-element.44), channel_id=1, source_target_pairs={{0,2},{1,3},{2,0},{3,1},{4,6},{5,7},{6,4},{7,5},{8,10},{9,11},{10,... | collective-permute-start | bytes 786440 | tf_op jit(solution)/shard_map/group_exchange/ppermute | solution.py:316
  35.0 1.2 collective-permute-start.13
  36.2 0.9 collective-permute-start.14
  37.1 6.8 %collective-permute-done.12 = bf16[128,1024]{1,0:T(8,128)(2,1)S(1)} collective-permute-done((bf16[128,1024]{1,0:T(8,128)(2,1)S(1)}, bf16[128,1024]{1,0:T(8,128)(2,1)S(1)}, u32[]{:S(2)}, u32[]{:S(2)}) %collective-permute-start.12) | collective-permute-done | bytes 262176 | tf_op jit(solution)/shard_map/group_exchange/ppermute | solution.py:316
  43.9 3.7 %collective-permute-done.13 = bf16[128,1024]{1,0:T(8,128)(2,1)S(1)} collective-permute-done((bf16[128,1024]{1,0:T(8,128)(2,1)S(1)}, bf16[128,1024]{1,0:T(8,128)(2,1)S(1)}, u32[]{:S(2)}, u32[]{:S(2)}) %collective-permute-start.13) | collective-permute-done | bytes 262176 | tf_op jit(solution)/shard_map/group_exchange/ppermute | solution.py:316
  47.6 1.1 collective-permute-done.14
  48.7 0.9 convolution_convert_fusion
  49.5 1.4 reshape.32
  51.0 4.4 %all-to-all-done = bf16[64,5,2,640]{3,2,1,0:T(2,128)(2,1)S(1)} async-done(((bf16[64,5,2,640]{3,2,1,0:T(2,128)(2,1)}), bf16[64,5,2,640]{3,2,1,0:T(2,128)(2,1)S(1)}, u32[]{:S(2)}, u32[]{:S(2)}) %all-to-all-start) | async-done | bytes 819232 | tf_op jit(solution)/shard_map/send_tokens/all_to_all | solution.py:342
  55.4 6.0 %all-to-all-start.1 = ((bf16[64,80,128]{2,1,0:T(8,128)(2,1)}), bf16[64,80,128]{2,1,0:T(8,128)(2,1)}, u32[]{:S(2)}, u32[]{:S(2)}) async-start(bf16[64,80,128]{2,1,0:T(8,128)(2,1)} %reshape.32), calls=%async_computation.1 | async-start | bytes 2621440 | tf_op jit(solution)/shard_map/send_hidden/all_to_all | solution.py:342
  61.4 0.6 fusion.16
  62.0 0.2 reshape.30.refs_0_
  62.2 0.2 reshape.31.refs_1_
  62.3 0.6 collective-permute-start.6
  63.0 2.9 %collective-permute-start.7 = (bf16[320,640]{1,0:T(8,128)(2,1)S(1)}, bf16[320,640]{1,0:T(8,128)(2,1)S(1)}, u32[]{:S(2)}, u32[]{:S(2)}) collective-permute-start(bf16[320,640]{1,0:T(8,128)(2,1)S(1)} %reshape.31.refs_1_), channel_id=1, source_target_pairs={{0,3},{1,0},{2,1},{3,2},{4,7},{5,4},{6,5},{7,6},{8,11},{9,8},{10,9... | collective-permute-start | bytes 1228808 | tf_op jit(solution)/shard_map/gather_width/ppermute | solution.py:316
  65.8 0.4 collective-permute-start.10
  66.2 1.7 collective-permute-start.11
  67.9 5.9 %up_sums.2 = (f32[640,1024]{1,0:T(8,128)}, f32[640,1024]{1,0:T(8,128)}) custom-call(s32[1]{0:T(128)} %bitcast.x_ref, bf16[320,640]{1,0:T(8,128)(2,1)S(1)} %reshape.30.refs_0_, bf16[320,640]{1,0:T(8,128)(2,1)S(1)} %reshape.31.refs_1_, bf16[2560,1024]{1,0:T(8,128)(2,1)} %bitcast.14, bf16[2560,1024]{1,0:T(8,128)(2,1)} %bitcast.21), custom_call_target="tpu_custom_call" | custom-call | flops 1677721600 | bytes 13107200 | tf_op jit(solution)/shard_map/gather_width/up_sums/pallas_call | solution.py:155
  73.7 2.4 %collective-permute-done.6.refs_1_ = bf16[320,640]{1,0:T(8,128)(2,1)S(1)} collective-permute-done((bf16[320,640]{1,0:T(8,128)(2,1)S(1)}, bf16[320,640]{1,0:T(8,128)(2,1)S(1)}, u32[]{:S(2)}, u32[]{:S(2)}) %collective-permute-start.6) | collective-permute-done | bytes 409632 | tf_op jit(solution)/shard_map/gather_width/ppermute | solution.py:319
  76.1 0.6 collective-permute-start.8
  76.7 2.7 %collective-permute-start.9 = (bf16[320,640]{1,0:T(8,128)(2,1)S(1)}, bf16[320,640]{1,0:T(8,128)(2,1)}, u32[]{:S(2)}, u32[]{:S(2)}) collective-permute-start(bf16[320,640]{1,0:T(8,128)(2,1)S(1)} %collective-permute-done.7.refs_2_), channel_id=1, source_target_pairs={{0,3},{1,0},{2,1},{3,2},{4,7},{5,4},{6,5},{7,6},{8,11},{9,8},{10,9... | collective-permute-start | bytes 1228808 | tf_op jit(solution)/shard_map/gather_width/ppermute | solution.py:316
  79.4 5.1 %collective-permute-done.10.refs_0_ = bf16[320,640]{1,0:T(8,128)(2,1)S(1)} collective-permute-done((bf16[320,640]{1,0:T(8,128)(2,1)S(1)}, bf16[320,640]{1,0:T(8,128)(2,1)S(1)}, u32[]{:S(2)}, u32[]{:S(2)}) %collective-permute-start.10) | collective-permute-done | bytes 409632 | tf_op jit(solution)/shard_map/gather_width/ppermute | solution.py:316
  84.5 0.4 collective-permute-done.11.refs_3_
  84.9 8.9 %up_sums.3 = (f32[640,1024]{1,0:T(8,128)}, f32[640,1024]{1,0:T(8,128)}) custom-call(s32[1]{0:T(128)} %bitcast.x_ref, bf16[320,640]{1,0:T(8,128)(2,1)S(1)} %collective-permute-done.10.refs_0_, bf16[320,640]{1,0:T(8,128)(2,1)S(1)} %collective-permute-done.6.refs_1_, bf16[320,640]{1,0:T(8,128)(2,1)S(1)} %collective-permute-done.7.refs_2_, ...), custom_call_target="tpu_custom_call" | custom-call | flops 3355443200 | bytes 15728640 | tf_op jit(solution)/shard_map/pre_activations/up_sums/pallas_call | solution.py:155
  93.7 2.0 %all-to-all-done.1 = bf16[64,80,128]{2,1,0:T(8,128)(2,1)} async-done(((bf16[64,80,128]{2,1,0:T(8,128)(2,1)}), bf16[64,80,128]{2,1,0:T(8,128)(2,1)}, u32[]{:S(2)}, u32[]{:S(2)}) %all-to-all-start.1) | async-done | bytes 1310752 | tf_op jit(solution)/shard_map/send_hidden/all_to_all | solution.py:342
  95.8 2.4 %reshape.33.h = bf16[640,1024]{1,0:T(8,128)(2,1)S(1)} reshape(bf16[64,80,128]{2,1,0:T(8,128)(2,1)} %all-to-all-done.1) | data formatting | bytes 2621440 | tf_op jit(solution)/shard_map/send_hidden/reshape | solution.py:351
  98.2 8.2 %middle.1 = (bf16[640,1024]{1,0:T(8,128)(2,1)S(1)}, bf16[640,1024]{1,0:T(8,128)(2,1)S(1)}, bf16[320,640]{1,0:T(8,128)(2,1)S(1)}, bf16[320,640]{1,0:T(8,128)(2,1)S(1)}) custom-call(s32[1]{0:T(128)} %bitcast.x_ref, bf16[320,640]{1,0:T(8,128)(2,1)S(1)} %collective-permute-done.8.top, bf16[320,640]{1,0:T(8,128)(2,1)} %collective-permute-done.9.bottom, ...), custom_call_target="tpu_custom_call" | custom-call | flops 3355443200 | bytes 11796480 | tf_op jit(solution)/shard_map/input_partials/middle/pallas_call | solution.py:223
  106.3 1.6 collective-permute-start.19
  108.0 0.5 collective-permute-start.15
  108.4 4.2 %down_halves.5 = (bf16[320,640]{1,0:T(8,128)(2,1)S(1)}, bf16[320,640]{1,0:T(8,128)(2,1)S(1)}) custom-call(s32[1]{0:T(128)} %bitcast.x_ref, bf16[640,1024]{1,0:T(8,128)(2,1)S(1)} %get-tuple-element.47.gg, bf16[640,1024]{1,0:T(8,128)(2,1)S(1)} %get-tuple-element.48.gu, bf16[2560,1024]{1,0:T(8,128)(2,1)} %bitcast.18, bf16[2560,1024]{1,0:T(8,128)(2,1)} %bitcast.25), custom_call_target="tpu_custom_call" | custom-call | flops 419430400 | bytes 7864320 | tf_op jit(solution)/shard_map/input_partials/down_halves/pallas_call | solution.py:266
  112.7 3.1 %collective-permute-start.17 = (bf16[320,640]{1,0:T(8,128)(2,1)S(1)}, bf16[320,640]{1,0:T(8,128)(2,1)S(1)}, u32[]{:S(2)}, u32[]{:S(2)}) collective-permute-start(bf16[320,640]{1,0:T(8,128)(2,1)S(1)} %get-tuple-element.52), channel_id=1, source_target_pairs={{0,3},{1,0},{2,1},{3,2},{4,7},{5,4},{6,5},{7,6},{8,11},{9,8},{10,9... | collective-permute-start | bytes 1228808 | tf_op jit(solution)/shard_map/sum_quarters/ppermute | solution.py:316
  115.7 4.2 %down_halves.4 = (f32[320,640]{1,0:T(8,128)S(1)}, f32[320,640]{1,0:T(8,128)S(1)}) custom-call(s32[1]{0:T(128)} %bitcast.x_ref, bf16[640,1024]{1,0:T(8,128)(2,1)S(1)} %get-tuple-element.47.gg, bf16[640,1024]{1,0:T(8,128)(2,1)S(1)} %get-tuple-element.48.gu, bf16[2560,1024]{1,0:T(8,128)(2,1)} %bitcast.19, bf16[2560,1024]{1,0:T(8,128)(2,1)} %bitcast.26), custom_call_target="tpu_custom_call" | custom-call | flops 419430400 | bytes 7864320 | tf_op jit(solution)/shard_map/input_partials/down_halves/pallas_call | solution.py:266
  120.0 0.1 add_convert_fusion
  120.1 3.3 %collective-permute-start.20 = (bf16[320,640]{1,0:T(8,128)(2,1)S(1)}, bf16[320,640]{1,0:T(8,128)(2,1)S(1)}, u32[]{:S(2)}, u32[]{:S(2)}) collective-permute-start(bf16[320,640]{1,0:T(8,128)(2,1)S(1)} %add_convert_fusion), channel_id=1, source_target_pairs={{0,3},{1,0},{2,1},{3,2},{4,7},{5,4},{6,5},{7,6},{8,11},{9,8},{10,9... | collective-permute-start | bytes 1228808 | tf_op jit(solution)/shard_map/sum_quarters/ppermute | solution.py:316
  123.4 0.1 add_convert_fusion.1
  123.6 4.2 %down_halves.3 = (f32[320,640]{1,0:T(8,128)S(1)}, f32[320,640]{1,0:T(8,128)S(1)}) custom-call(s32[1]{0:T(128)} %bitcast.x_ref, bf16[640,1024]{1,0:T(8,128)(2,1)S(1)} %get-tuple-element.47.gg, bf16[640,1024]{1,0:T(8,128)(2,1)S(1)} %get-tuple-element.48.gu, bf16[2560,1024]{1,0:T(8,128)(2,1)} %bitcast.20, bf16[2560,1024]{1,0:T(8,128)(2,1)} %bitcast.27), custom_call_target="tpu_custom_call" | custom-call | flops 419430400 | bytes 7864320 | tf_op jit(solution)/shard_map/input_partials/down_halves/pallas_call | solution.py:266
  127.8 1.5 collective-permute-done.18.refs_4_
  129.4 4.7 %collective-permute-done.20.refs_5_ = bf16[320,640]{1,0:T(8,128)(2,1)S(1)} collective-permute-done((bf16[320,640]{1,0:T(8,128)(2,1)S(1)}, bf16[320,640]{1,0:T(8,128)(2,1)S(1)}, u32[]{:S(2)}, u32[]{:S(2)}) %collective-permute-start.20) | collective-permute-done | bytes 409632 | tf_op jit(solution)/shard_map/sum_quarters/ppermute | solution.py:316
  134.0 2.5 %collective-permute-done.16.refs_1_ = bf16[320,640]{1,0:T(8,128)(2,1)S(1)} collective-permute-done((bf16[320,640]{1,0:T(8,128)(2,1)S(1)}, bf16[320,640]{1,0:T(8,128)(2,1)S(1)}, u32[]{:S(2)}, u32[]{:S(2)}) %collective-permute-start.16) | collective-permute-done | bytes 409632 | tf_op jit(solution)/shard_map/sum_quarters/ppermute | solution.py:319
  136.5 0.3 sum_halves.1
  136.8 0.3 reshape.34
  137.1 33.0 %all_to_all.15 = bf16[64,5,2,640]{3,2,1,0:T(2,128)(2,1)S(1)} all-to-all(bf16[64,5,2,640]{3,2,1,0:T(2,128)(2,1)S(1)} %reshape.34), channel_id=1, replica_groups=mesh['expert'=64,'etp'=4] {'expert'}, dimensions={0} | all-to-all | bytes 1638400 | tf_op jit(solution)/shard_map/return_tokens/all_to_all | solution.py:342
  170.1 0.3 reshape.35
  170.4 0.8 convolution_convert_fusion.2
  171.4 1.1 collective-permute-start.22
  172.5 2.2 %collective-permute-start.23 = (bf16[128,640]{1,0:T(8,128)(2,1)S(1)}, bf16[128,640]{1,0:T(8,128)(2,1)S(1)}, u32[]{:S(2)}, u32[]{:S(2)}) collective-permute-start(bf16[128,640]{1,0:T(8,128)(2,1)S(1)} %get-tuple-element.59), channel_id=1, source_target_pairs={{0,3},{1,0},{2,1},{3,2},{4,7},{5,4},{6,5},{7,6},{8,11},{9,8},{10,9... | collective-permute-start | bytes 491528 | tf_op jit(solution)/shard_map/return_tokens/ppermute | solution.py:319
  174.7 5.3 %collective-permute-done.21.b1 = bf16[128,640]{1,0:T(8,128)(2,1)S(1)} collective-permute-done((bf16[128,640]{1,0:T(8,128)(2,1)S(1)}, bf16[128,640]{1,0:T(8,128)(2,1)S(1)}, u32[]{:S(2)}, u32[]{:S(2)}) %collective-permute-start.21) | collective-permute-done | bytes 163872 | tf_op jit(solution)/shard_map/return_tokens/ppermute | solution.py:319
  179.9 1.5 collective-permute-done.22.b2
  181.5 0.9 join_columns.1
  (20 shorter events, 0.3 us)
Async XLA Ops:
  0.0 6.4 %copy-start = (s32[128,1]{0,1:T(1,128)S(1)}, s32[128,1]{0,1:T(1,128)}, u32[]{:S(2)}) copy-start(s32[128,1]{0,1:T(1,128)} %param.8) | copy-start | bytes 1540
  1.2 16.3 %collective-permute-start.3 = (bf16[128,640]{1,0:T(8,128)(2,1)S(1)}, bf16[128,640]{1,0:T(8,128)(2,1)S(1)}, u32[]{:S(2)}, u32[]{:S(2)}) collective-permute-start(bf16[128,640]{1,0:T(8,128)(2,1)S(1)} %get-tuple-element.32), channel_id=1, source_target_pairs={{0,2},{1,3},{2,0},{3,1},{4,6},{5,7},{6,4},{7,5},{8,10},{9,11},{10,... | collective-permute-start | bytes 491528 | tf_op jit(solution)/shard_map/group_exchange/ppermute | solution.py:316
  4.3 13.2 %collective-permute-start.4 = (bf16[128,640]{1,0:T(8,128)(2,1)S(1)}, bf16[128,640]{1,0:T(8,128)(2,1)S(1)}, u32[]{:S(2)}, u32[]{:S(2)}) collective-permute-start(bf16[128,640]{1,0:T(8,128)(2,1)S(1)} %get-tuple-element.33), channel_id=1, source_target_pairs={{0,3},{1,0},{2,1},{3,2},{4,7},{5,4},{6,5},{7,6},{8,11},{9,8},{10,9... | collective-permute-start | bytes 491528 | tf_op jit(solution)/shard_map/group_exchange/ppermute | solution.py:316
  5.5 12.0 %collective-permute-start.5 = (bf16[128,640]{1,0:T(8,128)(2,1)S(1)}, bf16[128,640]{1,0:T(8,128)(2,1)S(1)}, u32[]{:S(2)}, u32[]{:S(2)}) collective-permute-start(bf16[128,640]{1,0:T(8,128)(2,1)S(1)} %get-tuple-element.34), channel_id=1, source_target_pairs={{0,1},{1,2},{2,3},{3,0},{4,5},{5,6},{6,7},{7,4},{8,9},{9,10},{10,1... | collective-permute-start | bytes 491528 | tf_op jit(solution)/shard_map/group_exchange/ppermute | solution.py:316
  6.4 5.9 %collective-permute-start = (s32[1,128]{1,0:T(1,128)S(1)}, s32[1,128]{1,0:T(1,128)S(1)}, u32[]{:S(2)}, u32[]{:S(2)}) collective-permute-start(s32[1,128]{1,0:T(1,128)S(1)} %bitcast.10), channel_id=1, source_target_pairs={{0,2},{1,3},{2,0},{3,1},{4,6},{5,7},{6,4},{7,5},{8,10},{9,11},{10,... | collective-permute-start | bytes 1544 | tf_op jit(solution)/shard_map/group_exchange/ppermute | solution.py:316
  7.0 6.8 %collective-permute-start.1 = (s32[1,128]{1,0:T(1,128)S(1)}, s32[1,128]{1,0:T(1,128)S(1)}, u32[]{:S(2)}, u32[]{:S(2)}) collective-permute-start(s32[1,128]{1,0:T(1,128)S(1)} %bitcast.11), channel_id=1, source_target_pairs={{0,3},{1,0},{2,1},{3,2},{4,7},{5,4},{6,5},{7,6},{8,11},{9,8},{10,9... | collective-permute-start | bytes 1544 | tf_op jit(solution)/shard_map/group_exchange/ppermute | solution.py:316
  12.3 4.8 %collective-permute-start.2 = (s32[1,128]{1,0:T(1,128)S(1)}, s32[1,128]{1,0:T(1,128)S(1)}, u32[]{:S(2)}, u32[]{:S(2)}) collective-permute-start(s32[1,128]{1,0:T(1,128)S(1)} %bitcast.12), channel_id=1, source_target_pairs={{0,1},{1,2},{2,3},{3,0},{4,5},{5,6},{6,7},{7,4},{8,9},{9,10},{10,1... | collective-permute-start | bytes 1544 | tf_op jit(solution)/shard_map/group_exchange/ppermute | solution.py:316
  18.2 13.3 %copy-start.1 = (s32[128]{0:T(128)S(1)}, s32[128]{0:T(128)}, u32[]{:S(2)}) copy-start(s32[128]{0:T(128)} %param.9) | copy-start | bytes 1540
  19.4 36.0 %all-to-all-start = ((bf16[64,5,2,640]{3,2,1,0:T(2,128)(2,1)}), bf16[64,5,2,640]{3,2,1,0:T(2,128)(2,1)S(1)}, u32[]{:S(2)}, u32[]{:S(2)}) async-start(bf16[64,5,2,640]{3,2,1,0:T(2,128)(2,1)} %reshape.29), calls=%async_computation | async-start | bytes 1638400 | tf_op jit(solution)/shard_map/send_tokens/all_to_all | solution.py:342
  33.1 10.8 %collective-permute-start.12 = (bf16[128,1024]{1,0:T(8,128)(2,1)S(1)}, bf16[128,1024]{1,0:T(8,128)(2,1)S(1)}, u32[]{:S(2)}, u32[]{:S(2)}) collective-permute-start(bf16[128,1024]{1,0:T(8,128)(2,1)S(1)} %get-tuple-element.44), channel_id=1, source_target_pairs={{0,2},{1,3},{2,0},{3,1},{4,6},{5,7},{6,4},{7,5},{8,10},{9,11},{10,... | collective-permute-start | bytes 786440 | tf_op jit(solution)/shard_map/group_exchange/ppermute | solution.py:316
  35.0 12.6 %collective-permute-start.13 = (bf16[128,1024]{1,0:T(8,128)(2,1)S(1)}, bf16[128,1024]{1,0:T(8,128)(2,1)S(1)}, u32[]{:S(2)}, u32[]{:S(2)}) collective-permute-start(bf16[128,1024]{1,0:T(8,128)(2,1)S(1)} %get-tuple-element.45), channel_id=1, source_target_pairs={{0,3},{1,0},{2,1},{3,2},{4,7},{5,4},{6,5},{7,6},{8,11},{9,8},{10,9... | collective-permute-start | bytes 786440 | tf_op jit(solution)/shard_map/group_exchange/ppermute | solution.py:316
  36.2 12.5 %collective-permute-start.14 = (bf16[128,1024]{1,0:T(8,128)(2,1)S(1)}, bf16[128,1024]{1,0:T(8,128)(2,1)S(1)}, u32[]{:S(2)}, u32[]{:S(2)}) collective-permute-start(bf16[128,1024]{1,0:T(8,128)(2,1)S(1)} %get-tuple-element.46), channel_id=1, source_target_pairs={{0,1},{1,2},{2,3},{3,0},{4,5},{5,6},{6,7},{7,4},{8,9},{9,10},{10,1... | collective-permute-start | bytes 786440 | tf_op jit(solution)/shard_map/group_exchange/ppermute | solution.py:316
  55.4 40.4 %all-to-all-start.1 = ((bf16[64,80,128]{2,1,0:T(8,128)(2,1)}), bf16[64,80,128]{2,1,0:T(8,128)(2,1)}, u32[]{:S(2)}, u32[]{:S(2)}) async-start(bf16[64,80,128]{2,1,0:T(8,128)(2,1)} %reshape.32), calls=%async_computation.1 | async-start | bytes 2621440 | tf_op jit(solution)/shard_map/send_hidden/all_to_all | solution.py:342
  62.3 13.8 %collective-permute-start.6 = (bf16[320,640]{1,0:T(8,128)(2,1)S(1)}, bf16[320,640]{1,0:T(8,128)(2,1)S(1)}, u32[]{:S(2)}, u32[]{:S(2)}) collective-permute-start(bf16[320,640]{1,0:T(8,128)(2,1)S(1)} %reshape.30.refs_0_), channel_id=1, source_target_pairs={{0,1},{1,2},{2,3},{3,0},{4,5},{5,6},{6,7},{7,4},{8,9},{9,10},{10,1... | collective-permute-start | bytes 1228808 | tf_op jit(solution)/shard_map/gather_width/ppermute | solution.py:319
  63.0 13.1 %collective-permute-start.7 = (bf16[320,640]{1,0:T(8,128)(2,1)S(1)}, bf16[320,640]{1,0:T(8,128)(2,1)S(1)}, u32[]{:S(2)}, u32[]{:S(2)}) collective-permute-start(bf16[320,640]{1,0:T(8,128)(2,1)S(1)} %reshape.31.refs_1_), channel_id=1, source_target_pairs={{0,3},{1,0},{2,1},{3,2},{4,7},{5,4},{6,5},{7,6},{8,11},{9,8},{10,9... | collective-permute-start | bytes 1228808 | tf_op jit(solution)/shard_map/gather_width/ppermute | solution.py:316
  65.8 18.6 %collective-permute-start.10 = (bf16[320,640]{1,0:T(8,128)(2,1)S(1)}, bf16[320,640]{1,0:T(8,128)(2,1)S(1)}, u32[]{:S(2)}, u32[]{:S(2)}) collective-permute-start(bf16[320,640]{1,0:T(8,128)(2,1)S(1)} %reshape.30.refs_0_), channel_id=1, source_target_pairs={{0,3},{1,0},{2,1},{3,2},{4,7},{5,4},{6,5},{7,6},{8,11},{9,8},{10,9... | collective-permute-start | bytes 1228808 | tf_op jit(solution)/shard_map/gather_width/ppermute | solution.py:316
  66.2 18.7 %collective-permute-start.11 = (bf16[320,640]{1,0:T(8,128)(2,1)S(1)}, bf16[320,640]{1,0:T(8,128)(2,1)S(1)}, u32[]{:S(2)}, u32[]{:S(2)}) collective-permute-start(bf16[320,640]{1,0:T(8,128)(2,1)S(1)} %reshape.31.refs_1_), channel_id=1, source_target_pairs={{0,1},{1,2},{2,3},{3,0},{4,5},{5,6},{6,7},{7,4},{8,9},{9,10},{10,1... | collective-permute-start | bytes 1228808 | tf_op jit(solution)/shard_map/gather_width/ppermute | solution.py:319
  76.1 22.0 %collective-permute-start.8 = (bf16[320,640]{1,0:T(8,128)(2,1)S(1)}, bf16[320,640]{1,0:T(8,128)(2,1)S(1)}, u32[]{:S(2)}, u32[]{:S(2)}) collective-permute-start(bf16[320,640]{1,0:T(8,128)(2,1)S(1)} %collective-permute-done.6.refs_1_), channel_id=1, source_target_pairs={{0,1},{1,2},{2,3},{3,0},{4,5},{5,6},{6,7},{7,4},{8,9},{9,10},{10,1... | collective-permute-start | bytes 1228808 | tf_op jit(solution)/shard_map/gather_width/ppermute | solution.py:319
  76.7 21.4 %collective-permute-start.9 = (bf16[320,640]{1,0:T(8,128)(2,1)S(1)}, bf16[320,640]{1,0:T(8,128)(2,1)}, u32[]{:S(2)}, u32[]{:S(2)}) collective-permute-start(bf16[320,640]{1,0:T(8,128)(2,1)S(1)} %collective-permute-done.7.refs_2_), channel_id=1, source_target_pairs={{0,3},{1,0},{2,1},{3,2},{4,7},{5,4},{6,5},{7,6},{8,11},{9,8},{10,9... | collective-permute-start | bytes 1228808 | tf_op jit(solution)/shard_map/gather_width/ppermute | solution.py:316
  106.3 13.6 %collective-permute-start.19 = (bf16[320,640]{1,0:T(8,128)(2,1)S(1)}, bf16[320,640]{1,0:T(8,128)(2,1)S(1)}, u32[]{:S(2)}, u32[]{:S(2)}) collective-permute-start(bf16[320,640]{1,0:T(8,128)(2,1)S(1)} %get-tuple-element.56), channel_id=1, source_target_pairs={{0,3},{1,0},{2,1},{3,2},{4,7},{5,4},{6,5},{7,6},{8,11},{9,8},{10,9... | collective-permute-start | bytes 1228808 | tf_op jit(solution)/shard_map/sum_quarters/ppermute | solution.py:316
  108.0 15.4 %collective-permute-start.15 = (bf16[320,640]{1,0:T(8,128)(2,1)S(1)}, bf16[320,640]{1,0:T(8,128)(2,1)S(1)}, u32[]{:S(2)}, u32[]{:S(2)}) collective-permute-start(bf16[320,640]{1,0:T(8,128)(2,1)S(1)} %get-tuple-element.51), channel_id=1, source_target_pairs={{0,1},{1,2},{2,3},{3,0},{4,5},{5,6},{6,7},{7,4},{8,9},{9,10},{10,1... | collective-permute-start | bytes 1228808 | tf_op jit(solution)/shard_map/sum_quarters/ppermute | solution.py:319
  112.7 15.2 %collective-permute-start.17 = (bf16[320,640]{1,0:T(8,128)(2,1)S(1)}, bf16[320,640]{1,0:T(8,128)(2,1)S(1)}, u32[]{:S(2)}, u32[]{:S(2)}) collective-permute-start(bf16[320,640]{1,0:T(8,128)(2,1)S(1)} %get-tuple-element.52), channel_id=1, source_target_pairs={{0,3},{1,0},{2,1},{3,2},{4,7},{5,4},{6,5},{7,6},{8,11},{9,8},{10,9... | collective-permute-start | bytes 1228808 | tf_op jit(solution)/shard_map/sum_quarters/ppermute | solution.py:316
  115.7 13.6 %collective-permute-start.18 = (bf16[320,640]{1,0:T(8,128)(2,1)S(1)}, bf16[320,640]{1,0:T(8,128)(2,1)S(1)}, u32[]{:S(2)}, u32[]{:S(2)}) collective-permute-start(bf16[320,640]{1,0:T(8,128)(2,1)S(1)} %get-tuple-element.54), channel_id=1, source_target_pairs={{0,1},{1,2},{2,3},{3,0},{4,5},{5,6},{6,7},{7,4},{8,9},{9,10},{10,1... | collective-permute-start | bytes 1228808 | tf_op jit(solution)/shard_map/sum_quarters/ppermute | solution.py:319
  120.1 13.9 %collective-permute-start.20 = (bf16[320,640]{1,0:T(8,128)(2,1)S(1)}, bf16[320,640]{1,0:T(8,128)(2,1)S(1)}, u32[]{:S(2)}, u32[]{:S(2)}) collective-permute-start(bf16[320,640]{1,0:T(8,128)(2,1)S(1)} %add_convert_fusion), channel_id=1, source_target_pairs={{0,3},{1,0},{2,1},{3,2},{4,7},{5,4},{6,5},{7,6},{8,11},{9,8},{10,9... | collective-permute-start | bytes 1228808 | tf_op jit(solution)/shard_map/sum_quarters/ppermute | solution.py:316
  123.5 13.0 %collective-permute-start.16 = (bf16[320,640]{1,0:T(8,128)(2,1)S(1)}, bf16[320,640]{1,0:T(8,128)(2,1)S(1)}, u32[]{:S(2)}, u32[]{:S(2)}) collective-permute-start(bf16[320,640]{1,0:T(8,128)(2,1)S(1)} %add_convert_fusion.1), channel_id=1, source_target_pairs={{0,1},{1,2},{2,3},{3,0},{4,5},{5,6},{6,7},{7,4},{8,9},{9,10},{10,1... | collective-permute-start | bytes 1228808 | tf_op jit(solution)/shard_map/sum_quarters/ppermute | solution.py:319
  171.3 8.7 %collective-permute-start.21 = (bf16[128,640]{1,0:T(8,128)(2,1)S(1)}, bf16[128,640]{1,0:T(8,128)(2,1)S(1)}, u32[]{:S(2)}, u32[]{:S(2)}) collective-permute-start(bf16[128,640]{1,0:T(8,128)(2,1)S(1)} %get-tuple-element.61), channel_id=1, source_target_pairs={{0,2},{1,3},{2,0},{3,1},{4,6},{5,7},{6,4},{7,5},{8,10},{9,11},{10,... | collective-permute-start | bytes 491528 | tf_op jit(solution)/shard_map/return_tokens/ppermute | solution.py:319
  171.4 10.1 %collective-permute-start.22 = (bf16[128,640]{1,0:T(8,128)(2,1)S(1)}, bf16[128,640]{1,0:T(8,128)(2,1)S(1)}, u32[]{:S(2)}, u32[]{:S(2)}) collective-permute-start(bf16[128,640]{1,0:T(8,128)(2,1)S(1)} %get-tuple-element.60), channel_id=1, source_target_pairs={{0,1},{1,2},{2,3},{3,0},{4,5},{5,6},{6,7},{7,4},{8,9},{9,10},{10,1... | collective-permute-start | bytes 491528 | tf_op jit(solution)/shard_map/return_tokens/ppermute | solution.py:319
  172.5 9.0 %collective-permute-start.23 = (bf16[128,640]{1,0:T(8,128)(2,1)S(1)}, bf16[128,640]{1,0:T(8,128)(2,1)S(1)}, u32[]{:S(2)}, u32[]{:S(2)}) collective-permute-start(bf16[128,640]{1,0:T(8,128)(2,1)S(1)} %get-tuple-element.59), channel_id=1, source_target_pairs={{0,3},{1,0},{2,1},{3,2},{4,7},{5,4},{6,5},{7,6},{8,11},{9,8},{10,9... | collective-permute-start | bytes 491528 | tf_op jit(solution)/shard_map/return_tokens/ppermute | solution.py:319

commit v4 on v3

--- a/solution.py
+++ b/solution.py
@@ -125,57 +125,50 @@
 
 
 HIDDEN_TILE = 512
-
-
-def up_sums(uppers, lowers, offsets, gate_weight, up_weight, x, so_far=()):
-    half, depth = uppers[0].shape
+SCHEDULE_WEIGHT = 6
+
+
+def up_sums(blocks, offsets, gate_weight, up_weight, x, so_far=()):
+    rows, depth = blocks[0].shape
     hidden = gate_weight.shape[1]
-    rows, count = 2 * half, len(offsets)
-    tile = 256
+    count = len(offsets)
 
     def kernel(x_ref, *refs):
-        gate, up = refs[-2:]
-        starts = refs[4 * count : -2]
-        for k in range(2):
-            part = slice(k * half, (k + 1) * half)
-            blocks = refs[k * count : (k + 1) * count]
-            for n, out in enumerate((gate, up)):
-                weights = refs[(2 + n) * count : (3 + n) * count]
-                total = jnp.dot(blocks[0][...], weights[0][...], preferred_element_type=F32)
-                for block, w in zip(blocks[1:], weights[1:]):
-                    total += jnp.dot(block[...], w[...], preferred_element_type=F32)
-                if starts:
-                    total += starts[n][part, :]
-                out[part, :] = total
+        starts = refs[3 * count : -2]
+        for n, out in enumerate(refs[-2:]):
+            weights = refs[(1 + n) * count : (2 + n) * count]
+            total = jnp.dot(refs[0][...], weights[0][...], preferred_element_type=F32)
+            for block, w in zip(refs[1:count], weights[1:]):
+                total += jnp.dot(block[...], w[...], preferred_element_type=F32)
+            if starts:
+                total += starts[n][...]
+            out[...] = total
 
     def weight(offset):
-        return pl.BlockSpec((depth, tile), lambda j, x_ref: (quarter_at(x_ref, offset), j))
-
-    tiled = pl.BlockSpec((rows, tile), lambda j, x_ref: (0, j))
-    return pl.pallas_call(
-        kernel,
-        grid_spec=pltpu.PrefetchScalarGridSpec(
-            num_scalar_prefetch=1,
-            grid=(hidden // tile,),
-            in_specs=[pl.BlockSpec((half, depth), lambda j, x_ref: (0, 0))] * (2 * count)
+        return pl.BlockSpec((depth, HIDDEN_TILE), lambda j, x_ref: (quarter_at(x_ref, offset), j))
+
+    tiled = pl.BlockSpec((rows, HIDDEN_TILE), lambda j, x_ref: (0, j))
+    if so_far:
+        out_shape = [pltpu.HBM((rows, hidden), F32)] * 2
+    else:
+        out_shape = [jax.ShapeDtypeStruct((rows, hidden), F32)] * 2
+    return pl.pallas_call(
+        kernel,
+        grid_spec=pltpu.PrefetchScalarGridSpec(
+            num_scalar_prefetch=1,
+            grid=(hidden // HIDDEN_TILE,),
+            in_specs=[pl.BlockSpec((rows, depth), lambda j, x_ref: (0, 0))] * count
             + [weight(offset) for offset in offsets] * 2
             + [tiled] * len(so_far),
             out_specs=[tiled, tiled],
         ),
-        out_shape=[pltpu.HBM((rows, hidden), F32)] * 2,
+        out_shape=out_shape,
         compiler_params=params(),
         cost_estimate=cost(
-            4 * count * rows * depth * hidden, 4 * count * depth * hidden + 16 * rows * hidden
+            SCHEDULE_WEIGHT * 4 * count * rows * depth * hidden, 4 * count * depth * hidden + 16 * rows * hidden
         ),
         name="up_sums",
-    )(
-        x,
-        *uppers,
-        *lowers,
-        *([gate_weight] * count),
-        *([up_weight] * count),
-        *(in_hbm(array) for array in so_far),
-    )
+    )(x, *blocks, *([gate_weight] * count), *([up_weight] * count), *so_far)
 
 
 CONTRACT_LAST = (((1,), (1,)), ((), ()))
@@ -186,21 +179,52 @@
     return total + lax.dot_general(gu, wu, CONTRACT_LAST, preferred_element_type=F32)
 
 
-def middle(upper, lower, gate, up, scaled, offset, gate_weight, up_weight, x):
+def up_last(upper, lower, gate, up, offset, gate_weight, up_weight, x):
     half, depth = upper.shape
     rows, hidden = gate.shape
-    steps = hidden // HIDDEN_TILE
-
-    def kernel(x_ref, top, bottom, g_in, u_in, h, wg, wu, gg_out, gu_out, out_top, out_bottom, total):
-        step = pl.program_id(0)
-        for k, (t, out) in enumerate(((top, out_top), (bottom, out_bottom))):
+
+    def kernel(x_ref, top, bottom, g_in, u_in, wg, wu, for_gate, for_up):
+        for k, t in enumerate((top, bottom)):
             part = slice(k * half, (k + 1) * half)
             g = g_in[part, :] + jnp.dot(t[...], wg[...], preferred_element_type=F32)
             u = u_in[part, :] + jnp.dot(t[...], wu[...], preferred_element_type=F32)
             s = 1.0 / (1.0 + jnp.exp(-g))
-            hs = h[part, :].astype(F32) * s
-            gg = (hs * u * (1.0 + g * (1.0 - s))).astype(BF)
-            gu = (hs * g).astype(BF)
+            for_gate[part, :] = u * s * (1.0 + g * (1.0 - s))
+            for_up[part, :] = g * s
+
+    weight = pl.BlockSpec((depth, HIDDEN_TILE), lambda j, x_ref: (quarter_at(x_ref, offset), j))
+    tiled = pl.BlockSpec((rows, HIDDEN_TILE), lambda j, x_ref: (0, j))
+    halves = [pl.BlockSpec((half, depth), lambda j, x_ref: (0, 0))] * 2
+    return pl.pallas_call(
+        kernel,
+        grid_spec=pltpu.PrefetchScalarGridSpec(
+            num_scalar_prefetch=1,
+            grid=(hidden // HIDDEN_TILE,),
+            in_specs=halves + [tiled] * 2 + [weight] * 2,
+            out_specs=[tiled] * 2,
+        ),
+        out_shape=[pltpu.HBM((rows, hidden), F32)] * 2,
+        compiler_params=params(),
+        cost_estimate=cost(
+            4 * rows * depth * hidden, 4 * depth * hidden + 16 * rows * hidden, rows * hidden
+        ),
+        name="up_last",
+    )(x, upper, lower, gate, up, gate_weight, up_weight)
+
+
+def down_first(scaled, for_gate, for_up, offset, gate_weight, up_weight, x):
+    rows, hidden = scaled.shape
+    depth = gate_weight.shape[0] // 4
+    half = rows // 2
+    steps = hidden // HIDDEN_TILE
+
+    def kernel(x_ref, h, a, b, wg, wu, gg_out, gu_out, out_top, out_bottom, total):
+        step = pl.program_id(0)
+        for k, out in enumerate((out_top, out_bottom)):
+            part = slice(k * half, (k + 1) * half)
+            h_part = h[part, :].astype(F32)
+            gg = (h_part * a[part, :]).astype(BF)
+            gu = (h_part * b[part, :]).astype(BF)
             gg_out[part, :] = gg
             gu_out[part, :] = gu
             value = down_dot(gg, gu, wg[...], wu[...])
@@ -225,18 +249,16 @@
         grid_spec=pltpu.PrefetchScalarGridSpec(
             num_scalar_prefetch=1,
             grid=(steps,),
-            in_specs=halves + [tiled] * 3 + [weight] * 2,
+            in_specs=[tiled] * 3 + [weight] * 2,
             out_specs=[tiled] * 2 + halves,
             scratch_shapes=[pltpu.VMEM((rows, depth), F32)],
         ),
         out_shape=[jax.ShapeDtypeStruct((rows, hidden), BF)] * 2
         + [jax.ShapeDtypeStruct((half, depth), BF)] * 2,
         compiler_params=params(),
-        cost_estimate=cost(
-            8 * rows * depth * hidden, 4 * depth * hidden + 14 * rows * hidden, rows * hidden
-        ),
-        name="middle",
-    )(x, upper, lower, in_hbm(gate), in_hbm(up), scaled, gate_weight, up_weight)
+        cost_estimate=cost(4 * rows * depth * hidden, 4 * depth * hidden + 14 * rows * hidden),
+        name="down_first",
+    )(x, scaled, in_hbm(for_gate), in_hbm(for_up), gate_weight, up_weight)
 
 
 def down_halves(grad_gate, grad_up, gate_weight, up_weight, x, pieces, dtype):
@@ -343,27 +365,25 @@
 
     with jax.named_scope("send_tokens"):
         packed_tokens = pick(group_tokens).reshape(experts, capacity // 2, 2, quarter)
-        arrived = to_experts(packed_tokens)
-        top = arrived[: experts // 2].reshape(slots // 2, quarter)
-        bottom = arrived[experts // 2 :].reshape(slots // 2, quarter)
+        packed_hidden = pick(group_hidden).reshape(experts, capacity * hidden // 128, 128)
+        arrived, packed_hidden = lax.optimization_barrier((to_experts(packed_tokens), packed_hidden))
+        own_block = arrived.reshape(slots, quarter)
     with jax.named_scope("send_hidden"):
-        packed_hidden = pick(group_hidden).reshape(experts, capacity * hidden // 128, 128)
         scaled = to_experts(packed_hidden).reshape(slots, hidden)
 
+    half = slots // 2
     with jax.named_scope("gather_width"):
-        own_sums = up_sums((top,), (bottom,), (0,), gate_w, up_w, x)
-        left_top, right_bottom, *own_sums = lax.optimization_barrier(
-            (forward(top, 1), back(bottom, 1), *own_sums)
-        )
-        far_upper, far_lower = forward(left_top, 1), back(right_bottom, 1)
-        left_bottom, right_top = forward(bottom, 1), back(top, 1)
+        own_sums = up_sums((own_block,), (0,), gate_w, up_w, x)
+        left_block, right_block, *own_sums = lax.optimization_barrier(
+            (forward(own_block, 1), back(own_block, 1), *own_sums)
+        )
+        far_upper, far_lower = forward(left_block[:half], 1), back(right_block[half:], 1)
     with jax.named_scope("pre_activations"):
-        gate, up = up_sums(
-            (right_top, left_top), (right_bottom, left_bottom), (1, 3), gate_w, up_w, x, own_sums
-        )
+        gate, up = up_sums((right_block, left_block), (1, 3), gate_w, up_w, x, own_sums)
+        for_gate, for_up = up_last(far_upper, far_lower, in_hbm(gate), in_hbm(up), 2, gate_w, up_w, x)
     with jax.named_scope("input_partials"):
-        grad_gate, grad_up, far_top, far_bottom = middle(
-            far_upper, far_lower, gate, up, scaled, 2, gate_w, up_w, x
+        grad_gate, grad_up, far_top, far_bottom = down_first(
+            scaled, for_gate, for_up, 2, gate_w, up_w, x
         )
         right_bottom, left_top = down_halves(
             grad_gate, grad_up, gate_w, up_w, x, ((1, 1), (3, 0)), BF

time: 184 us -> 182 us (0.989)
  waiting for transfers between devices: 47.3 us -> 51.5 us
  starting transfers between devices: 52.8 us -> 48.7 us
  blocking collectives: 33 us -> 30.2 us
    pallas_call x1 -> x2, Pallas kernels: 8.15 us -> 12.3 us  [the longest x1 6.15 us: down_first(): pl.pallas_call(kernel, grid_spec=pltpu.PrefetchScalarGridSpec(num_scalar_...]
    pallas_call x2, Pallas kernels: 14.7 us -> 11.7 us  [up_sums(): pl.pallas_call(kernel, grid_spec=pltpu.PrefetchScalarGridSpec(num_scalar_...]
    all_to_all x1, blocking collectives: 33 us -> 30.2 us  [to_experts(): lax.all_to_all(array, 'expert', split_axis=0, concat_axis=0, tiled=True)]
    ppermute x9 -> x8, waiting for transfers between devices: 13.6 us -> 16.4 us  [forward(): return lax.ppermute(array, 'etp', [(i, (i + r) % etp) for i in range(etp)])]
    ppermute x9 -> x8, starting transfers between devices: 6.9 us -> 4.82 us  [forward(): return lax.ppermute(array, 'etp', [(i, (i + r) % etp) for i in range(etp)])]
    ppermute x15 -> x14, starting transfers between devices: 27.8 us -> 25.8 us  [back(): return lax.ppermute(array, 'etp', [(i, (i - r) % etp) for i in range(etp)])]
    ppermute x15 -> x14, waiting for transfers between devices: 27.2 us -> 28.1 us  [back(): return lax.ppermute(array, 'etp', [(i, (i - r) % etp) for i in range(etp)])]
  transfers between devices with their start and end apart: 26 -> 24, of which waited for: 15 -> 15; matrix products, arithmetic and copies ran while one was open for 3% -> 2% of each run, Pallas kernels for 16% -> 18%
where the time goes in v4:
time: 182 us; the launch traced here: 181 us
  waiting for transfers between devices  51.5 us (28%)
  starting transfers between devices  48.7 us (27%)
  Pallas kernels  40.7 us (22%)
  blocking collectives  30.2 us (17%)
  local copies, waits for them, and re-layouts  7.16 us (4%)
  matrix products  2.31 us (1%)
    all_to_all x1, blocking collectives, to_experts(): lax.all_to_all(array, 'expert', split_axis=0, concat_axis=0, tiled=True)  30.2 us
    ppermute x14, waiting for transfers between devices, back(): return lax.ppermute(array, 'etp', [(i, (i - r) % etp) for i in range(etp)])  28.1 us
    ppermute x14, starting transfers between devices, back(): return lax.ppermute(array, 'etp', [(i, (i - r) % etp) for i in range(etp)])  25.8 us
    all_to_all x2, starting transfers between devices, to_experts(): lax.all_to_all(array, 'expert', split_axis=0, concat_axis=0, tiled=True)  18.1 us
    ppermute x8, waiting for transfers between devices, forward(): return lax.ppermute(array, 'etp', [(i, (i + r) % etp) for i in range(etp)])  16.4 us
    pallas_call x3, Pallas kernels, down_halves(): pl.pallas_call(kernel, grid_spec=pltpu.PrefetchScalarGridSpec(num_scalar_...  12.5 us
    pallas_call x2, Pallas kernels, up_sums(): pl.pallas_call(kernel, grid_spec=pltpu.PrefetchScalarGridSpec(num_scalar_...  11.7 us
    all_to_all x2, waiting for transfers between devices, to_experts(): lax.all_to_all(array, 'expert', split_axis=0, concat_axis=0, tiled=True)  7.02 us
  transfers between devices with their start and end apart: 24, of which 15 were waited for; matrix products, arithmetic and copies ran while one was open for 2% of the time, Pallas kernels for 18%

profile of v4, /device:TPU:8, one launch (start us, length us, event | category | flops | bytes accessed | tf_op | source)
XLA Modules:
  0.0 181.0 jit_solution(18017188691997559828)
XLA Ops:
  0.0 1.2 split_columns.2
  1.2 3.1 %collective-permute-start.3 = (bf16[128,640]{1,0:T(8,128)(2,1)S(1)}, bf16[128,640]{1,0:T(8,128)(2,1)S(1)}, u32[]{:S(2)}, u32[]{:S(2)}) collective-permute-start(bf16[128,640]{1,0:T(8,128)(2,1)S(1)} %get-tuple-element.36), channel_id=1, source_target_pairs={{0,2},{1,3},{2,0},{3,1},{4,6},{5,7},{6,4},{7,5},{8,10},{9,11},{10,... | collective-permute-start | bytes 491528 | tf_op jit(solution)/shard_map/group_exchange/ppermute | solution.py:338
  4.3 1.1 collective-permute-start.4
  5.5 0.9 collective-permute-start.5
  6.4 0.6 collective-permute-start.2
  7.0 2.6 %collective-permute-start.1 = (s32[1,128]{1,0:T(1,128)S(1)}, s32[1,128]{1,0:T(1,128)S(1)}, u32[]{:S(2)}, u32[]{:S(2)}) collective-permute-start(s32[1,128]{1,0:T(1,128)S(1)} %bitcast.11), channel_id=1, source_target_pairs={{0,3},{1,0},{2,1},{3,2},{4,7},{5,4},{6,5},{7,6},{8,11},{9,8},{10,9... | collective-permute-start | bytes 1544 | tf_op jit(solution)/shard_map/group_exchange/ppermute | solution.py:338
  9.6 3.2 %collective-permute-done.2.r3 = s32[1,128]{1,0:T(1,128)S(1)} collective-permute-done((s32[1,128]{1,0:T(1,128)S(1)}, s32[1,128]{1,0:T(1,128)S(1)}, u32[]{:S(2)}, u32[]{:S(2)}) %collective-permute-start.2) | collective-permute-done | bytes 544 | tf_op jit(solution)/shard_map/group_exchange/ppermute | solution.py:338
  12.8 2.5 %collective-permute-start = (s32[1,128]{1,0:T(1,128)S(1)}, s32[1,128]{1,0:T(1,128)S(1)}, u32[]{:S(2)}, u32[]{:S(2)}) collective-permute-start(s32[1,128]{1,0:T(1,128)S(1)} %bitcast.12), channel_id=1, source_target_pairs={{0,2},{1,3},{2,0},{3,1},{4,6},{5,7},{6,4},{7,5},{8,10},{9,11},{10,... | collective-permute-start | bytes 1544 | tf_op jit(solution)/shard_map/group_exchange/ppermute | solution.py:338
  15.4 2.5 %collective-permute-done.r1 = s32[1,128]{1,0:T(1,128)S(1)} collective-permute-done((s32[1,128]{1,0:T(1,128)S(1)}, s32[1,128]{1,0:T(1,128)S(1)}, u32[]{:S(2)}, u32[]{:S(2)}) %collective-permute-start) | collective-permute-done | bytes 544 | tf_op jit(solution)/shard_map/group_exchange/ppermute | solution.py:338
  17.9 0.5 slot_matrix.1
  18.4 0.7 convolution_convert_fusion.1
  19.1 1.2 reshape.26
  20.3 12.1 %all-to-all-start = ((bf16[64,5,2,640]{3,2,1,0:T(2,128)(2,1)}), bf16[64,5,2,640]{3,2,1,0:T(2,128)(2,1)S(1)}, u32[]{:S(2)}, u32[]{:S(2)}) async-start(bf16[64,5,2,640]{3,2,1,0:T(2,128)(2,1)} %reshape.26), calls=%async_computation | async-start | bytes 1638400 | tf_op jit(solution)/shard_map/send_tokens/all_to_all | solution.py:364
  32.4 0.1 copy.7.refs_4_
  32.5 1.4 split_columns.3
  33.9 2.6 %collective-permute-start.6 = (bf16[128,1024]{1,0:T(8,128)(2,1)S(1)}, bf16[128,1024]{1,0:T(8,128)(2,1)S(1)}, u32[]{:S(2)}, u32[]{:S(2)}) collective-permute-start(bf16[128,1024]{1,0:T(8,128)(2,1)S(1)} %get-tuple-element.40), channel_id=1, source_target_pairs={{0,2},{1,3},{2,0},{3,1},{4,6},{5,7},{6,4},{7,5},{8,10},{9,11},{10,... | collective-permute-start | bytes 786440 | tf_op jit(solution)/shard_map/group_exchange/ppermute | solution.py:338
  36.6 1.2 collective-permute-start.7
  37.8 0.8 collective-permute-start.8
  38.6 6.1 %collective-permute-done.6 = bf16[128,1024]{1,0:T(8,128)(2,1)S(1)} collective-permute-done((bf16[128,1024]{1,0:T(8,128)(2,1)S(1)}, bf16[128,1024]{1,0:T(8,128)(2,1)S(1)}, u32[]{:S(2)}, u32[]{:S(2)}) %collective-permute-start.6) | collective-permute-done | bytes 262176 | tf_op jit(solution)/shard_map/group_exchange/ppermute | solution.py:338
  44.7 2.7 %collective-permute-done.7 = bf16[128,1024]{1,0:T(8,128)(2,1)S(1)} collective-permute-done((bf16[128,1024]{1,0:T(8,128)(2,1)S(1)}, bf16[128,1024]{1,0:T(8,128)(2,1)S(1)}, u32[]{:S(2)}, u32[]{:S(2)}) %collective-permute-start.7) | collective-permute-done | bytes 262176 | tf_op jit(solution)/shard_map/group_exchange/ppermute | solution.py:338
  47.4 2.1 %collective-permute-done.8 = bf16[128,1024]{1,0:T(8,128)(2,1)S(1)} collective-permute-done((bf16[128,1024]{1,0:T(8,128)(2,1)S(1)}, bf16[128,1024]{1,0:T(8,128)(2,1)S(1)}, u32[]{:S(2)}, u32[]{:S(2)}) %collective-permute-start.8) | collective-permute-done | bytes 262176 | tf_op jit(solution)/shard_map/group_exchange/ppermute | solution.py:338
  49.5 0.9 convolution_convert_fusion
  50.4 1.4 reshape.27
  51.8 4.5 %all-to-all-done = bf16[64,5,2,640]{3,2,1,0:T(2,128)(2,1)S(1)} async-done(((bf16[64,5,2,640]{3,2,1,0:T(2,128)(2,1)}), bf16[64,5,2,640]{3,2,1,0:T(2,128)(2,1)S(1)}, u32[]{:S(2)}, u32[]{:S(2)}) %all-to-all-start) | async-done | bytes 819232 | tf_op jit(solution)/shard_map/send_tokens/all_to_all | solution.py:364
  56.2 0.3 reshape.29.refs_0_
  56.6 0.3 collective-permute-start.10
  56.9 1.8 collective-permute-start.9
  58.7 6.0 %all-to-all-start.1 = ((bf16[64,80,128]{2,1,0:T(8,128)(2,1)}), bf16[64,80,128]{2,1,0:T(8,128)(2,1)}, u32[]{:S(2)}, u32[]{:S(2)}) async-start(bf16[64,80,128]{2,1,0:T(8,128)(2,1)} %reshape.27), calls=%async_computation.1 | async-start | bytes 2621440 | tf_op jit(solution)/shard_map/send_hidden/all_to_all | solution.py:364
  64.7 4.0 %up_sums.2 = (f32[640,1024]{1,0:T(8,128)S(1)}, f32[640,1024]{1,0:T(8,128)S(1)}) custom-call(s32[1]{0:T(128)} %bitcast.x_ref, bf16[640,640]{1,0:T(8,128)(2,1)S(1)} %reshape.29.refs_0_, bf16[2560,1024]{1,0:T(8,128)(2,1)} %bitcast.14, bf16[2560,1024]{1,0:T(8,128)(2,1)} %bitcast.22), custom_call_target="tpu_custom_call" | custom-call | flops 10066329600 | bytes 13107200 | tf_op jit(solution)/shard_map/gather_width/up_sums/pallas_call | solution.py:155
  68.7 7.2 %collective-permute-done.10.refs_0_ = bf16[640,640]{1,0:T(8,128)(2,1)S(1)} collective-permute-done((bf16[640,640]{1,0:T(8,128)(2,1)S(1)}, bf16[640,640]{1,0:T(8,128)(2,1)S(1)}, u32[]{:S(2)}, u32[]{:S(2)}) %collective-permute-start.10) | collective-permute-done | bytes 819232 | tf_op jit(solution)/shard_map/gather_width/ppermute | solution.py:338
  76.0 1.4 collective-permute-done.9.refs_1_
  77.4 1.0 slice.18
  78.5 1.6 collective-permute-start.12
  80.1 0.5 collective-permute-start.11
  80.6 7.6 %up_sums.3 = (f32[640,1024]{1,0:T(8,128)}, f32[640,1024]{1,0:T(8,128)}) custom-call(s32[1]{0:T(128)} %bitcast.x_ref, bf16[640,640]{1,0:T(8,128)(2,1)S(1)} %collective-permute-done.10.refs_0_, bf16[640,640]{1,0:T(8,128)(2,1)} %collective-permute-done.9.refs_1_, bf16[2560,1024]{1,0:T(8,128)(2,1)} %bitcast.15, bf16[2560,1024]{1,0:T(8,128)(2,1)} %bitcast.16, ...), custom_call_target="tpu_custom_call" | custom-call | flops 20132659200 | bytes 15728640 | tf_op jit(solution)/shard_map/pre_activations/up_sums/pallas_call | solution.py:155
  88.2 2.1 %collective-permute-done.11.top = bf16[320,640]{1,0:T(8,128)(2,1)S(1)} collective-permute-done((bf16[320,640]{1,0:T(8,128)(2,1)S(1)}, bf16[320,640]{1,0:T(8,128)(2,1)S(1)}, u32[]{:S(2)}, u32[]{:S(2)}) %collective-permute-start.11) | collective-permute-done | bytes 409632 | tf_op jit(solution)/shard_map/gather_width/ppermute | solution.py:341
  90.3 6.1 %up_last.1 = (f32[640,1024]{1,0:T(8,128)}, f32[640,1024]{1,0:T(8,128)}) custom-call(s32[1]{0:T(128)} %bitcast.x_ref, bf16[320,640]{1,0:T(8,128)(2,1)S(1)} %collective-permute-done.11.top, bf16[320,640]{1,0:T(8,128)(2,1)S(1)} %collective-permute-done.12.bottom, f32[640,1024]{1,0:T(8,128)} %get-tuple-element.51.g_in, f32[640,1024]{1,0:T(8,128)} %get-tuple-element.52.u_in, ...), custom_call_target="tpu_custom_call" | custom-call | flops 1677721600 | bytes 13107200 | tf_op jit(solution)/shard_map/pre_activations/up_last/pallas_call | solution.py:198
  96.5 2.6 %all-to-all-done.1 = bf16[64,80,128]{2,1,0:T(8,128)(2,1)} async-done(((bf16[64,80,128]{2,1,0:T(8,128)(2,1)}), bf16[64,80,128]{2,1,0:T(8,128)(2,1)}, u32[]{:S(2)}, u32[]{:S(2)}) %all-to-all-start.1) | async-done | bytes 1310752 | tf_op jit(solution)/shard_map/send_hidden/all_to_all | solution.py:364
  99.0 2.4 %reshape.28.h = bf16[640,1024]{1,0:T(8,128)(2,1)S(1)} reshape(bf16[64,80,128]{2,1,0:T(8,128)(2,1)} %all-to-all-done.1) | data formatting | bytes 2621440 | tf_op jit(solution)/shard_map/send_hidden/reshape | solution.py:372
  101.4 6.1 %down_first.1 = (bf16[640,1024]{1,0:T(8,128)(2,1)S(1)}, bf16[640,1024]{1,0:T(8,128)(2,1)S(1)}, bf16[320,640]{1,0:T(8,128)(2,1)S(1)}, bf16[320,640]{1,0:T(8,128)(2,1)S(1)}) custom-call(s32[1]{0:T(128)} %bitcast.x_ref, bf16[640,1024]{1,0:T(8,128)(2,1)S(1)} %reshape.28.h, f32[640,1024]{1,0:T(8,128)} %get-tuple-element.53.a, f32[640,1024]{1,0:T(8,128)} %get-tuple-element.54.b, ...), custom_call_target="tpu_custom_call" | custom-call | flops 1677721600 | bytes 11796480 | tf_op jit(solution)/shard_map/input_partials/down_first/pallas_call | solution.py:247
  107.6 1.9 %collective-permute-start.17 = (bf16[320,640]{1,0:T(8,128)(2,1)S(1)}, bf16[320,640]{1,0:T(8,128)(2,1)S(1)}, u32[]{:S(2)}, u32[]{:S(2)}) collective-permute-start(bf16[320,640]{1,0:T(8,128)(2,1)S(1)} %get-tuple-element.64), channel_id=1, source_target_pairs={{0,3},{1,0},{2,1},{3,2},{4,7},{5,4},{6,5},{7,6},{8,11},{9,8},{10,9... | collective-permute-start | bytes 1228808 | tf_op jit(solution)/shard_map/sum_quarters/ppermute | solution.py:338
  109.4 0.2 collective-permute-start.13
  109.7 4.2 %down_halves.5 = (bf16[320,640]{1,0:T(8,128)(2,1)S(1)}, bf16[320,640]{1,0:T(8,128)(2,1)S(1)}) custom-call(s32[1]{0:T(128)} %bitcast.x_ref, bf16[640,1024]{1,0:T(8,128)(2,1)S(1)} %get-tuple-element.55.gg, bf16[640,1024]{1,0:T(8,128)(2,1)S(1)} %get-tuple-element.56.gu, bf16[2560,1024]{1,0:T(8,128)(2,1)} %bitcast.19, bf16[2560,1024]{1,0:T(8,128)(2,1)} %bitcast.27), custom_call_target="tpu_custom_call" | custom-call | flops 419430400 | bytes 7864320 | tf_op jit(solution)/shard_map/input_partials/down_halves/pallas_call | solution.py:288
  113.8 3.1 %collective-permute-start.15 = (bf16[320,640]{1,0:T(8,128)(2,1)S(1)}, bf16[320,640]{1,0:T(8,128)(2,1)S(1)}, u32[]{:S(2)}, u32[]{:S(2)}) collective-permute-start(bf16[320,640]{1,0:T(8,128)(2,1)S(1)} %get-tuple-element.60), channel_id=1, source_target_pairs={{0,3},{1,0},{2,1},{3,2},{4,7},{5,4},{6,5},{7,6},{8,11},{9,8},{10,9... | collective-permute-start | bytes 1228808 | tf_op jit(solution)/shard_map/sum_quarters/ppermute | solution.py:338
  116.9 4.2 %down_halves.4 = (f32[320,640]{1,0:T(8,128)S(1)}, f32[320,640]{1,0:T(8,128)S(1)}) custom-call(s32[1]{0:T(128)} %bitcast.x_ref, bf16[640,1024]{1,0:T(8,128)(2,1)S(1)} %get-tuple-element.55.gg, bf16[640,1024]{1,0:T(8,128)(2,1)S(1)} %get-tuple-element.56.gu, bf16[2560,1024]{1,0:T(8,128)(2,1)} %bitcast.20, bf16[2560,1024]{1,0:T(8,128)(2,1)} %bitcast.28), custom_call_target="tpu_custom_call" | custom-call | flops 419430400 | bytes 7864320 | tf_op jit(solution)/shard_map/input_partials/down_halves/pallas_call | solution.py:288
  121.1 0.1 add_convert_fusion
  121.2 3.3 %collective-permute-start.18 = (bf16[320,640]{1,0:T(8,128)(2,1)S(1)}, bf16[320,640]{1,0:T(8,128)(2,1)S(1)}, u32[]{:S(2)}, u32[]{:S(2)}) collective-permute-start(bf16[320,640]{1,0:T(8,128)(2,1)S(1)} %add_convert_fusion), channel_id=1, source_target_pairs={{0,3},{1,0},{2,1},{3,2},{4,7},{5,4},{6,5},{7,6},{8,11},{9,8},{10,9... | collective-permute-start | bytes 1228808 | tf_op jit(solution)/shard_map/sum_quarters/ppermute | solution.py:338
  124.6 0.1 add_convert_fusion.1
  124.7 0.1 collective-permute-start.14
  124.7 4.2 %down_halves.3 = (f32[320,640]{1,0:T(8,128)S(1)}, f32[320,640]{1,0:T(8,128)S(1)}) custom-call(s32[1]{0:T(128)} %bitcast.x_ref, bf16[640,1024]{1,0:T(8,128)(2,1)S(1)} %get-tuple-element.55.gg, bf16[640,1024]{1,0:T(8,128)(2,1)S(1)} %get-tuple-element.56.gu, bf16[2560,1024]{1,0:T(8,128)(2,1)} %bitcast.21, bf16[2560,1024]{1,0:T(8,128)(2,1)} %bitcast.29), custom_call_target="tpu_custom_call" | custom-call | flops 419430400 | bytes 7864320 | tf_op jit(solution)/shard_map/input_partials/down_halves/pallas_call | solution.py:288
  128.9 2.0 %collective-permute-done.16.refs_4_ = bf16[320,640]{1,0:T(8,128)(2,1)S(1)} collective-permute-done((bf16[320,640]{1,0:T(8,128)(2,1)S(1)}, bf16[320,640]{1,0:T(8,128)(2,1)S(1)}, u32[]{:S(2)}, u32[]{:S(2)}) %collective-permute-start.16) | collective-permute-done | bytes 409632 | tf_op jit(solution)/shard_map/sum_quarters/ppermute | solution.py:341
  131.0 4.3 %collective-permute-done.18.refs_5_ = bf16[320,640]{1,0:T(8,128)(2,1)S(1)} collective-permute-done((bf16[320,640]{1,0:T(8,128)(2,1)S(1)}, bf16[320,640]{1,0:T(8,128)(2,1)S(1)}, u32[]{:S(2)}, u32[]{:S(2)}) %collective-permute-start.18) | collective-permute-done | bytes 409632 | tf_op jit(solution)/shard_map/sum_quarters/ppermute | solution.py:338
  135.2 2.7 %collective-permute-done.14.refs_1_ = bf16[320,640]{1,0:T(8,128)(2,1)S(1)} collective-permute-done((bf16[320,640]{1,0:T(8,128)(2,1)S(1)}, bf16[320,640]{1,0:T(8,128)(2,1)S(1)}, u32[]{:S(2)}, u32[]{:S(2)}) %collective-permute-start.14) | collective-permute-done | bytes 409632 | tf_op jit(solution)/shard_map/sum_quarters/ppermute | solution.py:341
  138.0 0.2 sum_halves.1
  138.2 0.3 reshape.30
  138.6 30.2 %all_to_all.15 = bf16[64,5,2,640]{3,2,1,0:T(2,128)(2,1)S(1)} all-to-all(bf16[64,5,2,640]{3,2,1,0:T(2,128)(2,1)S(1)} %reshape.30), channel_id=1, replica_groups=mesh['expert'=64,'etp'=4] {'expert'}, dimensions={0} | all-to-all | bytes 1638400 | tf_op jit(solution)/shard_map/return_tokens/all_to_all | solution.py:364
  168.7 0.3 reshape.31
  169.0 0.8 convolution_convert_fusion.2
  169.9 0.4 collective-permute-start.21
  170.2 1.7 collective-permute-start.20
  172.0 0.1 collective-permute-start.19
  172.1 4.8 %collective-permute-done.21.b3 = bf16[128,640]{1,0:T(8,128)(2,1)S(1)} collective-permute-done((bf16[128,640]{1,0:T(8,128)(2,1)S(1)}, bf16[128,640]{1,0:T(8,128)(2,1)S(1)}, u32[]{:S(2)}, u32[]{:S(2)}) %collective-permute-start.21) | collective-permute-done | bytes 163872 | tf_op jit(solution)/shard_map/return_tokens/ppermute | solution.py:341
  177.0 3.2 %collective-permute-done.20.b2 = bf16[128,640]{1,0:T(8,128)(2,1)S(1)} collective-permute-done((bf16[128,640]{1,0:T(8,128)(2,1)S(1)}, bf16[128,640]{1,0:T(8,128)(2,1)S(1)}, u32[]{:S(2)}, u32[]{:S(2)}) %collective-permute-start.20) | collective-permute-done | bytes 163872 | tf_op jit(solution)/shard_map/return_tokens/ppermute | solution.py:341
  180.1 0.9 join_columns.1
  (17 shorter events, 0.1 us)
Async XLA Ops:
  0.0 6.4 %copy-start = (s32[128,1]{0,1:T(1,128)S(1)}, s32[128,1]{0,1:T(1,128)}, u32[]{:S(2)}) copy-start(s32[128,1]{0,1:T(1,128)} %param.8) | copy-start | bytes 1540
  1.2 17.1 %collective-permute-start.3 = (bf16[128,640]{1,0:T(8,128)(2,1)S(1)}, bf16[128,640]{1,0:T(8,128)(2,1)S(1)}, u32[]{:S(2)}, u32[]{:S(2)}) collective-permute-start(bf16[128,640]{1,0:T(8,128)(2,1)S(1)} %get-tuple-element.36), channel_id=1, source_target_pairs={{0,2},{1,3},{2,0},{3,1},{4,6},{5,7},{6,4},{7,5},{8,10},{9,11},{10,... | collective-permute-start | bytes 491528 | tf_op jit(solution)/shard_map/group_exchange/ppermute | solution.py:338
  4.3 14.0 %collective-permute-start.4 = (bf16[128,640]{1,0:T(8,128)(2,1)S(1)}, bf16[128,640]{1,0:T(8,128)(2,1)S(1)}, u32[]{:S(2)}, u32[]{:S(2)}) collective-permute-start(bf16[128,640]{1,0:T(8,128)(2,1)S(1)} %get-tuple-element.37), channel_id=1, source_target_pairs={{0,3},{1,0},{2,1},{3,2},{4,7},{5,4},{6,5},{7,6},{8,11},{9,8},{10,9... | collective-permute-start | bytes 491528 | tf_op jit(solution)/shard_map/group_exchange/ppermute | solution.py:338
  5.5 12.9 %collective-permute-start.5 = (bf16[128,640]{1,0:T(8,128)(2,1)S(1)}, bf16[128,640]{1,0:T(8,128)(2,1)S(1)}, u32[]{:S(2)}, u32[]{:S(2)}) collective-permute-start(bf16[128,640]{1,0:T(8,128)(2,1)S(1)} %get-tuple-element.38), channel_id=1, source_target_pairs={{0,1},{1,2},{2,3},{3,0},{4,5},{5,6},{6,7},{7,4},{8,9},{9,10},{10,1... | collective-permute-start | bytes 491528 | tf_op jit(solution)/shard_map/group_exchange/ppermute | solution.py:338
  6.4 6.4 %collective-permute-start.2 = (s32[1,128]{1,0:T(1,128)S(1)}, s32[1,128]{1,0:T(1,128)S(1)}, u32[]{:S(2)}, u32[]{:S(2)}) collective-permute-start(s32[1,128]{1,0:T(1,128)S(1)} %bitcast.10), channel_id=1, source_target_pairs={{0,1},{1,2},{2,3},{3,0},{4,5},{5,6},{6,7},{7,4},{8,9},{9,10},{10,1... | collective-permute-start | bytes 1544 | tf_op jit(solution)/shard_map/group_exchange/ppermute | solution.py:338
  7.0 8.4 %collective-permute-start.1 = (s32[1,128]{1,0:T(1,128)S(1)}, s32[1,128]{1,0:T(1,128)S(1)}, u32[]{:S(2)}, u32[]{:S(2)}) collective-permute-start(s32[1,128]{1,0:T(1,128)S(1)} %bitcast.11), channel_id=1, source_target_pairs={{0,3},{1,0},{2,1},{3,2},{4,7},{5,4},{6,5},{7,6},{8,11},{9,8},{10,9... | collective-permute-start | bytes 1544 | tf_op jit(solution)/shard_map/group_exchange/ppermute | solution.py:338
  12.8 5.0 %collective-permute-start = (s32[1,128]{1,0:T(1,128)S(1)}, s32[1,128]{1,0:T(1,128)S(1)}, u32[]{:S(2)}, u32[]{:S(2)}) collective-permute-start(s32[1,128]{1,0:T(1,128)S(1)} %bitcast.12), channel_id=1, source_target_pairs={{0,2},{1,3},{2,0},{3,1},{4,6},{5,7},{6,4},{7,5},{8,10},{9,11},{10,... | collective-permute-start | bytes 1544 | tf_op jit(solution)/shard_map/group_exchange/ppermute | solution.py:338
  19.0 13.3 %copy-start.1 = (s32[128]{0:T(128)S(1)}, s32[128]{0:T(128)}, u32[]{:S(2)}) copy-start(s32[128]{0:T(128)} %param.9) | copy-start | bytes 1540
  20.3 36.0 %all-to-all-start = ((bf16[64,5,2,640]{3,2,1,0:T(2,128)(2,1)}), bf16[64,5,2,640]{3,2,1,0:T(2,128)(2,1)S(1)}, u32[]{:S(2)}, u32[]{:S(2)}) async-start(bf16[64,5,2,640]{3,2,1,0:T(2,128)(2,1)} %reshape.26), calls=%async_computation | async-start | bytes 1638400 | tf_op jit(solution)/shard_map/send_tokens/all_to_all | solution.py:364
  33.9 10.8 %collective-permute-start.6 = (bf16[128,1024]{1,0:T(8,128)(2,1)S(1)}, bf16[128,1024]{1,0:T(8,128)(2,1)S(1)}, u32[]{:S(2)}, u32[]{:S(2)}) collective-permute-start(bf16[128,1024]{1,0:T(8,128)(2,1)S(1)} %get-tuple-element.40), channel_id=1, source_target_pairs={{0,2},{1,3},{2,0},{3,1},{4,6},{5,7},{6,4},{7,5},{8,10},{9,11},{10,... | collective-permute-start | bytes 786440 | tf_op jit(solution)/shard_map/group_exchange/ppermute | solution.py:338
  36.6 10.8 %collective-permute-start.7 = (bf16[128,1024]{1,0:T(8,128)(2,1)S(1)}, bf16[128,1024]{1,0:T(8,128)(2,1)S(1)}, u32[]{:S(2)}, u32[]{:S(2)}) collective-permute-start(bf16[128,1024]{1,0:T(8,128)(2,1)S(1)} %get-tuple-element.41), channel_id=1, source_target_pairs={{0,3},{1,0},{2,1},{3,2},{4,7},{5,4},{6,5},{7,6},{8,11},{9,8},{10,9... | collective-permute-start | bytes 786440 | tf_op jit(solution)/shard_map/group_exchange/ppermute | solution.py:338
  37.8 11.7 %collective-permute-start.8 = (bf16[128,1024]{1,0:T(8,128)(2,1)S(1)}, bf16[128,1024]{1,0:T(8,128)(2,1)S(1)}, u32[]{:S(2)}, u32[]{:S(2)}) collective-permute-start(bf16[128,1024]{1,0:T(8,128)(2,1)S(1)} %get-tuple-element.42), channel_id=1, source_target_pairs={{0,1},{1,2},{2,3},{3,0},{4,5},{5,6},{6,7},{7,4},{8,9},{9,10},{10,1... | collective-permute-start | bytes 786440 | tf_op jit(solution)/shard_map/group_exchange/ppermute | solution.py:338
  56.6 19.4 %collective-permute-start.10 = (bf16[640,640]{1,0:T(8,128)(2,1)S(1)}, bf16[640,640]{1,0:T(8,128)(2,1)S(1)}, u32[]{:S(2)}, u32[]{:S(2)}) collective-permute-start(bf16[640,640]{1,0:T(8,128)(2,1)S(1)} %reshape.29.refs_0_), channel_id=1, source_target_pairs={{0,3},{1,0},{2,1},{3,2},{4,7},{5,4},{6,5},{7,6},{8,11},{9,8},{10,9... | collective-permute-start | bytes 2457608 | tf_op jit(solution)/shard_map/gather_width/ppermute | solution.py:338
  56.9 20.5 %collective-permute-start.9 = (bf16[640,640]{1,0:T(8,128)(2,1)S(1)}, bf16[640,640]{1,0:T(8,128)(2,1)}, u32[]{:S(2)}, u32[]{:S(2)}) collective-permute-start(bf16[640,640]{1,0:T(8,128)(2,1)S(1)} %reshape.29.refs_0_), channel_id=1, source_target_pairs={{0,1},{1,2},{2,3},{3,0},{4,5},{5,6},{6,7},{7,4},{8,9},{9,10},{10,1... | collective-permute-start | bytes 2457608 | tf_op jit(solution)/shard_map/gather_width/ppermute | solution.py:341
  58.7 40.4 %all-to-all-start.1 = ((bf16[64,80,128]{2,1,0:T(8,128)(2,1)}), bf16[64,80,128]{2,1,0:T(8,128)(2,1)}, u32[]{:S(2)}, u32[]{:S(2)}) async-start(bf16[64,80,128]{2,1,0:T(8,128)(2,1)} %reshape.27), calls=%async_computation.1 | async-start | bytes 2621440 | tf_op jit(solution)/shard_map/send_hidden/all_to_all | solution.py:364
  78.5 9.7 %collective-permute-start.12 = (bf16[320,640]{1,0:T(8,128)(2,1)S(1)}, bf16[320,640]{1,0:T(8,128)(2,1)S(1)}, u32[]{:S(2)}, u32[]{:S(2)}) collective-permute-start(bf16[320,640]{1,0:T(8,128)(2,1)S(1)} %slice.19), channel_id=1, source_target_pairs={{0,3},{1,0},{2,1},{3,2},{4,7},{5,4},{6,5},{7,6},{8,11},{9,8},{10,9... | collective-permute-start | bytes 1228808 | tf_op jit(solution)/shard_map/gather_width/ppermute | solution.py:338
  80.1 10.3 %collective-permute-start.11 = (bf16[320,640]{1,0:T(8,128)(2,1)S(1)}, bf16[320,640]{1,0:T(8,128)(2,1)S(1)}, u32[]{:S(2)}, u32[]{:S(2)}) collective-permute-start(bf16[320,640]{1,0:T(8,128)(2,1)S(1)} %slice.18), channel_id=1, source_target_pairs={{0,1},{1,2},{2,3},{3,0},{4,5},{5,6},{6,7},{7,4},{8,9},{9,10},{10,1... | collective-permute-start | bytes 1228808 | tf_op jit(solution)/shard_map/gather_width/ppermute | solution.py:341
  107.6 13.6 %collective-permute-start.17 = (bf16[320,640]{1,0:T(8,128)(2,1)S(1)}, bf16[320,640]{1,0:T(8,128)(2,1)S(1)}, u32[]{:S(2)}, u32[]{:S(2)}) collective-permute-start(bf16[320,640]{1,0:T(8,128)(2,1)S(1)} %get-tuple-element.64), channel_id=1, source_target_pairs={{0,3},{1,0},{2,1},{3,2},{4,7},{5,4},{6,5},{7,6},{8,11},{9,8},{10,9... | collective-permute-start | bytes 1228808 | tf_op jit(solution)/shard_map/sum_quarters/ppermute | solution.py:338
  109.4 15.1 %collective-permute-start.13 = (bf16[320,640]{1,0:T(8,128)(2,1)S(1)}, bf16[320,640]{1,0:T(8,128)(2,1)S(1)}, u32[]{:S(2)}, u32[]{:S(2)}) collective-permute-start(bf16[320,640]{1,0:T(8,128)(2,1)S(1)} %get-tuple-element.59), channel_id=1, source_target_pairs={{0,1},{1,2},{2,3},{3,0},{4,5},{5,6},{6,7},{7,4},{8,9},{9,10},{10,1... | collective-permute-start | bytes 1228808 | tf_op jit(solution)/shard_map/sum_quarters/ppermute | solution.py:341
  113.8 15.1 %collective-permute-start.15 = (bf16[320,640]{1,0:T(8,128)(2,1)S(1)}, bf16[320,640]{1,0:T(8,128)(2,1)S(1)}, u32[]{:S(2)}, u32[]{:S(2)}) collective-permute-start(bf16[320,640]{1,0:T(8,128)(2,1)S(1)} %get-tuple-element.60), channel_id=1, source_target_pairs={{0,3},{1,0},{2,1},{3,2},{4,7},{5,4},{6,5},{7,6},{8,11},{9,8},{10,9... | collective-permute-start | bytes 1228808 | tf_op jit(solution)/shard_map/sum_quarters/ppermute | solution.py:338
  116.9 14.0 %collective-permute-start.16 = (bf16[320,640]{1,0:T(8,128)(2,1)S(1)}, bf16[320,640]{1,0:T(8,128)(2,1)S(1)}, u32[]{:S(2)}, u32[]{:S(2)}) collective-permute-start(bf16[320,640]{1,0:T(8,128)(2,1)S(1)} %get-tuple-element.62), channel_id=1, source_target_pairs={{0,1},{1,2},{2,3},{3,0},{4,5},{5,6},{6,7},{7,4},{8,9},{9,10},{10,1... | collective-permute-start | bytes 1228808 | tf_op jit(solution)/shard_map/sum_quarters/ppermute | solution.py:341
  121.2 14.0 %collective-permute-start.18 = (bf16[320,640]{1,0:T(8,128)(2,1)S(1)}, bf16[320,640]{1,0:T(8,128)(2,1)S(1)}, u32[]{:S(2)}, u32[]{:S(2)}) collective-permute-start(bf16[320,640]{1,0:T(8,128)(2,1)S(1)} %add_convert_fusion), channel_id=1, source_target_pairs={{0,3},{1,0},{2,1},{3,2},{4,7},{5,4},{6,5},{7,6},{8,11},{9,8},{10,9... | collective-permute-start | bytes 1228808 | tf_op jit(solution)/shard_map/sum_quarters/ppermute | solution.py:338
  124.7 13.3 %collective-permute-start.14 = (bf16[320,640]{1,0:T(8,128)(2,1)S(1)}, bf16[320,640]{1,0:T(8,128)(2,1)S(1)}, u32[]{:S(2)}, u32[]{:S(2)}) collective-permute-start(bf16[320,640]{1,0:T(8,128)(2,1)S(1)} %add_convert_fusion.1), channel_id=1, source_target_pairs={{0,1},{1,2},{2,3},{3,0},{4,5},{5,6},{6,7},{7,4},{8,9},{9,10},{10,1... | collective-permute-start | bytes 1228808 | tf_op jit(solution)/shard_map/sum_quarters/ppermute | solution.py:341
  169.9 7.1 %collective-permute-start.21 = (bf16[128,640]{1,0:T(8,128)(2,1)S(1)}, bf16[128,640]{1,0:T(8,128)(2,1)S(1)}, u32[]{:S(2)}, u32[]{:S(2)}) collective-permute-start(bf16[128,640]{1,0:T(8,128)(2,1)S(1)} %get-tuple-element.65), channel_id=1, source_target_pairs={{0,3},{1,0},{2,1},{3,2},{4,7},{5,4},{6,5},{7,6},{8,11},{9,8},{10,9... | collective-permute-start | bytes 491528 | tf_op jit(solution)/shard_map/return_tokens/ppermute | solution.py:341
  170.2 9.9 %collective-permute-start.20 = (bf16[128,640]{1,0:T(8,128)(2,1)S(1)}, bf16[128,640]{1,0:T(8,128)(2,1)S(1)}, u32[]{:S(2)}, u32[]{:S(2)}) collective-permute-start(bf16[128,640]{1,0:T(8,128)(2,1)S(1)} %get-tuple-element.66), channel_id=1, source_target_pairs={{0,1},{1,2},{2,3},{3,0},{4,5},{5,6},{6,7},{7,4},{8,9},{9,10},{10,1... | collective-permute-start | bytes 491528 | tf_op jit(solution)/shard_map/return_tokens/ppermute | solution.py:341
  172.0 8.1 %collective-permute-start.19 = (bf16[128,640]{1,0:T(8,128)(2,1)S(1)}, bf16[128,640]{1,0:T(8,128)(2,1)S(1)}, u32[]{:S(2)}, u32[]{:S(2)}) collective-permute-start(bf16[128,640]{1,0:T(8,128)(2,1)S(1)} %get-tuple-element.67), channel_id=1, source_target_pairs={{0,2},{1,3},{2,0},{3,1},{4,6},{5,7},{6,4},{7,5},{8,10},{9,11},{10,... | collective-permute-start | bytes 491528 | tf_op jit(solution)/shard_map/return_tokens/ppermute | solution.py:341

commit v5 on v4

--- a/solution.py
+++ b/solution.py
@@ -83,13 +83,14 @@
     )(x, *blocks)
 
 
-def slot_matrix(route_blocks, x, offsets, experts, capacity):
-    own_rows = route_blocks[0].shape[1]
+def slot_index(group_routes, x, offsets, experts, capacity):
+    own_rows = group_routes.shape[1]
     group = own_rows * len(offsets)
-    slots = experts * capacity
-
-    def kernel(x_ref, r0, r1, r2, r3, out):
-        routes = jnp.concatenate([r[...] for r in (r0, r1, r2, r3)], axis=1)
+
+    def kernel(x_ref, all_routes, out):
+        routes = jnp.concatenate(
+            [all_routes[pl.ds(quarter_at(x_ref, offset), 1), :] for offset in offsets], axis=1
+        )
 
         def places(axis):
             row = lax.broadcasted_iota(jnp.int32, (group, group), axis)
@@ -104,24 +105,21 @@
         named = jnp.where(same, 1.0, 0.0)
         counts = jnp.dot(named.astype(BF), before, preferred_element_type=F32)
         rank = jnp.sum(named * counts, axis=0, keepdims=True).astype(jnp.int32)
-        slot = routes * capacity + rank
-        filled = lax.broadcasted_iota(jnp.int32, (slots, group), 0) == slot
-        out[...] = jnp.where(filled, 1.0, 0.0).astype(BF)
-
-    block = pl.BlockSpec((1, own_rows), lambda i, x_ref: (0, 0))
+        out[...] = routes * capacity + rank
+
     return pl.pallas_call(
         kernel,
         grid_spec=pltpu.PrefetchScalarGridSpec(
             num_scalar_prefetch=1,
             grid=(1,),
-            in_specs=[block] * 4,
-            out_specs=pl.BlockSpec((slots, group), lambda i, x_ref: (0, 0)),
-        ),
-        out_shape=jax.ShapeDtypeStruct((slots, group), BF),
+            in_specs=[pl.BlockSpec(group_routes.shape, lambda i, x_ref: (0, 0))],
+            out_specs=pl.BlockSpec((1, group), lambda i, x_ref: (0, 0)),
+        ),
+        out_shape=jax.ShapeDtypeStruct((1, group), jnp.int32),
         compiler_params=params(),
         cost_estimate=cost(0, 0),
-        name="slot_matrix",
-    )(x, *route_blocks)
+        name="slot_index",
+    )(x, group_routes)
 
 
 HIDDEN_TILE = 512
@@ -346,8 +344,7 @@
         group_tokens = jnp.concatenate(
             [token_parts[0]] + [back(token_parts[k], ahead[k]) for k in (1, 2, 3)]
         )
-        own_routes = routes.reshape(1, own_rows)
-        route_blocks = [own_routes] + [back(own_routes, r) for r in ahead[1:]]
+        group_routes = lax.all_gather(routes.reshape(1, own_rows), "etp", axis=0, tiled=True)
         scales = jnp.exp2(exponents.astype(F32))[:, None]
         hidden_parts = split_columns(hidden_grad, x, [-r for r in ahead], scales)
         group_hidden = jnp.concatenate(
@@ -355,7 +352,8 @@
         )
 
     with jax.named_scope("slots"):
-        select = slot_matrix(route_blocks, x, ahead, experts, capacity)
+        slot = slot_index(group_routes, x, ahead, experts, capacity)
+        select = (jnp.arange(slots, dtype=jnp.int32)[:, None] == slot).astype(BF)
 
     def pick(rows):
         return jnp.dot(select, rows, preferred_element_type=F32).astype(BF)
@@ -365,7 +363,7 @@
 
     with jax.named_scope("send_tokens"):
         packed_tokens = pick(group_tokens).reshape(experts, capacity // 2, 2, quarter)
-        packed_hidden = pick(group_hidden).reshape(experts, capacity * hidden // 128, 128)
+        packed_hidden = pick(group_hidden).reshape(experts, capacity // 2, 2, hidden)
         arrived, packed_hidden = lax.optimization_barrier((to_experts(packed_tokens), packed_hidden))
         own_block = arrived.reshape(slots, quarter)
     with jax.named_scope("send_hidden"):

time: 182 us -> 181 us (level)
  blocking collectives: 30.2 us -> 40.4 us
  starting transfers between devices: 48.7 us -> 41.5 us
  waiting for transfers between devices: 51.5 us -> 48.9 us
    all_gather x0 -> x1, blocking collectives: none -> 10.2 us  [on_device(): lax.all_gather(routes.reshape(1, own_rows), 'etp', axis=0, tiled=True)]
    ppermute x14 -> x11, starting transfers between devices: 25.8 us -> 18.3 us  [back(): return lax.ppermute(array, 'etp', [(i, (i - r) % etp) for i in range(etp)])]
    ppermute x14 -> x11, waiting for transfers between devices: 28.1 us -> 24.1 us  [back(): return lax.ppermute(array, 'etp', [(i, (i - r) % etp) for i in range(etp)])]
  transfers between devices with their start and end apart: 24 -> 21, of which waited for: 15 -> 14; matrix products, arithmetic and copies ran while one was open for 2% -> 1% of each run, Pallas kernels for 18% -> 17%
where the time goes in v5:
time: 181 us
  waiting for transfers between devices  48.9 us (27%)
  starting transfers between devices  41.5 us (23%)
  blocking collectives  40.4 us (22%)
  Pallas kernels  40.1 us (22%)
  local copies, waits for them, and re-layouts  6.96 us (4%)
  matrix products  2.37 us (1%)
    all_to_all x1, blocking collectives, to_experts(): lax.all_to_all(array, 'expert', split_axis=0, concat_axis=0, tiled=True)  30.1 us
    ppermute x11, waiting for transfers between devices, back(): return lax.ppermute(array, 'etp', [(i, (i - r) % etp) for i in range(etp)])  24.1 us
    ppermute x11, starting transfers between devices, back(): return lax.ppermute(array, 'etp', [(i, (i - r) % etp) for i in range(etp)])  18.3 us
    all_to_all x2, starting transfers between devices, to_experts(): lax.all_to_all(array, 'expert', split_axis=0, concat_axis=0, tiled=True)  18.1 us
    ppermute x8, waiting for transfers between devices, forward(): return lax.ppermute(array, 'etp', [(i, (i + r) % etp) for i in range(etp)])  16.4 us
    pallas_call x3, Pallas kernels, down_halves(): pl.pallas_call(kernel, grid_spec=pltpu.PrefetchScalarGridSpec(num_scalar_...  12.5 us
    pallas_call x2, Pallas kernels, up_sums(): pl.pallas_call(kernel, grid_spec=pltpu.PrefetchScalarGridSpec(num_scalar_...  11.3 us
    all_gather x1, blocking collectives, on_device(): lax.all_gather(routes.reshape(1, own_rows), 'etp', axis=0, tiled=True)  10.2 us
  transfers between devices with their start and end apart: 21, of which 14 were waited for; matrix products, arithmetic and copies ran while one was open for 1% of the time, Pallas kernels for 17%

profile of v5, /device:TPU:8, one launch (start us, length us, event | category | flops | bytes accessed | tf_op | source)
XLA Modules:
  0.0 180.7 jit_solution(727231881636477424)
XLA Ops:
  0.0 1.2 split_columns.2
  1.2 3.1 %collective-permute-start = (bf16[128,640]{1,0:T(8,128)(2,1)S(1)}, bf16[128,640]{1,0:T(8,128)(2,1)S(1)}, u32[]{:S(2)}, u32[]{:S(2)}) collective-permute-start(bf16[128,640]{1,0:T(8,128)(2,1)S(1)} %get-tuple-element.36), channel_id=1, source_target_pairs={{0,2},{1,3},{2,0},{3,1},{4,6},{5,7},{6,4},{7,5},{8,10},{9,11},{10,... | collective-permute-start | bytes 491528 | tf_op jit(solution)/shard_map/group_exchange/ppermute | solution.py:336
  4.3 1.1 collective-permute-start.1
  5.5 0.9 collective-permute-start.2
  6.4 10.2 %all-gather = s32[512,1]{0,1:T(1,128)S(1)} all-gather(s32[128,1]{0,1:T(1,128)S(1)} %copy-done), channel_id=2, replica_groups=mesh['expert'=64,'etp'=4] {'etp'}, dimensions={0}, use_global_device_ids=true | all-gather | bytes 2560 | tf_op jit(solution)/shard_map/group_exchange/all_gather | solution.py:347
  16.6 0.2 slot_index.1
  16.8 0.0 collective-permute-done
  16.9 0.0 collective-permute-done.1
  16.9 0.7 convolution_convert_fusion.1
  17.6 0.0 copy-start.1
  17.6 1.2 reshape.26
  18.8 12.1 %all-to-all-start = ((bf16[64,5,2,640]{3,2,1,0:T(2,128)(2,1)}), bf16[64,5,2,640]{3,2,1,0:T(2,128)(2,1)S(1)}, u32[]{:S(2)}, u32[]{:S(2)}) async-start(bf16[64,5,2,640]{3,2,1,0:T(2,128)(2,1)} %reshape.26), calls=%async_computation | async-start | bytes 1638400 | tf_op jit(solution)/shard_map/send_tokens/all_to_all | solution.py:362
  30.9 0.1 copy.7.refs_4_
  31.1 1.4 split_columns.3
  32.5 0.9 collective-permute-start.3
  33.4 1.6 collective-permute-start.4
  35.0 0.5 collective-permute-start.5
  35.5 7.8 %collective-permute-done.3 = bf16[128,1024]{1,0:T(8,128)(2,1)S(1)} collective-permute-done((bf16[128,1024]{1,0:T(8,128)(2,1)S(1)}, bf16[128,1024]{1,0:T(8,128)(2,1)S(1)}, u32[]{:S(2)}, u32[]{:S(2)}) %collective-permute-start.3) | collective-permute-done | bytes 262176 | tf_op jit(solution)/shard_map/group_exchange/ppermute | solution.py:336
  43.3 3.0 %collective-permute-done.4 = bf16[128,1024]{1,0:T(8,128)(2,1)S(1)} collective-permute-done((bf16[128,1024]{1,0:T(8,128)(2,1)S(1)}, bf16[128,1024]{1,0:T(8,128)(2,1)S(1)}, u32[]{:S(2)}, u32[]{:S(2)}) %collective-permute-start.4) | collective-permute-done | bytes 262176 | tf_op jit(solution)/shard_map/group_exchange/ppermute | solution.py:336
  46.3 1.8 collective-permute-done.5
  48.1 0.8 convolution_convert_fusion
  48.9 1.4 reshape.27
  50.3 4.5 %all-to-all-done = bf16[64,5,2,640]{3,2,1,0:T(2,128)(2,1)S(1)} async-done(((bf16[64,5,2,640]{3,2,1,0:T(2,128)(2,1)}), bf16[64,5,2,640]{3,2,1,0:T(2,128)(2,1)S(1)}, u32[]{:S(2)}, u32[]{:S(2)}) %all-to-all-start) | async-done | bytes 819232 | tf_op jit(solution)/shard_map/send_tokens/all_to_all | solution.py:362
  54.8 0.3 reshape.29.refs_0_
  55.1 0.9 collective-permute-start.7
  56.0 1.2 collective-permute-start.6
  57.2 6.0 %all-to-all-start.1 = ((bf16[64,5,2,1024]{3,2,1,0:T(2,128)(2,1)}), bf16[64,5,2,1024]{3,2,1,0:T(2,128)(2,1)}, u32[]{:S(2)}, u32[]{:S(2)}) async-start(bf16[64,5,2,1024]{3,2,1,0:T(2,128)(2,1)} %reshape.27), calls=%async_computation.1 | async-start | bytes 2621440 | tf_op jit(solution)/shard_map/send_hidden/all_to_all | solution.py:362
  63.2 4.0 %up_sums.2 = (f32[640,1024]{1,0:T(8,128)S(1)}, f32[640,1024]{1,0:T(8,128)S(1)}) custom-call(s32[1]{0:T(128)} %bitcast.x_ref, bf16[640,640]{1,0:T(8,128)(2,1)S(1)} %reshape.29.refs_0_, bf16[2560,1024]{1,0:T(8,128)(2,1)} %bitcast.12, bf16[2560,1024]{1,0:T(8,128)(2,1)} %bitcast.20), custom_call_target="tpu_custom_call" | custom-call | flops 10066329600 | bytes 13107200 | tf_op jit(solution)/shard_map/gather_width/up_sums/pallas_call | solution.py:153
  67.2 7.3 %collective-permute-done.7.refs_0_ = bf16[640,640]{1,0:T(8,128)(2,1)S(1)} collective-permute-done((bf16[640,640]{1,0:T(8,128)(2,1)S(1)}, bf16[640,640]{1,0:T(8,128)(2,1)S(1)}, u32[]{:S(2)}, u32[]{:S(2)}) %collective-permute-start.7) | collective-permute-done | bytes 819232 | tf_op jit(solution)/shard_map/gather_width/ppermute | solution.py:336
  74.5 1.8 collective-permute-done.6.refs_1_
  76.4 0.5 collective-permute-start.9
  76.9 1.7 collective-permute-start.8
  78.6 7.3 %up_sums.3 = (f32[640,1024]{1,0:T(8,128)}, f32[640,1024]{1,0:T(8,128)}) custom-call(s32[1]{0:T(128)} %bitcast.x_ref, bf16[640,640]{1,0:T(8,128)(2,1)S(1)} %collective-permute-done.7.refs_0_, bf16[640,640]{1,0:T(8,128)(2,1)S(1)} %collective-permute-done.6.refs_1_, bf16[2560,1024]{1,0:T(8,128)(2,1)} %bitcast.13, bf16[2560,1024]{1,0:T(8,128)(2,1)} %bitcast.14, ...), custom_call_target="tpu_custom_call" | custom-call | flops 20132659200 | bytes 15728640 | tf_op jit(solution)/shard_map/pre_activations/up_sums/pallas_call | solution.py:153
  85.9 0.2 collective-permute-done.9.bottom
  86.1 1.5 collective-permute-done.8.top
  87.6 6.1 %up_last.1 = (f32[640,1024]{1,0:T(8,128)}, f32[640,1024]{1,0:T(8,128)}) custom-call(s32[1]{0:T(128)} %bitcast.x_ref, bf16[320,640]{1,0:T(8,128)(2,1)S(1)} %collective-permute-done.8.top, bf16[320,640]{1,0:T(8,128)(2,1)S(1)} %collective-permute-done.9.bottom, f32[640,1024]{1,0:T(8,128)} %get-tuple-element.51.g_in, f32[640,1024]{1,0:T(8,128)} %get-tuple-element.52.u_in, ...), custom_call_target="tpu_custom_call" | custom-call | flops 1677721600 | bytes 13107200 | tf_op jit(solution)/shard_map/pre_activations/up_last/pallas_call | solution.py:196
  93.7 3.9 %all-to-all-done.1 = bf16[64,5,2,1024]{3,2,1,0:T(2,128)(2,1)} async-done(((bf16[64,5,2,1024]{3,2,1,0:T(2,128)(2,1)}), bf16[64,5,2,1024]{3,2,1,0:T(2,128)(2,1)}, u32[]{:S(2)}, u32[]{:S(2)}) %all-to-all-start.1) | async-done | bytes 1310752 | tf_op jit(solution)/shard_map/send_hidden/all_to_all | solution.py:362
  97.5 3.2 %reshape.28.h = bf16[640,1024]{1,0:T(8,128)(2,1)S(1)} reshape(bf16[64,5,2,1024]{3,2,1,0:T(2,128)(2,1)} %all-to-all-done.1) | data formatting | bytes 2621440 | tf_op jit(solution)/shard_map/send_hidden/reshape | solution.py:370
  100.7 6.1 %down_first.1 = (bf16[640,1024]{1,0:T(8,128)(2,1)S(1)}, bf16[640,1024]{1,0:T(8,128)(2,1)S(1)}, bf16[320,640]{1,0:T(8,128)(2,1)S(1)}, bf16[320,640]{1,0:T(8,128)(2,1)S(1)}) custom-call(s32[1]{0:T(128)} %bitcast.x_ref, bf16[640,1024]{1,0:T(8,128)(2,1)S(1)} %reshape.28.h, f32[640,1024]{1,0:T(8,128)} %get-tuple-element.53.a, f32[640,1024]{1,0:T(8,128)} %get-tuple-element.54.b, ...), custom_call_target="tpu_custom_call" | custom-call | flops 1677721600 | bytes 11796480 | tf_op jit(solution)/shard_map/input_partials/down_first/pallas_call | solution.py:245
  106.9 2.1 %collective-permute-start.14 = (bf16[320,640]{1,0:T(8,128)(2,1)S(1)}, bf16[320,640]{1,0:T(8,128)(2,1)S(1)}, u32[]{:S(2)}, u32[]{:S(2)}) collective-permute-start(bf16[320,640]{1,0:T(8,128)(2,1)S(1)} %get-tuple-element.64), channel_id=1, source_target_pairs={{0,3},{1,0},{2,1},{3,2},{4,7},{5,4},{6,5},{7,6},{8,11},{9,8},{10,9... | collective-permute-start | bytes 1228808 | tf_op jit(solution)/shard_map/sum_quarters/ppermute | solution.py:336
  109.0 0.0 collective-permute-start.10
  109.0 4.2 %down_halves.5 = (bf16[320,640]{1,0:T(8,128)(2,1)S(1)}, bf16[320,640]{1,0:T(8,128)(2,1)S(1)}) custom-call(s32[1]{0:T(128)} %bitcast.x_ref, bf16[640,1024]{1,0:T(8,128)(2,1)S(1)} %get-tuple-element.55.gg, bf16[640,1024]{1,0:T(8,128)(2,1)S(1)} %get-tuple-element.56.gu, bf16[2560,1024]{1,0:T(8,128)(2,1)} %bitcast.17, bf16[2560,1024]{1,0:T(8,128)(2,1)} %bitcast.25), custom_call_target="tpu_custom_call" | custom-call | flops 419430400 | bytes 7864320 | tf_op jit(solution)/shard_map/input_partials/down_halves/pallas_call | solution.py:286
  113.2 3.3 %collective-permute-start.12 = (bf16[320,640]{1,0:T(8,128)(2,1)S(1)}, bf16[320,640]{1,0:T(8,128)(2,1)S(1)}, u32[]{:S(2)}, u32[]{:S(2)}) collective-permute-start(bf16[320,640]{1,0:T(8,128)(2,1)S(1)} %get-tuple-element.60), channel_id=1, source_target_pairs={{0,3},{1,0},{2,1},{3,2},{4,7},{5,4},{6,5},{7,6},{8,11},{9,8},{10,9... | collective-permute-start | bytes 1228808 | tf_op jit(solution)/shard_map/sum_quarters/ppermute | solution.py:336
  116.5 0.0 collective-permute-start.13
  116.5 4.2 %down_halves.4 = (f32[320,640]{1,0:T(8,128)S(1)}, f32[320,640]{1,0:T(8,128)S(1)}) custom-call(s32[1]{0:T(128)} %bitcast.x_ref, bf16[640,1024]{1,0:T(8,128)(2,1)S(1)} %get-tuple-element.55.gg, bf16[640,1024]{1,0:T(8,128)(2,1)S(1)} %get-tuple-element.56.gu, bf16[2560,1024]{1,0:T(8,128)(2,1)} %bitcast.18, bf16[2560,1024]{1,0:T(8,128)(2,1)} %bitcast.26), custom_call_target="tpu_custom_call" | custom-call | flops 419430400 | bytes 7864320 | tf_op jit(solution)/shard_map/input_partials/down_halves/pallas_call | solution.py:286
  120.7 0.1 add_convert_fusion
  120.8 3.3 %collective-permute-start.15 = (bf16[320,640]{1,0:T(8,128)(2,1)S(1)}, bf16[320,640]{1,0:T(8,128)(2,1)S(1)}, u32[]{:S(2)}, u32[]{:S(2)}) collective-permute-start(bf16[320,640]{1,0:T(8,128)(2,1)S(1)} %add_convert_fusion), channel_id=1, source_target_pairs={{0,3},{1,0},{2,1},{3,2},{4,7},{5,4},{6,5},{7,6},{8,11},{9,8},{10,9... | collective-permute-start | bytes 1228808 | tf_op jit(solution)/shard_map/sum_quarters/ppermute | solution.py:336
  124.1 0.1 add_convert_fusion.1
  124.2 0.1 collective-permute-start.11
  124.3 4.2 %down_halves.3 = (f32[320,640]{1,0:T(8,128)S(1)}, f32[320,640]{1,0:T(8,128)S(1)}) custom-call(s32[1]{0:T(128)} %bitcast.x_ref, bf16[640,1024]{1,0:T(8,128)(2,1)S(1)} %get-tuple-element.55.gg, bf16[640,1024]{1,0:T(8,128)(2,1)S(1)} %get-tuple-element.56.gu, bf16[2560,1024]{1,0:T(8,128)(2,1)} %bitcast.19, bf16[2560,1024]{1,0:T(8,128)(2,1)} %bitcast.27), custom_call_target="tpu_custom_call" | custom-call | flops 419430400 | bytes 7864320 | tf_op jit(solution)/shard_map/input_partials/down_halves/pallas_call | solution.py:286
  128.5 2.0 %collective-permute-done.13.refs_4_ = bf16[320,640]{1,0:T(8,128)(2,1)S(1)} collective-permute-done((bf16[320,640]{1,0:T(8,128)(2,1)S(1)}, bf16[320,640]{1,0:T(8,128)(2,1)S(1)}, u32[]{:S(2)}, u32[]{:S(2)}) %collective-permute-start.13) | collective-permute-done | bytes 409632 | tf_op jit(solution)/shard_map/sum_quarters/ppermute | solution.py:339
  130.6 4.0 %collective-permute-done.15.refs_5_ = bf16[320,640]{1,0:T(8,128)(2,1)S(1)} collective-permute-done((bf16[320,640]{1,0:T(8,128)(2,1)S(1)}, bf16[320,640]{1,0:T(8,128)(2,1)S(1)}, u32[]{:S(2)}, u32[]{:S(2)}) %collective-permute-start.15) | collective-permute-done | bytes 409632 | tf_op jit(solution)/shard_map/sum_quarters/ppermute | solution.py:336
  134.6 3.0 %collective-permute-done.11.refs_1_ = bf16[320,640]{1,0:T(8,128)(2,1)S(1)} collective-permute-done((bf16[320,640]{1,0:T(8,128)(2,1)S(1)}, bf16[320,640]{1,0:T(8,128)(2,1)S(1)}, u32[]{:S(2)}, u32[]{:S(2)}) %collective-permute-start.11) | collective-permute-done | bytes 409632 | tf_op jit(solution)/shard_map/sum_quarters/ppermute | solution.py:339
  137.6 0.2 sum_halves.1
  137.8 0.3 reshape.30
  138.1 30.1 %all_to_all.15 = bf16[64,5,2,640]{3,2,1,0:T(2,128)(2,1)S(1)} all-to-all(bf16[64,5,2,640]{3,2,1,0:T(2,128)(2,1)S(1)} %reshape.30), channel_id=1, replica_groups=mesh['expert'=64,'etp'=4] {'expert'}, dimensions={0} | all-to-all | bytes 1638400 | tf_op jit(solution)/shard_map/return_tokens/all_to_all | solution.py:362
  168.3 0.3 reshape.31
  168.6 0.8 convolution_convert_fusion.2
  169.4 0.1 fusion.19
  169.5 0.4 collective-permute-start.18
  169.9 1.7 collective-permute-start.17
  171.6 5.0 %collective-permute-done.18.b3 = bf16[128,640]{1,0:T(8,128)(2,1)S(1)} collective-permute-done((bf16[128,640]{1,0:T(8,128)(2,1)S(1)}, bf16[128,640]{1,0:T(8,128)(2,1)S(1)}, u32[]{:S(2)}, u32[]{:S(2)}) %collective-permute-start.18) | collective-permute-done | bytes 163872 | tf_op jit(solution)/shard_map/return_tokens/ppermute | solution.py:339
  176.6 3.2 %collective-permute-done.17.b2 = bf16[128,640]{1,0:T(8,128)(2,1)S(1)} collective-permute-done((bf16[128,640]{1,0:T(8,128)(2,1)S(1)}, bf16[128,640]{1,0:T(8,128)(2,1)S(1)}, u32[]{:S(2)}, u32[]{:S(2)}) %collective-permute-start.17) | collective-permute-done | bytes 163872 | tf_op jit(solution)/shard_map/return_tokens/ppermute | solution.py:339
  179.8 0.9 join_columns.1
  (12 shorter events, 0.1 us)
Async XLA Ops:
  0.0 6.4 %copy-start = (s32[128,1]{0,1:T(1,128)S(1)}, s32[128,1]{0,1:T(1,128)}, u32[]{:S(2)}) copy-start(s32[128,1]{0,1:T(1,128)} %param.8) | copy-start | bytes 1540
  1.2 15.6 %collective-permute-start = (bf16[128,640]{1,0:T(8,128)(2,1)S(1)}, bf16[128,640]{1,0:T(8,128)(2,1)S(1)}, u32[]{:S(2)}, u32[]{:S(2)}) collective-permute-start(bf16[128,640]{1,0:T(8,128)(2,1)S(1)} %get-tuple-element.36), channel_id=1, source_target_pairs={{0,2},{1,3},{2,0},{3,1},{4,6},{5,7},{6,4},{7,5},{8,10},{9,11},{10,... | collective-permute-start | bytes 491528 | tf_op jit(solution)/shard_map/group_exchange/ppermute | solution.py:336
  4.3 12.5 %collective-permute-start.1 = (bf16[128,640]{1,0:T(8,128)(2,1)S(1)}, bf16[128,640]{1,0:T(8,128)(2,1)S(1)}, u32[]{:S(2)}, u32[]{:S(2)}) collective-permute-start(bf16[128,640]{1,0:T(8,128)(2,1)S(1)} %get-tuple-element.37), channel_id=1, source_target_pairs={{0,3},{1,0},{2,1},{3,2},{4,7},{5,4},{6,5},{7,6},{8,11},{9,8},{10,9... | collective-permute-start | bytes 491528 | tf_op jit(solution)/shard_map/group_exchange/ppermute | solution.py:336
  5.5 11.4 %collective-permute-start.2 = (bf16[128,640]{1,0:T(8,128)(2,1)S(1)}, bf16[128,640]{1,0:T(8,128)(2,1)S(1)}, u32[]{:S(2)}, u32[]{:S(2)}) collective-permute-start(bf16[128,640]{1,0:T(8,128)(2,1)S(1)} %get-tuple-element.38), channel_id=1, source_target_pairs={{0,1},{1,2},{2,3},{3,0},{4,5},{5,6},{6,7},{7,4},{8,9},{9,10},{10,1... | collective-permute-start | bytes 491528 | tf_op jit(solution)/shard_map/group_exchange/ppermute | solution.py:336
  17.6 13.3 %copy-start.1 = (s32[128]{0:T(128)S(1)}, s32[128]{0:T(128)}, u32[]{:S(2)}) copy-start(s32[128]{0:T(128)} %param.9) | copy-start | bytes 1540
  18.8 36.0 %all-to-all-start = ((bf16[64,5,2,640]{3,2,1,0:T(2,128)(2,1)}), bf16[64,5,2,640]{3,2,1,0:T(2,128)(2,1)S(1)}, u32[]{:S(2)}, u32[]{:S(2)}) async-start(bf16[64,5,2,640]{3,2,1,0:T(2,128)(2,1)} %reshape.26), calls=%async_computation | async-start | bytes 1638400 | tf_op jit(solution)/shard_map/send_tokens/all_to_all | solution.py:362
  32.5 10.8 %collective-permute-start.3 = (bf16[128,1024]{1,0:T(8,128)(2,1)S(1)}, bf16[128,1024]{1,0:T(8,128)(2,1)S(1)}, u32[]{:S(2)}, u32[]{:S(2)}) collective-permute-start(bf16[128,1024]{1,0:T(8,128)(2,1)S(1)} %get-tuple-element.40), channel_id=1, source_target_pairs={{0,2},{1,3},{2,0},{3,1},{4,6},{5,7},{6,4},{7,5},{8,10},{9,11},{10,... | collective-permute-start | bytes 786440 | tf_op jit(solution)/shard_map/group_exchange/ppermute | solution.py:336
  33.4 12.8 %collective-permute-start.4 = (bf16[128,1024]{1,0:T(8,128)(2,1)S(1)}, bf16[128,1024]{1,0:T(8,128)(2,1)S(1)}, u32[]{:S(2)}, u32[]{:S(2)}) collective-permute-start(bf16[128,1024]{1,0:T(8,128)(2,1)S(1)} %get-tuple-element.41), channel_id=1, source_target_pairs={{0,3},{1,0},{2,1},{3,2},{4,7},{5,4},{6,5},{7,6},{8,11},{9,8},{10,9... | collective-permute-start | bytes 786440 | tf_op jit(solution)/shard_map/group_exchange/ppermute | solution.py:336
  35.0 13.1 %collective-permute-start.5 = (bf16[128,1024]{1,0:T(8,128)(2,1)S(1)}, bf16[128,1024]{1,0:T(8,128)(2,1)S(1)}, u32[]{:S(2)}, u32[]{:S(2)}) collective-permute-start(bf16[128,1024]{1,0:T(8,128)(2,1)S(1)} %get-tuple-element.42), channel_id=1, source_target_pairs={{0,1},{1,2},{2,3},{3,0},{4,5},{5,6},{6,7},{7,4},{8,9},{9,10},{10,1... | collective-permute-start | bytes 786440 | tf_op jit(solution)/shard_map/group_exchange/ppermute | solution.py:336
  55.1 19.4 %collective-permute-start.7 = (bf16[640,640]{1,0:T(8,128)(2,1)S(1)}, bf16[640,640]{1,0:T(8,128)(2,1)S(1)}, u32[]{:S(2)}, u32[]{:S(2)}) collective-permute-start(bf16[640,640]{1,0:T(8,128)(2,1)S(1)} %reshape.29.refs_0_), channel_id=1, source_target_pairs={{0,3},{1,0},{2,1},{3,2},{4,7},{5,4},{6,5},{7,6},{8,11},{9,8},{10,9... | collective-permute-start | bytes 2457608 | tf_op jit(solution)/shard_map/gather_width/ppermute | solution.py:336
  56.0 20.3 %collective-permute-start.6 = (bf16[640,640]{1,0:T(8,128)(2,1)S(1)}, bf16[640,640]{1,0:T(8,128)(2,1)S(1)}, u32[]{:S(2)}, u32[]{:S(2)}) collective-permute-start(bf16[640,640]{1,0:T(8,128)(2,1)S(1)} %reshape.29.refs_0_), channel_id=1, source_target_pairs={{0,1},{1,2},{2,3},{3,0},{4,5},{5,6},{6,7},{7,4},{8,9},{9,10},{10,1... | collective-permute-start | bytes 2457608 | tf_op jit(solution)/shard_map/gather_width/ppermute | solution.py:339
  57.2 40.3 %all-to-all-start.1 = ((bf16[64,5,2,1024]{3,2,1,0:T(2,128)(2,1)}), bf16[64,5,2,1024]{3,2,1,0:T(2,128)(2,1)}, u32[]{:S(2)}, u32[]{:S(2)}) async-start(bf16[64,5,2,1024]{3,2,1,0:T(2,128)(2,1)} %reshape.27), calls=%async_computation.1 | async-start | bytes 2621440 | tf_op jit(solution)/shard_map/send_hidden/all_to_all | solution.py:362
  76.4 9.7 %collective-permute-start.9 = (bf16[320,640]{1,0:T(8,128)(2,1)S(1)}, bf16[320,640]{1,0:T(8,128)(2,1)S(1)}, u32[]{:S(2)}, u32[]{:S(2)}) collective-permute-start(bf16[320,640]{1,0:T(8,128)(2,1)S(1)} %slice.19), channel_id=1, source_target_pairs={{0,3},{1,0},{2,1},{3,2},{4,7},{5,4},{6,5},{7,6},{8,11},{9,8},{10,9... | collective-permute-start | bytes 1228808 | tf_op jit(solution)/shard_map/gather_width/ppermute | solution.py:336
  76.9 10.7 %collective-permute-start.8 = (bf16[320,640]{1,0:T(8,128)(2,1)S(1)}, bf16[320,640]{1,0:T(8,128)(2,1)S(1)}, u32[]{:S(2)}, u32[]{:S(2)}) collective-permute-start(bf16[320,640]{1,0:T(8,128)(2,1)S(1)} %slice.18), channel_id=1, source_target_pairs={{0,1},{1,2},{2,3},{3,0},{4,5},{5,6},{6,7},{7,4},{8,9},{9,10},{10,1... | collective-permute-start | bytes 1228808 | tf_op jit(solution)/shard_map/gather_width/ppermute | solution.py:339
  106.9 13.8 %collective-permute-start.14 = (bf16[320,640]{1,0:T(8,128)(2,1)S(1)}, bf16[320,640]{1,0:T(8,128)(2,1)S(1)}, u32[]{:S(2)}, u32[]{:S(2)}) collective-permute-start(bf16[320,640]{1,0:T(8,128)(2,1)S(1)} %get-tuple-element.64), channel_id=1, source_target_pairs={{0,3},{1,0},{2,1},{3,2},{4,7},{5,4},{6,5},{7,6},{8,11},{9,8},{10,9... | collective-permute-start | bytes 1228808 | tf_op jit(solution)/shard_map/sum_quarters/ppermute | solution.py:336
  109.0 15.1 %collective-permute-start.10 = (bf16[320,640]{1,0:T(8,128)(2,1)S(1)}, bf16[320,640]{1,0:T(8,128)(2,1)S(1)}, u32[]{:S(2)}, u32[]{:S(2)}) collective-permute-start(bf16[320,640]{1,0:T(8,128)(2,1)S(1)} %get-tuple-element.59), channel_id=1, source_target_pairs={{0,1},{1,2},{2,3},{3,0},{4,5},{5,6},{6,7},{7,4},{8,9},{9,10},{10,1... | collective-permute-start | bytes 1228808 | tf_op jit(solution)/shard_map/sum_quarters/ppermute | solution.py:339
  113.2 15.3 %collective-permute-start.12 = (bf16[320,640]{1,0:T(8,128)(2,1)S(1)}, bf16[320,640]{1,0:T(8,128)(2,1)S(1)}, u32[]{:S(2)}, u32[]{:S(2)}) collective-permute-start(bf16[320,640]{1,0:T(8,128)(2,1)S(1)} %get-tuple-element.60), channel_id=1, source_target_pairs={{0,3},{1,0},{2,1},{3,2},{4,7},{5,4},{6,5},{7,6},{8,11},{9,8},{10,9... | collective-permute-start | bytes 1228808 | tf_op jit(solution)/shard_map/sum_quarters/ppermute | solution.py:336
  116.5 14.0 %collective-permute-start.13 = (bf16[320,640]{1,0:T(8,128)(2,1)S(1)}, bf16[320,640]{1,0:T(8,128)(2,1)S(1)}, u32[]{:S(2)}, u32[]{:S(2)}) collective-permute-start(bf16[320,640]{1,0:T(8,128)(2,1)S(1)} %get-tuple-element.62), channel_id=1, source_target_pairs={{0,1},{1,2},{2,3},{3,0},{4,5},{5,6},{6,7},{7,4},{8,9},{9,10},{10,1... | collective-permute-start | bytes 1228808 | tf_op jit(solution)/shard_map/sum_quarters/ppermute | solution.py:339
  120.8 13.8 %collective-permute-start.15 = (bf16[320,640]{1,0:T(8,128)(2,1)S(1)}, bf16[320,640]{1,0:T(8,128)(2,1)S(1)}, u32[]{:S(2)}, u32[]{:S(2)}) collective-permute-start(bf16[320,640]{1,0:T(8,128)(2,1)S(1)} %add_convert_fusion), channel_id=1, source_target_pairs={{0,3},{1,0},{2,1},{3,2},{4,7},{5,4},{6,5},{7,6},{8,11},{9,8},{10,9... | collective-permute-start | bytes 1228808 | tf_op jit(solution)/shard_map/sum_quarters/ppermute | solution.py:336
  124.2 13.3 %collective-permute-start.11 = (bf16[320,640]{1,0:T(8,128)(2,1)S(1)}, bf16[320,640]{1,0:T(8,128)(2,1)S(1)}, u32[]{:S(2)}, u32[]{:S(2)}) collective-permute-start(bf16[320,640]{1,0:T(8,128)(2,1)S(1)} %add_convert_fusion.1), channel_id=1, source_target_pairs={{0,1},{1,2},{2,3},{3,0},{4,5},{5,6},{6,7},{7,4},{8,9},{9,10},{10,1... | collective-permute-start | bytes 1228808 | tf_op jit(solution)/shard_map/sum_quarters/ppermute | solution.py:339
  169.5 7.1 %collective-permute-start.18 = (bf16[128,640]{1,0:T(8,128)(2,1)S(1)}, bf16[128,640]{1,0:T(8,128)(2,1)S(1)}, u32[]{:S(2)}, u32[]{:S(2)}) collective-permute-start(bf16[128,640]{1,0:T(8,128)(2,1)S(1)} %get-tuple-element.65), channel_id=1, source_target_pairs={{0,3},{1,0},{2,1},{3,2},{4,7},{5,4},{6,5},{7,6},{8,11},{9,8},{10,9... | collective-permute-start | bytes 491528 | tf_op jit(solution)/shard_map/return_tokens/ppermute | solution.py:339
  169.9 9.9 %collective-permute-start.17 = (bf16[128,640]{1,0:T(8,128)(2,1)S(1)}, bf16[128,640]{1,0:T(8,128)(2,1)S(1)}, u32[]{:S(2)}, u32[]{:S(2)}) collective-permute-start(bf16[128,640]{1,0:T(8,128)(2,1)S(1)} %get-tuple-element.66), channel_id=1, source_target_pairs={{0,1},{1,2},{2,3},{3,0},{4,5},{5,6},{6,7},{7,4},{8,9},{9,10},{10,1... | collective-permute-start | bytes 491528 | tf_op jit(solution)/shard_map/return_tokens/ppermute | solution.py:339
  171.6 8.2 %collective-permute-start.16 = (bf16[128,640]{1,0:T(8,128)(2,1)S(1)}, bf16[128,640]{1,0:T(8,128)(2,1)S(1)}, u32[]{:S(2)}, u32[]{:S(2)}) collective-permute-start(bf16[128,640]{1,0:T(8,128)(2,1)S(1)} %get-tuple-element.67), channel_id=1, source_target_pairs={{0,2},{1,3},{2,0},{3,1},{4,6},{5,7},{6,4},{7,5},{8,10},{9,11},{10,... | collective-permute-start | bytes 491528 | tf_op jit(solution)/shard_map/return_tokens/ppermute | solution.py:339

commit v6 on v5

--- a/solution.py
+++ b/solution.py
@@ -363,7 +363,7 @@
 
     with jax.named_scope("send_tokens"):
         packed_tokens = pick(group_tokens).reshape(experts, capacity // 2, 2, quarter)
-        packed_hidden = pick(group_hidden).reshape(experts, capacity // 2, 2, hidden)
+        packed_hidden = pick(group_hidden).reshape(experts, capacity * hidden // 128, 128)
         arrived, packed_hidden = lax.optimization_barrier((to_experts(packed_tokens), packed_hidden))
         own_block = arrived.reshape(slots, quarter)
     with jax.named_scope("send_hidden"):
@@ -371,7 +371,7 @@
 
     half = slots // 2
     with jax.named_scope("gather_width"):
-        own_sums = up_sums((own_block,), (0,), gate_w, up_w, x)
+        own_sums = up_sums((in_hbm(own_block),), (0,), gate_w, up_w, x)
         left_block, right_block, *own_sums = lax.optimization_barrier(
             (forward(own_block, 1), back(own_block, 1), *own_sums)
         )

time: 181 us -> 179 us (0.989)
    reshape x1, local copies, waits for them, and re-layouts: 3.2 us -> 0.58 us  [on_device(): scaled = to_experts(packed_hidden).reshape(slots, hidden)]
  transfers between devices with their start and end apart: 21 -> 21, of which waited for: 14 -> 14; matrix products, arithmetic and copies ran while one was open for 1% -> 1% of each run, Pallas kernels for 17% -> 18%
where the time goes in v6:
time: 179 us
  waiting for transfers between devices  48.4 us (27%)
  starting transfers between devices  41.3 us (23%)
  Pallas kernels  40.6 us (23%)
  blocking collectives  40.4 us (23%)
  local copies, waits for them, and re-layouts  5.31 us (3%)
  matrix products  2.37 us (1%)
    all_to_all x1, blocking collectives, to_experts(): lax.all_to_all(array, 'expert', split_axis=0, concat_axis=0, tiled=True)  30.1 us
    ppermute x11, waiting for transfers between devices, back(): return lax.ppermute(array, 'etp', [(i, (i - r) % etp) for i in range(etp)])  24.1 us
    ppermute x11, starting transfers between devices, back(): return lax.ppermute(array, 'etp', [(i, (i - r) % etp) for i in range(etp)])  18.2 us
    all_to_all x2, starting transfers between devices, to_experts(): lax.all_to_all(array, 'expert', split_axis=0, concat_axis=0, tiled=True)  17.9 us
    ppermute x8, waiting for transfers between devices, forward(): return lax.ppermute(array, 'etp', [(i, (i + r) % etp) for i in range(etp)])  16.2 us
    pallas_call x3, Pallas kernels, down_halves(): pl.pallas_call(kernel, grid_spec=pltpu.PrefetchScalarGridSpec(num_scalar_...  12.7 us
    pallas_call x2, Pallas kernels, up_sums(): pl.pallas_call(kernel, grid_spec=pltpu.PrefetchScalarGridSpec(num_scalar_...  11.5 us
    all_gather x1, blocking collectives, on_device(): lax.all_gather(routes.reshape(1, own_rows), 'etp', axis=0, tiled=True)  10.2 us
  transfers between devices with their start and end apart: 21, of which 14 were waited for; matrix products, arithmetic and copies ran while one was open for 1% of the time, Pallas kernels for 18%

profile of v6, /device:TPU:8, one launch (start us, length us, event | category | flops | bytes accessed | tf_op | source)
XLA Modules:
  0.0 178.8 jit_solution(4508751899813751219)
XLA Ops:
  0.0 1.2 split_columns.2
  1.2 3.1 %collective-permute-start = (bf16[128,640]{1,0:T(8,128)(2,1)S(1)}, bf16[128,640]{1,0:T(8,128)(2,1)S(1)}, u32[]{:S(2)}, u32[]{:S(2)}) collective-permute-start(bf16[128,640]{1,0:T(8,128)(2,1)S(1)} %get-tuple-element.36), channel_id=1, source_target_pairs={{0,2},{1,3},{2,0},{3,1},{4,6},{5,7},{6,4},{7,5},{8,10},{9,11},{10,... | collective-permute-start | bytes 491528 | tf_op jit(solution)/shard_map/group_exchange/ppermute | solution.py:336
  4.3 1.1 collective-permute-start.1
  5.5 0.9 collective-permute-start.2
  6.4 10.2 %all-gather = s32[512,1]{0,1:T(1,128)S(1)} all-gather(s32[128,1]{0,1:T(1,128)S(1)} %copy-done), channel_id=2, replica_groups=mesh['expert'=64,'etp'=4] {'etp'}, dimensions={0}, use_global_device_ids=true | all-gather | bytes 2560 | tf_op jit(solution)/shard_map/group_exchange/all_gather | solution.py:347
  16.6 0.2 slot_index.1
  16.9 0.0 collective-permute-done.2
  16.9 0.7 convolution_convert_fusion.1
  17.6 0.0 copy-start.1
  17.6 1.2 reshape.26
  18.8 12.1 %all-to-all-start = ((bf16[64,5,2,640]{3,2,1,0:T(2,128)(2,1)}), bf16[64,5,2,640]{3,2,1,0:T(2,128)(2,1)S(1)}, u32[]{:S(2)}, u32[]{:S(2)}) async-start(bf16[64,5,2,640]{3,2,1,0:T(2,128)(2,1)} %reshape.26), calls=%async_computation | async-start | bytes 1638400 | tf_op jit(solution)/shard_map/send_tokens/all_to_all | solution.py:362
  30.9 0.1 copy.7.refs_4_
  31.1 1.4 split_columns.3
  32.5 0.9 collective-permute-start.3
  33.4 1.6 collective-permute-start.4
  35.0 0.5 collective-permute-start.5
  35.5 7.8 %collective-permute-done.3 = bf16[128,1024]{1,0:T(8,128)(2,1)S(1)} collective-permute-done((bf16[128,1024]{1,0:T(8,128)(2,1)S(1)}, bf16[128,1024]{1,0:T(8,128)(2,1)S(1)}, u32[]{:S(2)}, u32[]{:S(2)}) %collective-permute-start.3) | collective-permute-done | bytes 262176 | tf_op jit(solution)/shard_map/group_exchange/ppermute | solution.py:336
  43.3 3.0 %collective-permute-done.4 = bf16[128,1024]{1,0:T(8,128)(2,1)S(1)} collective-permute-done((bf16[128,1024]{1,0:T(8,128)(2,1)S(1)}, bf16[128,1024]{1,0:T(8,128)(2,1)S(1)}, u32[]{:S(2)}, u32[]{:S(2)}) %collective-permute-start.4) | collective-permute-done | bytes 262176 | tf_op jit(solution)/shard_map/group_exchange/ppermute | solution.py:336
  46.3 1.8 %collective-permute-done.5 = bf16[128,1024]{1,0:T(8,128)(2,1)S(1)} collective-permute-done((bf16[128,1024]{1,0:T(8,128)(2,1)S(1)}, bf16[128,1024]{1,0:T(8,128)(2,1)S(1)}, u32[]{:S(2)}, u32[]{:S(2)}) %collective-permute-start.5) | collective-permute-done | bytes 262176 | tf_op jit(solution)/shard_map/group_exchange/ppermute | solution.py:336
  48.1 0.8 convolution_convert_fusion
  48.9 1.4 reshape.27
  50.3 4.5 %all-to-all-done = bf16[64,5,2,640]{3,2,1,0:T(2,128)(2,1)S(1)} async-done(((bf16[64,5,2,640]{3,2,1,0:T(2,128)(2,1)}), bf16[64,5,2,640]{3,2,1,0:T(2,128)(2,1)S(1)}, u32[]{:S(2)}, u32[]{:S(2)}) %all-to-all-start) | async-done | bytes 819232 | tf_op jit(solution)/shard_map/send_tokens/all_to_all | solution.py:362
  54.8 1.2 reshape.29.refs_0_
  56.0 0.8 collective-permute-start.7
  56.8 1.2 collective-permute-start.6
  58.0 5.8 %all-to-all-start.1 = ((bf16[64,80,128]{2,1,0:T(8,128)(2,1)}), bf16[64,80,128]{2,1,0:T(8,128)(2,1)S(1)}, u32[]{:S(2)}, u32[]{:S(2)}) async-start(bf16[64,80,128]{2,1,0:T(8,128)(2,1)} %reshape.27), calls=%async_computation.1 | async-start | bytes 2621440 | tf_op jit(solution)/shard_map/send_hidden/all_to_all | solution.py:362
  63.9 4.3 %up_sums.2 = (f32[640,1024]{1,0:T(8,128)S(1)}, f32[640,1024]{1,0:T(8,128)S(1)}) custom-call(s32[1]{0:T(128)} %bitcast.x_ref, bf16[640,640]{1,0:T(8,128)(2,1)} %reshape.29.refs_0_, bf16[2560,1024]{1,0:T(8,128)(2,1)} %bitcast.12, bf16[2560,1024]{1,0:T(8,128)(2,1)} %bitcast.20), custom_call_target="tpu_custom_call" | custom-call | flops 10066329600 | bytes 13107200 | tf_op jit(solution)/shard_map/gather_width/up_sums/pallas_call | solution.py:153
  68.2 7.3 %collective-permute-done.7.refs_0_ = bf16[640,640]{1,0:T(8,128)(2,1)S(1)} collective-permute-done((bf16[640,640]{1,0:T(8,128)(2,1)}, bf16[640,640]{1,0:T(8,128)(2,1)S(1)}, u32[]{:S(2)}, u32[]{:S(2)}) %collective-permute-start.7) | collective-permute-done | bytes 819232 | tf_op jit(solution)/shard_map/gather_width/ppermute | solution.py:336
  75.5 1.8 collective-permute-done.6.refs_1_
  77.4 0.5 collective-permute-start.9
  77.9 1.7 collective-permute-start.8
  79.7 7.2 %up_sums.3 = (f32[640,1024]{1,0:T(8,128)}, f32[640,1024]{1,0:T(8,128)}) custom-call(s32[1]{0:T(128)} %bitcast.x_ref, bf16[640,640]{1,0:T(8,128)(2,1)S(1)} %collective-permute-done.7.refs_0_, bf16[640,640]{1,0:T(8,128)(2,1)S(1)} %collective-permute-done.6.refs_1_, bf16[2560,1024]{1,0:T(8,128)(2,1)} %bitcast.13, bf16[2560,1024]{1,0:T(8,128)(2,1)} %bitcast.14, ...), custom_call_target="tpu_custom_call" | custom-call | flops 20132659200 | bytes 15728640 | tf_op jit(solution)/shard_map/pre_activations/up_sums/pallas_call | solution.py:153
  86.9 0.1 collective-permute-done.9.bottom
  87.0 1.5 collective-permute-done.8.top
  88.5 6.2 %up_last.1 = (f32[640,1024]{1,0:T(8,128)}, f32[640,1024]{1,0:T(8,128)}) custom-call(s32[1]{0:T(128)} %bitcast.x_ref, bf16[320,640]{1,0:T(8,128)(2,1)S(1)} %collective-permute-done.8.top, bf16[320,640]{1,0:T(8,128)(2,1)S(1)} %collective-permute-done.9.bottom, f32[640,1024]{1,0:T(8,128)} %get-tuple-element.51.g_in, f32[640,1024]{1,0:T(8,128)} %get-tuple-element.52.u_in, ...), custom_call_target="tpu_custom_call" | custom-call | flops 1677721600 | bytes 13107200 | tf_op jit(solution)/shard_map/pre_activations/up_last/pallas_call | solution.py:196
  94.7 3.6 %all-to-all-done.1 = bf16[64,80,128]{2,1,0:T(8,128)(2,1)S(1)} async-done(((bf16[64,80,128]{2,1,0:T(8,128)(2,1)}), bf16[64,80,128]{2,1,0:T(8,128)(2,1)S(1)}, u32[]{:S(2)}, u32[]{:S(2)}) %all-to-all-start.1) | async-done | bytes 1310752 | tf_op jit(solution)/shard_map/send_hidden/all_to_all | solution.py:362
  98.3 0.6 reshape.28.h
  98.9 6.1 %down_first.1 = (bf16[640,1024]{1,0:T(8,128)(2,1)S(1)}, bf16[640,1024]{1,0:T(8,128)(2,1)S(1)}, bf16[320,640]{1,0:T(8,128)(2,1)S(1)}, bf16[320,640]{1,0:T(8,128)(2,1)S(1)}) custom-call(s32[1]{0:T(128)} %bitcast.x_ref, bf16[640,1024]{1,0:T(8,128)(2,1)S(1)} %reshape.28.h, f32[640,1024]{1,0:T(8,128)} %get-tuple-element.53.a, f32[640,1024]{1,0:T(8,128)} %get-tuple-element.54.b, ...), custom_call_target="tpu_custom_call" | custom-call | flops 1677721600 | bytes 11796480 | tf_op jit(solution)/shard_map/input_partials/down_first/pallas_call | solution.py:245
  105.0 2.1 %collective-permute-start.14 = (bf16[320,640]{1,0:T(8,128)(2,1)S(1)}, bf16[320,640]{1,0:T(8,128)(2,1)S(1)}, u32[]{:S(2)}, u32[]{:S(2)}) collective-permute-start(bf16[320,640]{1,0:T(8,128)(2,1)S(1)} %get-tuple-element.64), channel_id=1, source_target_pairs={{0,3},{1,0},{2,1},{3,2},{4,7},{5,4},{6,5},{7,6},{8,11},{9,8},{10,9... | collective-permute-start | bytes 1228808 | tf_op jit(solution)/shard_map/sum_quarters/ppermute | solution.py:336
  107.2 0.0 collective-permute-start.10
  107.2 4.2 %down_halves.5 = (bf16[320,640]{1,0:T(8,128)(2,1)S(1)}, bf16[320,640]{1,0:T(8,128)(2,1)S(1)}) custom-call(s32[1]{0:T(128)} %bitcast.x_ref, bf16[640,1024]{1,0:T(8,128)(2,1)S(1)} %get-tuple-element.55.gg, bf16[640,1024]{1,0:T(8,128)(2,1)S(1)} %get-tuple-element.56.gu, bf16[2560,1024]{1,0:T(8,128)(2,1)} %bitcast.17, bf16[2560,1024]{1,0:T(8,128)(2,1)} %bitcast.25), custom_call_target="tpu_custom_call" | custom-call | flops 419430400 | bytes 7864320 | tf_op jit(solution)/shard_map/input_partials/down_halves/pallas_call | solution.py:286
  111.4 3.3 %collective-permute-start.12 = (bf16[320,640]{1,0:T(8,128)(2,1)S(1)}, bf16[320,640]{1,0:T(8,128)(2,1)S(1)}, u32[]{:S(2)}, u32[]{:S(2)}) collective-permute-start(bf16[320,640]{1,0:T(8,128)(2,1)S(1)} %get-tuple-element.60), channel_id=1, source_target_pairs={{0,3},{1,0},{2,1},{3,2},{4,7},{5,4},{6,5},{7,6},{8,11},{9,8},{10,9... | collective-permute-start | bytes 1228808 | tf_op jit(solution)/shard_map/sum_quarters/ppermute | solution.py:336
  114.7 0.0 collective-permute-start.13
  114.7 4.2 %down_halves.4 = (f32[320,640]{1,0:T(8,128)S(1)}, f32[320,640]{1,0:T(8,128)S(1)}) custom-call(s32[1]{0:T(128)} %bitcast.x_ref, bf16[640,1024]{1,0:T(8,128)(2,1)S(1)} %get-tuple-element.55.gg, bf16[640,1024]{1,0:T(8,128)(2,1)S(1)} %get-tuple-element.56.gu, bf16[2560,1024]{1,0:T(8,128)(2,1)} %bitcast.18, bf16[2560,1024]{1,0:T(8,128)(2,1)} %bitcast.26), custom_call_target="tpu_custom_call" | custom-call | flops 419430400 | bytes 7864320 | tf_op jit(solution)/shard_map/input_partials/down_halves/pallas_call | solution.py:286
  119.0 0.0 collective-permute-done.14
  119.0 0.1 add_convert_fusion
  119.1 3.3 %collective-permute-start.15 = (bf16[320,640]{1,0:T(8,128)(2,1)S(1)}, bf16[320,640]{1,0:T(8,128)(2,1)S(1)}, u32[]{:S(2)}, u32[]{:S(2)}) collective-permute-start(bf16[320,640]{1,0:T(8,128)(2,1)S(1)} %add_convert_fusion), channel_id=1, source_target_pairs={{0,3},{1,0},{2,1},{3,2},{4,7},{5,4},{6,5},{7,6},{8,11},{9,8},{10,9... | collective-permute-start | bytes 1228808 | tf_op jit(solution)/shard_map/sum_quarters/ppermute | solution.py:336
  122.4 0.1 add_convert_fusion.1
  122.5 0.1 collective-permute-start.11
  122.6 4.2 %down_halves.3 = (f32[320,640]{1,0:T(8,128)S(1)}, f32[320,640]{1,0:T(8,128)S(1)}) custom-call(s32[1]{0:T(128)} %bitcast.x_ref, bf16[640,1024]{1,0:T(8,128)(2,1)S(1)} %get-tuple-element.55.gg, bf16[640,1024]{1,0:T(8,128)(2,1)S(1)} %get-tuple-element.56.gu, bf16[2560,1024]{1,0:T(8,128)(2,1)} %bitcast.19, bf16[2560,1024]{1,0:T(8,128)(2,1)} %bitcast.27), custom_call_target="tpu_custom_call" | custom-call | flops 419430400 | bytes 7864320 | tf_op jit(solution)/shard_map/input_partials/down_halves/pallas_call | solution.py:286
  126.8 1.8 %collective-permute-done.13.refs_4_ = bf16[320,640]{1,0:T(8,128)(2,1)S(1)} collective-permute-done((bf16[320,640]{1,0:T(8,128)(2,1)S(1)}, bf16[320,640]{1,0:T(8,128)(2,1)S(1)}, u32[]{:S(2)}, u32[]{:S(2)}) %collective-permute-start.13) | collective-permute-done | bytes 409632 | tf_op jit(solution)/shard_map/sum_quarters/ppermute | solution.py:339
  128.7 4.1 %collective-permute-done.15.refs_5_ = bf16[320,640]{1,0:T(8,128)(2,1)S(1)} collective-permute-done((bf16[320,640]{1,0:T(8,128)(2,1)S(1)}, bf16[320,640]{1,0:T(8,128)(2,1)S(1)}, u32[]{:S(2)}, u32[]{:S(2)}) %collective-permute-start.15) | collective-permute-done | bytes 409632 | tf_op jit(solution)/shard_map/sum_quarters/ppermute | solution.py:336
  132.7 3.0 %collective-permute-done.11.refs_1_ = bf16[320,640]{1,0:T(8,128)(2,1)S(1)} collective-permute-done((bf16[320,640]{1,0:T(8,128)(2,1)S(1)}, bf16[320,640]{1,0:T(8,128)(2,1)S(1)}, u32[]{:S(2)}, u32[]{:S(2)}) %collective-permute-start.11) | collective-permute-done | bytes 409632 | tf_op jit(solution)/shard_map/sum_quarters/ppermute | solution.py:339
  135.7 0.3 sum_halves.1
  136.0 0.3 reshape.30
  136.3 30.1 %all_to_all.15 = bf16[64,5,2,640]{3,2,1,0:T(2,128)(2,1)S(1)} all-to-all(bf16[64,5,2,640]{3,2,1,0:T(2,128)(2,1)S(1)} %reshape.30), channel_id=1, replica_groups=mesh['expert'=64,'etp'=4] {'expert'}, dimensions={0} | all-to-all | bytes 1638400 | tf_op jit(solution)/shard_map/return_tokens/all_to_all | solution.py:362
  166.5 0.3 reshape.31
  166.8 0.8 convolution_convert_fusion.2
  167.6 0.1 fusion.19
  167.7 0.4 collective-permute-start.18
  168.0 1.7 collective-permute-start.17
  169.8 5.0 %collective-permute-done.18.b3 = bf16[128,640]{1,0:T(8,128)(2,1)S(1)} collective-permute-done((bf16[128,640]{1,0:T(8,128)(2,1)S(1)}, bf16[128,640]{1,0:T(8,128)(2,1)S(1)}, u32[]{:S(2)}, u32[]{:S(2)}) %collective-permute-start.18) | collective-permute-done | bytes 163872 | tf_op jit(solution)/shard_map/return_tokens/ppermute | solution.py:339
  174.8 3.2 %collective-permute-done.17.b2 = bf16[128,640]{1,0:T(8,128)(2,1)S(1)} collective-permute-done((bf16[128,640]{1,0:T(8,128)(2,1)S(1)}, bf16[128,640]{1,0:T(8,128)(2,1)S(1)}, u32[]{:S(2)}, u32[]{:S(2)}) %collective-permute-start.17) | collective-permute-done | bytes 163872 | tf_op jit(solution)/shard_map/return_tokens/ppermute | solution.py:339
  177.9 0.9 join_columns.1
  (12 shorter events, 0.1 us)
Async XLA Ops:
  0.0 6.4 %copy-start = (s32[128,1]{0,1:T(1,128)S(1)}, s32[128,1]{0,1:T(1,128)}, u32[]{:S(2)}) copy-start(s32[128,1]{0,1:T(1,128)} %param.8) | copy-start | bytes 1540
  1.2 15.6 %collective-permute-start = (bf16[128,640]{1,0:T(8,128)(2,1)S(1)}, bf16[128,640]{1,0:T(8,128)(2,1)S(1)}, u32[]{:S(2)}, u32[]{:S(2)}) collective-permute-start(bf16[128,640]{1,0:T(8,128)(2,1)S(1)} %get-tuple-element.36), channel_id=1, source_target_pairs={{0,2},{1,3},{2,0},{3,1},{4,6},{5,7},{6,4},{7,5},{8,10},{9,11},{10,... | collective-permute-start | bytes 491528 | tf_op jit(solution)/shard_map/group_exchange/ppermute | solution.py:336
  4.3 12.5 %collective-permute-start.1 = (bf16[128,640]{1,0:T(8,128)(2,1)S(1)}, bf16[128,640]{1,0:T(8,128)(2,1)S(1)}, u32[]{:S(2)}, u32[]{:S(2)}) collective-permute-start(bf16[128,640]{1,0:T(8,128)(2,1)S(1)} %get-tuple-element.37), channel_id=1, source_target_pairs={{0,3},{1,0},{2,1},{3,2},{4,7},{5,4},{6,5},{7,6},{8,11},{9,8},{10,9... | collective-permute-start | bytes 491528 | tf_op jit(solution)/shard_map/group_exchange/ppermute | solution.py:336
  5.5 11.4 %collective-permute-start.2 = (bf16[128,640]{1,0:T(8,128)(2,1)S(1)}, bf16[128,640]{1,0:T(8,128)(2,1)S(1)}, u32[]{:S(2)}, u32[]{:S(2)}) collective-permute-start(bf16[128,640]{1,0:T(8,128)(2,1)S(1)} %get-tuple-element.38), channel_id=1, source_target_pairs={{0,1},{1,2},{2,3},{3,0},{4,5},{5,6},{6,7},{7,4},{8,9},{9,10},{10,1... | collective-permute-start | bytes 491528 | tf_op jit(solution)/shard_map/group_exchange/ppermute | solution.py:336
  17.6 13.3 %copy-start.1 = (s32[128]{0:T(128)S(1)}, s32[128]{0:T(128)}, u32[]{:S(2)}) copy-start(s32[128]{0:T(128)} %param.9) | copy-start | bytes 1540
  18.8 36.0 %all-to-all-start = ((bf16[64,5,2,640]{3,2,1,0:T(2,128)(2,1)}), bf16[64,5,2,640]{3,2,1,0:T(2,128)(2,1)S(1)}, u32[]{:S(2)}, u32[]{:S(2)}) async-start(bf16[64,5,2,640]{3,2,1,0:T(2,128)(2,1)} %reshape.26), calls=%async_computation | async-start | bytes 1638400 | tf_op jit(solution)/shard_map/send_tokens/all_to_all | solution.py:362
  32.5 10.8 %collective-permute-start.3 = (bf16[128,1024]{1,0:T(8,128)(2,1)S(1)}, bf16[128,1024]{1,0:T(8,128)(2,1)S(1)}, u32[]{:S(2)}, u32[]{:S(2)}) collective-permute-start(bf16[128,1024]{1,0:T(8,128)(2,1)S(1)} %get-tuple-element.40), channel_id=1, source_target_pairs={{0,2},{1,3},{2,0},{3,1},{4,6},{5,7},{6,4},{7,5},{8,10},{9,11},{10,... | collective-permute-start | bytes 786440 | tf_op jit(solution)/shard_map/group_exchange/ppermute | solution.py:336
  33.4 12.8 %collective-permute-start.4 = (bf16[128,1024]{1,0:T(8,128)(2,1)S(1)}, bf16[128,1024]{1,0:T(8,128)(2,1)S(1)}, u32[]{:S(2)}, u32[]{:S(2)}) collective-permute-start(bf16[128,1024]{1,0:T(8,128)(2,1)S(1)} %get-tuple-element.41), channel_id=1, source_target_pairs={{0,3},{1,0},{2,1},{3,2},{4,7},{5,4},{6,5},{7,6},{8,11},{9,8},{10,9... | collective-permute-start | bytes 786440 | tf_op jit(solution)/shard_map/group_exchange/ppermute | solution.py:336
  35.0 13.1 %collective-permute-start.5 = (bf16[128,1024]{1,0:T(8,128)(2,1)S(1)}, bf16[128,1024]{1,0:T(8,128)(2,1)S(1)}, u32[]{:S(2)}, u32[]{:S(2)}) collective-permute-start(bf16[128,1024]{1,0:T(8,128)(2,1)S(1)} %get-tuple-element.42), channel_id=1, source_target_pairs={{0,1},{1,2},{2,3},{3,0},{4,5},{5,6},{6,7},{7,4},{8,9},{9,10},{10,1... | collective-permute-start | bytes 786440 | tf_op jit(solution)/shard_map/group_exchange/ppermute | solution.py:336
  56.0 19.5 %collective-permute-start.7 = (bf16[640,640]{1,0:T(8,128)(2,1)}, bf16[640,640]{1,0:T(8,128)(2,1)S(1)}, u32[]{:S(2)}, u32[]{:S(2)}) collective-permute-start(bf16[640,640]{1,0:T(8,128)(2,1)} %reshape.29.refs_0_), channel_id=1, source_target_pairs={{0,3},{1,0},{2,1},{3,2},{4,7},{5,4},{6,5},{7,6},{8,11},{9,8},{10,9... | collective-permute-start | bytes 2457608 | tf_op jit(solution)/shard_map/gather_width/ppermute | solution.py:336
  56.8 20.5 %collective-permute-start.6 = (bf16[640,640]{1,0:T(8,128)(2,1)}, bf16[640,640]{1,0:T(8,128)(2,1)S(1)}, u32[]{:S(2)}, u32[]{:S(2)}) collective-permute-start(bf16[640,640]{1,0:T(8,128)(2,1)} %reshape.29.refs_0_), channel_id=1, source_target_pairs={{0,1},{1,2},{2,3},{3,0},{4,5},{5,6},{6,7},{7,4},{8,9},{9,10},{10,1... | collective-permute-start | bytes 2457608 | tf_op jit(solution)/shard_map/gather_width/ppermute | solution.py:339
  58.0 40.3 %all-to-all-start.1 = ((bf16[64,80,128]{2,1,0:T(8,128)(2,1)}), bf16[64,80,128]{2,1,0:T(8,128)(2,1)S(1)}, u32[]{:S(2)}, u32[]{:S(2)}) async-start(bf16[64,80,128]{2,1,0:T(8,128)(2,1)} %reshape.27), calls=%async_computation.1 | async-start | bytes 2621440 | tf_op jit(solution)/shard_map/send_hidden/all_to_all | solution.py:362
  77.4 9.6 %collective-permute-start.9 = (bf16[320,640]{1,0:T(8,128)(2,1)S(1)}, bf16[320,640]{1,0:T(8,128)(2,1)S(1)}, u32[]{:S(2)}, u32[]{:S(2)}) collective-permute-start(bf16[320,640]{1,0:T(8,128)(2,1)S(1)} %slice.19), channel_id=1, source_target_pairs={{0,3},{1,0},{2,1},{3,2},{4,7},{5,4},{6,5},{7,6},{8,11},{9,8},{10,9... | collective-permute-start | bytes 1228808 | tf_op jit(solution)/shard_map/gather_width/ppermute | solution.py:336
  77.9 10.6 %collective-permute-start.8 = (bf16[320,640]{1,0:T(8,128)(2,1)S(1)}, bf16[320,640]{1,0:T(8,128)(2,1)S(1)}, u32[]{:S(2)}, u32[]{:S(2)}) collective-permute-start(bf16[320,640]{1,0:T(8,128)(2,1)S(1)} %slice.18), channel_id=1, source_target_pairs={{0,1},{1,2},{2,3},{3,0},{4,5},{5,6},{6,7},{7,4},{8,9},{9,10},{10,1... | collective-permute-start | bytes 1228808 | tf_op jit(solution)/shard_map/gather_width/ppermute | solution.py:339
  105.0 13.9 %collective-permute-start.14 = (bf16[320,640]{1,0:T(8,128)(2,1)S(1)}, bf16[320,640]{1,0:T(8,128)(2,1)S(1)}, u32[]{:S(2)}, u32[]{:S(2)}) collective-permute-start(bf16[320,640]{1,0:T(8,128)(2,1)S(1)} %get-tuple-element.64), channel_id=1, source_target_pairs={{0,3},{1,0},{2,1},{3,2},{4,7},{5,4},{6,5},{7,6},{8,11},{9,8},{10,9... | collective-permute-start | bytes 1228808 | tf_op jit(solution)/shard_map/sum_quarters/ppermute | solution.py:336
  107.2 15.2 %collective-permute-start.10 = (bf16[320,640]{1,0:T(8,128)(2,1)S(1)}, bf16[320,640]{1,0:T(8,128)(2,1)S(1)}, u32[]{:S(2)}, u32[]{:S(2)}) collective-permute-start(bf16[320,640]{1,0:T(8,128)(2,1)S(1)} %get-tuple-element.59), channel_id=1, source_target_pairs={{0,1},{1,2},{2,3},{3,0},{4,5},{5,6},{6,7},{7,4},{8,9},{9,10},{10,1... | collective-permute-start | bytes 1228808 | tf_op jit(solution)/shard_map/sum_quarters/ppermute | solution.py:339
  111.4 15.4 %collective-permute-start.12 = (bf16[320,640]{1,0:T(8,128)(2,1)S(1)}, bf16[320,640]{1,0:T(8,128)(2,1)S(1)}, u32[]{:S(2)}, u32[]{:S(2)}) collective-permute-start(bf16[320,640]{1,0:T(8,128)(2,1)S(1)} %get-tuple-element.60), channel_id=1, source_target_pairs={{0,3},{1,0},{2,1},{3,2},{4,7},{5,4},{6,5},{7,6},{8,11},{9,8},{10,9... | collective-permute-start | bytes 1228808 | tf_op jit(solution)/shard_map/sum_quarters/ppermute | solution.py:336
  114.7 13.9 %collective-permute-start.13 = (bf16[320,640]{1,0:T(8,128)(2,1)S(1)}, bf16[320,640]{1,0:T(8,128)(2,1)S(1)}, u32[]{:S(2)}, u32[]{:S(2)}) collective-permute-start(bf16[320,640]{1,0:T(8,128)(2,1)S(1)} %get-tuple-element.62), channel_id=1, source_target_pairs={{0,1},{1,2},{2,3},{3,0},{4,5},{5,6},{6,7},{7,4},{8,9},{9,10},{10,1... | collective-permute-start | bytes 1228808 | tf_op jit(solution)/shard_map/sum_quarters/ppermute | solution.py:339
  119.1 13.7 %collective-permute-start.15 = (bf16[320,640]{1,0:T(8,128)(2,1)S(1)}, bf16[320,640]{1,0:T(8,128)(2,1)S(1)}, u32[]{:S(2)}, u32[]{:S(2)}) collective-permute-start(bf16[320,640]{1,0:T(8,128)(2,1)S(1)} %add_convert_fusion), channel_id=1, source_target_pairs={{0,3},{1,0},{2,1},{3,2},{4,7},{5,4},{6,5},{7,6},{8,11},{9,8},{10,9... | collective-permute-start | bytes 1228808 | tf_op jit(solution)/shard_map/sum_quarters/ppermute | solution.py:336
  122.5 13.2 %collective-permute-start.11 = (bf16[320,640]{1,0:T(8,128)(2,1)S(1)}, bf16[320,640]{1,0:T(8,128)(2,1)S(1)}, u32[]{:S(2)}, u32[]{:S(2)}) collective-permute-start(bf16[320,640]{1,0:T(8,128)(2,1)S(1)} %add_convert_fusion.1), channel_id=1, source_target_pairs={{0,1},{1,2},{2,3},{3,0},{4,5},{5,6},{6,7},{7,4},{8,9},{9,10},{10,1... | collective-permute-start | bytes 1228808 | tf_op jit(solution)/shard_map/sum_quarters/ppermute | solution.py:339
  167.7 7.1 %collective-permute-start.18 = (bf16[128,640]{1,0:T(8,128)(2,1)S(1)}, bf16[128,640]{1,0:T(8,128)(2,1)S(1)}, u32[]{:S(2)}, u32[]{:S(2)}) collective-permute-start(bf16[128,640]{1,0:T(8,128)(2,1)S(1)} %get-tuple-element.65), channel_id=1, source_target_pairs={{0,3},{1,0},{2,1},{3,2},{4,7},{5,4},{6,5},{7,6},{8,11},{9,8},{10,9... | collective-permute-start | bytes 491528 | tf_op jit(solution)/shard_map/return_tokens/ppermute | solution.py:339
  168.0 9.9 %collective-permute-start.17 = (bf16[128,640]{1,0:T(8,128)(2,1)S(1)}, bf16[128,640]{1,0:T(8,128)(2,1)S(1)}, u32[]{:S(2)}, u32[]{:S(2)}) collective-permute-start(bf16[128,640]{1,0:T(8,128)(2,1)S(1)} %get-tuple-element.66), channel_id=1, source_target_pairs={{0,1},{1,2},{2,3},{3,0},{4,5},{5,6},{6,7},{7,4},{8,9},{9,10},{10,1... | collective-permute-start | bytes 491528 | tf_op jit(solution)/shard_map/return_tokens/ppermute | solution.py:339
  169.8 8.2 %collective-permute-start.16 = (bf16[128,640]{1,0:T(8,128)(2,1)S(1)}, bf16[128,640]{1,0:T(8,128)(2,1)S(1)}, u32[]{:S(2)}, u32[]{:S(2)}) collective-permute-start(bf16[128,640]{1,0:T(8,128)(2,1)S(1)} %get-tuple-element.67), channel_id=1, source_target_pairs={{0,2},{1,3},{2,0},{3,1},{4,6},{5,7},{6,4},{7,5},{8,10},{9,11},{10,... | collective-permute-start | bytes 491528 | tf_op jit(solution)/shard_map/return_tokens/ppermute | solution.py:339

commit v7 on v6

--- a/solution.py
+++ b/solution.py
@@ -7,16 +7,15 @@
 
 BF = jnp.bfloat16
 F32 = jnp.float32
-VMEM_LIMIT = 20 * 1024 * 1024
 
 
 def cost(flops, nbytes, trans=0):
     return pl.CostEstimate(flops=flops, bytes_accessed=nbytes, transcendentals=trans)
 
 
-def params(grid_rank=1):
+def params(megabytes=20):
     return pltpu.CompilerParams(
-        dimension_semantics=("arbitrary",) * grid_rank, vmem_limit_bytes=VMEM_LIMIT
+        dimension_semantics=("arbitrary",), vmem_limit_bytes=megabytes * 1024 * 1024
     )
 
 
@@ -187,8 +186,8 @@
             g = g_in[part, :] + jnp.dot(t[...], wg[...], preferred_element_type=F32)
             u = u_in[part, :] + jnp.dot(t[...], wu[...], preferred_element_type=F32)
             s = 1.0 / (1.0 + jnp.exp(-g))
-            for_gate[part, :] = u * s * (1.0 + g * (1.0 - s))
-            for_up[part, :] = g * s
+            for_gate[part, :] = (u * s * (1.0 + g * (1.0 - s))).astype(BF)
+            for_up[part, :] = (g * s).astype(BF)
 
     weight = pl.BlockSpec((depth, HIDDEN_TILE), lambda j, x_ref: (quarter_at(x_ref, offset), j))
     tiled = pl.BlockSpec((rows, HIDDEN_TILE), lambda j, x_ref: (0, j))
@@ -201,10 +200,10 @@
             in_specs=halves + [tiled] * 2 + [weight] * 2,
             out_specs=[tiled] * 2,
         ),
-        out_shape=[pltpu.HBM((rows, hidden), F32)] * 2,
+        out_shape=[pltpu.HBM((rows, hidden), BF)] * 2,
         compiler_params=params(),
         cost_estimate=cost(
-            4 * rows * depth * hidden, 4 * depth * hidden + 16 * rows * hidden, rows * hidden
+            4 * rows * depth * hidden, 4 * depth * hidden + 12 * rows * hidden, rows * hidden
         ),
         name="up_last",
     )(x, upper, lower, gate, up, gate_weight, up_weight)
@@ -214,47 +213,32 @@
     rows, hidden = scaled.shape
     depth = gate_weight.shape[0] // 4
     half = rows // 2
-    steps = hidden // HIDDEN_TILE
-
-    def kernel(x_ref, h, a, b, wg, wu, gg_out, gu_out, out_top, out_bottom, total):
-        step = pl.program_id(0)
+
+    def kernel(x_ref, h, a, b, wg, wu, gg_out, gu_out, out_top, out_bottom):
         for k, out in enumerate((out_top, out_bottom)):
             part = slice(k * half, (k + 1) * half)
             h_part = h[part, :].astype(F32)
-            gg = (h_part * a[part, :]).astype(BF)
-            gu = (h_part * b[part, :]).astype(BF)
+            gg = (h_part * a[part, :].astype(F32)).astype(BF)
+            gu = (h_part * b[part, :].astype(F32)).astype(BF)
             gg_out[part, :] = gg
             gu_out[part, :] = gu
-            value = down_dot(gg, gu, wg[...], wu[...])
-
-            @pl.when(step == 0)
-            def _():
-                total[part, :] = value
-
-            @pl.when((step > 0) & (step < steps - 1))
-            def _():
-                total[part, :] += value
-
-            @pl.when(step == steps - 1)
-            def _():
-                out[...] = (total[part, :] + value).astype(BF)
-
-    weight = pl.BlockSpec((depth, HIDDEN_TILE), lambda j, x_ref: (quarter_at(x_ref, offset), j))
-    tiled = pl.BlockSpec((rows, HIDDEN_TILE), lambda j, x_ref: (0, j))
-    halves = [pl.BlockSpec((half, depth), lambda j, x_ref: (0, 0))] * 2
-    return pl.pallas_call(
-        kernel,
-        grid_spec=pltpu.PrefetchScalarGridSpec(
-            num_scalar_prefetch=1,
-            grid=(steps,),
-            in_specs=[tiled] * 3 + [weight] * 2,
-            out_specs=[tiled] * 2 + halves,
-            scratch_shapes=[pltpu.VMEM((rows, depth), F32)],
+            out[...] = down_dot(gg, gu, wg[...], wu[...]).astype(BF)
+
+    weight = pl.BlockSpec((depth, hidden), lambda k, x_ref: (quarter_at(x_ref, offset), 0))
+    whole = pl.BlockSpec((rows, hidden), lambda k, x_ref: (0, 0))
+    halves = [pl.BlockSpec((half, depth), lambda k, x_ref: (0, 0))] * 2
+    return pl.pallas_call(
+        kernel,
+        grid_spec=pltpu.PrefetchScalarGridSpec(
+            num_scalar_prefetch=1,
+            grid=(1,),
+            in_specs=[whole] * 3 + [weight] * 2,
+            out_specs=[whole] * 2 + halves,
         ),
         out_shape=[jax.ShapeDtypeStruct((rows, hidden), BF)] * 2
         + [jax.ShapeDtypeStruct((half, depth), BF)] * 2,
-        compiler_params=params(),
-        cost_estimate=cost(4 * rows * depth * hidden, 4 * depth * hidden + 14 * rows * hidden),
+        compiler_params=params(megabytes=30),
+        cost_estimate=cost(4 * rows * depth * hidden, 4 * depth * hidden + 10 * rows * hidden),
         name="down_first",
     )(x, scaled, in_hbm(for_gate), in_hbm(for_up), gate_weight, up_weight)
 
@@ -315,7 +299,7 @@
     return pl.pallas_call(
         kernel,
         out_shape=jax.ShapeDtypeStruct((2 * rows, width), BF),
-        compiler_params=pltpu.CompilerParams(vmem_limit_bytes=VMEM_LIMIT),
+        compiler_params=pltpu.CompilerParams(vmem_limit_bytes=20 * 1024 * 1024),
         cost_estimate=cost(4 * rows * width, 16 * rows * width),
         name="sum_halves",
     )(*upper, *lower)
@@ -371,13 +355,13 @@
 
     half = slots // 2
     with jax.named_scope("gather_width"):
-        own_sums = up_sums((in_hbm(own_block),), (0,), gate_w, up_w, x)
+        own_sums = up_sums((own_block,), (0,), gate_w, up_w, x)
         left_block, right_block, *own_sums = lax.optimization_barrier(
             (forward(own_block, 1), back(own_block, 1), *own_sums)
         )
         far_upper, far_lower = forward(left_block[:half], 1), back(right_block[half:], 1)
     with jax.named_scope("pre_activations"):
-        gate, up = up_sums((right_block, left_block), (1, 3), gate_w, up_w, x, own_sums)
+        gate, up = up_sums((in_hbm(right_block), in_hbm(left_block)), (1, 3), gate_w, up_w, x, own_sums)
         for_gate, for_up = up_last(far_upper, far_lower, in_hbm(gate), in_hbm(up), 2, gate_w, up_w, x)
     with jax.named_scope("input_partials"):
         grad_gate, grad_up, far_top, far_bottom = down_first(

time: 179 us -> 177 us (0.989)
  transfers between devices with their start and end apart: 21 -> 21, of which waited for: 14 -> 13; matrix products, arithmetic and copies ran while one was open for 1% -> 2% of each run, Pallas kernels for 18% -> 18%
where the time goes in v7:
time: 177 us
  waiting for transfers between devices  47.4 us (27%)
  starting transfers between devices  41.4 us (23%)
  blocking collectives  40.4 us (23%)
  Pallas kernels  39.3 us (22%)
  local copies, waits for them, and re-layouts  5.4 us (3%)
  matrix products  2.36 us (1%)
    all_to_all x1, blocking collectives, to_experts(): lax.all_to_all(array, 'expert', split_axis=0, concat_axis=0, tiled=True)  30.2 us
    ppermute x11, waiting for transfers between devices, back(): return lax.ppermute(array, 'etp', [(i, (i - r) % etp) for i in range(etp)])  24.1 us
    ppermute x11, starting transfers between devices, back(): return lax.ppermute(array, 'etp', [(i, (i - r) % etp) for i in range(etp)])  18.5 us
    all_to_all x2, starting transfers between devices, to_experts(): lax.all_to_all(array, 'expert', split_axis=0, concat_axis=0, tiled=True)  17.9 us
    ppermute x8, waiting for transfers between devices, forward(): return lax.ppermute(array, 'etp', [(i, (i + r) % etp) for i in range(etp)])  15.9 us
    pallas_call x3, Pallas kernels, down_halves(): pl.pallas_call(kernel, grid_spec=pltpu.PrefetchScalarGridSpec(num_scalar_...  12.7 us
    pallas_call x2, Pallas kernels, up_sums(): pl.pallas_call(kernel, grid_spec=pltpu.PrefetchScalarGridSpec(num_scalar_...  11.9 us
    all_gather x1, blocking collectives, on_device(): lax.all_gather(routes.reshape(1, own_rows), 'etp', axis=0, tiled=True)  10.2 us
  transfers between devices with their start and end apart: 21, of which 13 were waited for; matrix products, arithmetic and copies ran while one was open for 2% of the time, Pallas kernels for 18%

profile of v7, /device:TPU:8, one launch (start us, length us, event | category | flops | bytes accessed | tf_op | source)
XLA Modules:
  0.0 176.6 jit_solution(15761498730262387298)
XLA Ops:
  0.0 1.2 split_columns.2
  1.2 3.1 %collective-permute-start = (bf16[128,640]{1,0:T(8,128)(2,1)S(1)}, bf16[128,640]{1,0:T(8,128)(2,1)S(1)}, u32[]{:S(2)}, u32[]{:S(2)}) collective-permute-start(bf16[128,640]{1,0:T(8,128)(2,1)S(1)} %get-tuple-element.36), channel_id=1, source_target_pairs={{0,2},{1,3},{2,0},{3,1},{4,6},{5,7},{6,4},{7,5},{8,10},{9,11},{10,... | collective-permute-start | bytes 491528 | tf_op jit(solution)/shard_map/group_exchange/ppermute | solution.py:320
  4.3 1.1 collective-permute-start.1
  5.5 0.9 collective-permute-start.2
  6.4 10.2 %all-gather = s32[512,1]{0,1:T(1,128)S(1)} all-gather(s32[128,1]{0,1:T(1,128)S(1)} %copy-done.1), channel_id=2, replica_groups=mesh['expert'=64,'etp'=4] {'etp'}, dimensions={0}, use_global_device_ids=true | all-gather | bytes 2560 | tf_op jit(solution)/shard_map/group_exchange/all_gather | solution.py:331
  16.6 0.2 slot_index.1
  16.9 0.0 collective-permute-done.1
  16.9 0.0 collective-permute-done.2
  16.9 0.7 convolution_convert_fusion.1
  17.6 0.0 copy-start.2
  17.6 1.2 reshape.26
  18.8 12.1 %all-to-all-start = ((bf16[64,5,2,640]{3,2,1,0:T(2,128)(2,1)}), bf16[64,5,2,640]{3,2,1,0:T(2,128)(2,1)S(1)}, u32[]{:S(2)}, u32[]{:S(2)}) async-start(bf16[64,5,2,640]{3,2,1,0:T(2,128)(2,1)} %reshape.26), calls=%async_computation | async-start | bytes 1638400 | tf_op jit(solution)/shard_map/send_tokens/all_to_all | solution.py:346
  30.9 0.1 copy.7.refs_4_
  31.0 1.4 split_columns.3
  32.5 0.9 collective-permute-start.3
  33.4 1.6 collective-permute-start.4
  35.0 0.5 collective-permute-start.5
  35.5 7.8 %collective-permute-done.3 = bf16[128,1024]{1,0:T(8,128)(2,1)S(1)} collective-permute-done((bf16[128,1024]{1,0:T(8,128)(2,1)S(1)}, bf16[128,1024]{1,0:T(8,128)(2,1)S(1)}, u32[]{:S(2)}, u32[]{:S(2)}) %collective-permute-start.3) | collective-permute-done | bytes 262176 | tf_op jit(solution)/shard_map/group_exchange/ppermute | solution.py:320
  43.3 3.0 %collective-permute-done.4 = bf16[128,1024]{1,0:T(8,128)(2,1)S(1)} collective-permute-done((bf16[128,1024]{1,0:T(8,128)(2,1)S(1)}, bf16[128,1024]{1,0:T(8,128)(2,1)S(1)}, u32[]{:S(2)}, u32[]{:S(2)}) %collective-permute-start.4) | collective-permute-done | bytes 262176 | tf_op jit(solution)/shard_map/group_exchange/ppermute | solution.py:320
  46.2 1.8 %collective-permute-done.5 = bf16[128,1024]{1,0:T(8,128)(2,1)S(1)} collective-permute-done((bf16[128,1024]{1,0:T(8,128)(2,1)S(1)}, bf16[128,1024]{1,0:T(8,128)(2,1)S(1)}, u32[]{:S(2)}, u32[]{:S(2)}) %collective-permute-start.5) | collective-permute-done | bytes 262176 | tf_op jit(solution)/shard_map/group_exchange/ppermute | solution.py:320
  48.0 0.8 convolution_convert_fusion
  48.9 1.4 reshape.27
  50.3 4.5 %all-to-all-done = bf16[64,5,2,640]{3,2,1,0:T(2,128)(2,1)S(1)} async-done(((bf16[64,5,2,640]{3,2,1,0:T(2,128)(2,1)}), bf16[64,5,2,640]{3,2,1,0:T(2,128)(2,1)S(1)}, u32[]{:S(2)}, u32[]{:S(2)}) %all-to-all-start) | async-done | bytes 819232 | tf_op jit(solution)/shard_map/send_tokens/all_to_all | solution.py:346
  54.8 0.3 reshape.29.refs_0_
  55.1 0.9 collective-permute-start.7
  56.0 1.2 collective-permute-start.6
  57.2 5.8 %all-to-all-start.1 = ((bf16[64,80,128]{2,1,0:T(8,128)(2,1)}), bf16[64,80,128]{2,1,0:T(8,128)(2,1)S(1)}, u32[]{:S(2)}, u32[]{:S(2)}) async-start(bf16[64,80,128]{2,1,0:T(8,128)(2,1)} %reshape.27), calls=%async_computation.1 | async-start | bytes 2621440 | tf_op jit(solution)/shard_map/send_hidden/all_to_all | solution.py:346
  63.0 4.0 %up_sums.2 = (f32[640,1024]{1,0:T(8,128)S(1)}, f32[640,1024]{1,0:T(8,128)S(1)}) custom-call(s32[1]{0:T(128)} %bitcast.x_ref, bf16[640,640]{1,0:T(8,128)(2,1)S(1)} %reshape.29.refs_0_, bf16[2560,1024]{1,0:T(8,128)(2,1)} %bitcast.12, bf16[2560,1024]{1,0:T(8,128)(2,1)} %bitcast.20), custom_call_target="tpu_custom_call" | custom-call | flops 10066329600 | bytes 13107200 | tf_op jit(solution)/shard_map/gather_width/up_sums/pallas_call | solution.py:152
  67.1 7.4 %collective-permute-done.7.refs_0_ = bf16[640,640]{1,0:T(8,128)(2,1)S(1)} collective-permute-done((bf16[640,640]{1,0:T(8,128)(2,1)S(1)}, bf16[640,640]{1,0:T(8,128)(2,1)S(1)}, u32[]{:S(2)}, u32[]{:S(2)}) %collective-permute-start.7) | collective-permute-done | bytes 819232 | tf_op jit(solution)/shard_map/gather_width/ppermute | solution.py:320
  74.5 1.9 %collective-permute-done.6.refs_1_ = bf16[640,640]{1,0:T(8,128)(2,1)} collective-permute-done((bf16[640,640]{1,0:T(8,128)(2,1)S(1)}, bf16[640,640]{1,0:T(8,128)(2,1)}, u32[]{:S(2)}, u32[]{:S(2)}) %collective-permute-start.6) | collective-permute-done | bytes 819232 | tf_op jit(solution)/shard_map/gather_width/ppermute | solution.py:323
  76.4 1.0 slice.18
  77.4 0.7 collective-permute-start.9
  78.2 1.6 collective-permute-start.8
  79.7 7.9 %up_sums.3 = (f32[640,1024]{1,0:T(8,128)}, f32[640,1024]{1,0:T(8,128)}) custom-call(s32[1]{0:T(128)} %bitcast.x_ref, bf16[640,640]{1,0:T(8,128)(2,1)} %copy-done, bf16[640,640]{1,0:T(8,128)(2,1)} %collective-permute-done.6.refs_1_, bf16[2560,1024]{1,0:T(8,128)(2,1)} %bitcast.13, bf16[2560,1024]{1,0:T(8,128)(2,1)} %bitcast.14, bf16[2560,1024]{1,0:T(8,128)(2,1)} %bitcast.21, ...), custom_call_target="tpu_custom_call" | custom-call | flops 20132659200 | bytes 15728640 | tf_op jit(solution)/shard_map/pre_activations/up_sums/pallas_call | solution.py:152
  87.6 0.0 collective-permute-done.9.bottom
  87.6 1.1 collective-permute-done.8.top
  88.7 5.9 %up_last.1 = (bf16[640,1024]{1,0:T(8,128)(2,1)}, bf16[640,1024]{1,0:T(8,128)(2,1)}) custom-call(s32[1]{0:T(128)} %bitcast.x_ref, bf16[320,640]{1,0:T(8,128)(2,1)S(1)} %collective-permute-done.8.top, bf16[320,640]{1,0:T(8,128)(2,1)S(1)} %collective-permute-done.9.bottom, f32[640,1024]{1,0:T(8,128)} %get-tuple-element.51.g_in, ...), custom_call_target="tpu_custom_call" | custom-call | flops 1677721600 | bytes 10485760 | tf_op jit(solution)/shard_map/pre_activations/up_last/pallas_call | solution.py:195
  94.6 2.9 %all-to-all-done.1 = bf16[64,80,128]{2,1,0:T(8,128)(2,1)S(1)} async-done(((bf16[64,80,128]{2,1,0:T(8,128)(2,1)}), bf16[64,80,128]{2,1,0:T(8,128)(2,1)S(1)}, u32[]{:S(2)}, u32[]{:S(2)}) %all-to-all-start.1) | async-done | bytes 1310752 | tf_op jit(solution)/shard_map/send_hidden/all_to_all | solution.py:346
  97.5 0.6 reshape.28.h
  98.1 4.7 %down_first.1 = (bf16[640,1024]{1,0:T(8,128)(2,1)S(1)}, bf16[640,1024]{1,0:T(8,128)(2,1)S(1)}, bf16[320,640]{1,0:T(8,128)(2,1)S(1)}, bf16[320,640]{1,0:T(8,128)(2,1)S(1)}) custom-call(s32[1]{0:T(128)} %bitcast.x_ref, bf16[640,1024]{1,0:T(8,128)(2,1)S(1)} %reshape.28.h, bf16[640,1024]{1,0:T(8,128)(2,1)} %get-tuple-element.53.a, ...), custom_call_target="tpu_custom_call" | custom-call | flops 1677721600 | bytes 9175040 | tf_op jit(solution)/shard_map/input_partials/down_first/pallas_call | solution.py:230
  102.8 2.1 %collective-permute-start.14 = (bf16[320,640]{1,0:T(8,128)(2,1)S(1)}, bf16[320,640]{1,0:T(8,128)(2,1)S(1)}, u32[]{:S(2)}, u32[]{:S(2)}) collective-permute-start(bf16[320,640]{1,0:T(8,128)(2,1)S(1)} %get-tuple-element.64), channel_id=1, source_target_pairs={{0,3},{1,0},{2,1},{3,2},{4,7},{5,4},{6,5},{7,6},{8,11},{9,8},{10,9... | collective-permute-start | bytes 1228808 | tf_op jit(solution)/shard_map/sum_quarters/ppermute | solution.py:320
  104.9 4.2 %down_halves.5 = (bf16[320,640]{1,0:T(8,128)(2,1)S(1)}, bf16[320,640]{1,0:T(8,128)(2,1)S(1)}) custom-call(s32[1]{0:T(128)} %bitcast.x_ref, bf16[640,1024]{1,0:T(8,128)(2,1)S(1)} %get-tuple-element.55.gg, bf16[640,1024]{1,0:T(8,128)(2,1)S(1)} %get-tuple-element.56.gu, bf16[2560,1024]{1,0:T(8,128)(2,1)} %bitcast.17, bf16[2560,1024]{1,0:T(8,128)(2,1)} %bitcast.25), custom_call_target="tpu_custom_call" | custom-call | flops 419430400 | bytes 7864320 | tf_op jit(solution)/shard_map/input_partials/down_halves/pallas_call | solution.py:270
  109.2 3.3 %collective-permute-start.12 = (bf16[320,640]{1,0:T(8,128)(2,1)S(1)}, bf16[320,640]{1,0:T(8,128)(2,1)S(1)}, u32[]{:S(2)}, u32[]{:S(2)}) collective-permute-start(bf16[320,640]{1,0:T(8,128)(2,1)S(1)} %get-tuple-element.60), channel_id=1, source_target_pairs={{0,3},{1,0},{2,1},{3,2},{4,7},{5,4},{6,5},{7,6},{8,11},{9,8},{10,9... | collective-permute-start | bytes 1228808 | tf_op jit(solution)/shard_map/sum_quarters/ppermute | solution.py:320
  112.5 0.0 collective-permute-start.13
  112.5 4.2 %down_halves.4 = (f32[320,640]{1,0:T(8,128)S(1)}, f32[320,640]{1,0:T(8,128)S(1)}) custom-call(s32[1]{0:T(128)} %bitcast.x_ref, bf16[640,1024]{1,0:T(8,128)(2,1)S(1)} %get-tuple-element.55.gg, bf16[640,1024]{1,0:T(8,128)(2,1)S(1)} %get-tuple-element.56.gu, bf16[2560,1024]{1,0:T(8,128)(2,1)} %bitcast.18, bf16[2560,1024]{1,0:T(8,128)(2,1)} %bitcast.26), custom_call_target="tpu_custom_call" | custom-call | flops 419430400 | bytes 7864320 | tf_op jit(solution)/shard_map/input_partials/down_halves/pallas_call | solution.py:270
  116.7 0.1 add_convert_fusion
  116.8 3.3 %collective-permute-start.15 = (bf16[320,640]{1,0:T(8,128)(2,1)S(1)}, bf16[320,640]{1,0:T(8,128)(2,1)S(1)}, u32[]{:S(2)}, u32[]{:S(2)}) collective-permute-start(bf16[320,640]{1,0:T(8,128)(2,1)S(1)} %add_convert_fusion), channel_id=1, source_target_pairs={{0,3},{1,0},{2,1},{3,2},{4,7},{5,4},{6,5},{7,6},{8,11},{9,8},{10,9... | collective-permute-start | bytes 1228808 | tf_op jit(solution)/shard_map/sum_quarters/ppermute | solution.py:320
  120.1 0.1 add_convert_fusion.1
  120.2 0.1 collective-permute-start.11
  120.3 4.2 %down_halves.3 = (f32[320,640]{1,0:T(8,128)S(1)}, f32[320,640]{1,0:T(8,128)S(1)}) custom-call(s32[1]{0:T(128)} %bitcast.x_ref, bf16[640,1024]{1,0:T(8,128)(2,1)S(1)} %get-tuple-element.55.gg, bf16[640,1024]{1,0:T(8,128)(2,1)S(1)} %get-tuple-element.56.gu, bf16[2560,1024]{1,0:T(8,128)(2,1)} %bitcast.19, bf16[2560,1024]{1,0:T(8,128)(2,1)} %bitcast.27), custom_call_target="tpu_custom_call" | custom-call | flops 419430400 | bytes 7864320 | tf_op jit(solution)/shard_map/input_partials/down_halves/pallas_call | solution.py:270
  124.6 1.8 %collective-permute-done.13.refs_4_ = bf16[320,640]{1,0:T(8,128)(2,1)S(1)} collective-permute-done((bf16[320,640]{1,0:T(8,128)(2,1)S(1)}, bf16[320,640]{1,0:T(8,128)(2,1)S(1)}, u32[]{:S(2)}, u32[]{:S(2)}) %collective-permute-start.13) | collective-permute-done | bytes 409632 | tf_op jit(solution)/shard_map/sum_quarters/ppermute | solution.py:323
  126.4 4.1 %collective-permute-done.15.refs_5_ = bf16[320,640]{1,0:T(8,128)(2,1)S(1)} collective-permute-done((bf16[320,640]{1,0:T(8,128)(2,1)S(1)}, bf16[320,640]{1,0:T(8,128)(2,1)S(1)}, u32[]{:S(2)}, u32[]{:S(2)}) %collective-permute-start.15) | collective-permute-done | bytes 409632 | tf_op jit(solution)/shard_map/sum_quarters/ppermute | solution.py:320
  130.5 3.0 %collective-permute-done.11.refs_1_ = bf16[320,640]{1,0:T(8,128)(2,1)S(1)} collective-permute-done((bf16[320,640]{1,0:T(8,128)(2,1)S(1)}, bf16[320,640]{1,0:T(8,128)(2,1)S(1)}, u32[]{:S(2)}, u32[]{:S(2)}) %collective-permute-start.11) | collective-permute-done | bytes 409632 | tf_op jit(solution)/shard_map/sum_quarters/ppermute | solution.py:323
  133.5 0.3 sum_halves.1
  133.7 0.3 reshape.30
  134.1 30.2 %all_to_all.15 = bf16[64,5,2,640]{3,2,1,0:T(2,128)(2,1)S(1)} all-to-all(bf16[64,5,2,640]{3,2,1,0:T(2,128)(2,1)S(1)} %reshape.30), channel_id=1, replica_groups=mesh['expert'=64,'etp'=4] {'expert'}, dimensions={0} | all-to-all | bytes 1638400 | tf_op jit(solution)/shard_map/return_tokens/all_to_all | solution.py:346
  164.2 0.3 reshape.31
  164.5 0.8 convolution_convert_fusion.2
  165.4 0.1 fusion.19
  165.4 0.4 collective-permute-start.18
  165.8 1.7 collective-permute-start.17
  167.5 5.0 %collective-permute-done.18.b3 = bf16[128,640]{1,0:T(8,128)(2,1)S(1)} collective-permute-done((bf16[128,640]{1,0:T(8,128)(2,1)S(1)}, bf16[128,640]{1,0:T(8,128)(2,1)S(1)}, u32[]{:S(2)}, u32[]{:S(2)}) %collective-permute-start.18) | collective-permute-done | bytes 163872 | tf_op jit(solution)/shard_map/return_tokens/ppermute | solution.py:323
  172.5 3.2 %collective-permute-done.17.b2 = bf16[128,640]{1,0:T(8,128)(2,1)S(1)} collective-permute-done((bf16[128,640]{1,0:T(8,128)(2,1)S(1)}, bf16[128,640]{1,0:T(8,128)(2,1)S(1)}, u32[]{:S(2)}, u32[]{:S(2)}) %collective-permute-start.17) | collective-permute-done | bytes 163872 | tf_op jit(solution)/shard_map/return_tokens/ppermute | solution.py:323
  175.7 0.9 join_columns.1
  (14 shorter events, 0.1 us)
Async XLA Ops:
  0.0 6.4 %copy-start.1 = (s32[128,1]{0,1:T(1,128)S(1)}, s32[128,1]{0,1:T(1,128)}, u32[]{:S(2)}) copy-start(s32[128,1]{0,1:T(1,128)} %param.8) | copy-start | bytes 1540
  1.2 15.6 %collective-permute-start = (bf16[128,640]{1,0:T(8,128)(2,1)S(1)}, bf16[128,640]{1,0:T(8,128)(2,1)S(1)}, u32[]{:S(2)}, u32[]{:S(2)}) collective-permute-start(bf16[128,640]{1,0:T(8,128)(2,1)S(1)} %get-tuple-element.36), channel_id=1, source_target_pairs={{0,2},{1,3},{2,0},{3,1},{4,6},{5,7},{6,4},{7,5},{8,10},{9,11},{10,... | collective-permute-start | bytes 491528 | tf_op jit(solution)/shard_map/group_exchange/ppermute | solution.py:320
  4.3 12.5 %collective-permute-start.1 = (bf16[128,640]{1,0:T(8,128)(2,1)S(1)}, bf16[128,640]{1,0:T(8,128)(2,1)S(1)}, u32[]{:S(2)}, u32[]{:S(2)}) collective-permute-start(bf16[128,640]{1,0:T(8,128)(2,1)S(1)} %get-tuple-element.37), channel_id=1, source_target_pairs={{0,3},{1,0},{2,1},{3,2},{4,7},{5,4},{6,5},{7,6},{8,11},{9,8},{10,9... | collective-permute-start | bytes 491528 | tf_op jit(solution)/shard_map/group_exchange/ppermute | solution.py:320
  5.5 11.4 %collective-permute-start.2 = (bf16[128,640]{1,0:T(8,128)(2,1)S(1)}, bf16[128,640]{1,0:T(8,128)(2,1)S(1)}, u32[]{:S(2)}, u32[]{:S(2)}) collective-permute-start(bf16[128,640]{1,0:T(8,128)(2,1)S(1)} %get-tuple-element.38), channel_id=1, source_target_pairs={{0,1},{1,2},{2,3},{3,0},{4,5},{5,6},{6,7},{7,4},{8,9},{9,10},{10,1... | collective-permute-start | bytes 491528 | tf_op jit(solution)/shard_map/group_exchange/ppermute | solution.py:320
  17.6 13.3 %copy-start.2 = (s32[128]{0:T(128)S(1)}, s32[128]{0:T(128)}, u32[]{:S(2)}) copy-start(s32[128]{0:T(128)} %param.9) | copy-start | bytes 1540
  18.8 36.0 %all-to-all-start = ((bf16[64,5,2,640]{3,2,1,0:T(2,128)(2,1)}), bf16[64,5,2,640]{3,2,1,0:T(2,128)(2,1)S(1)}, u32[]{:S(2)}, u32[]{:S(2)}) async-start(bf16[64,5,2,640]{3,2,1,0:T(2,128)(2,1)} %reshape.26), calls=%async_computation | async-start | bytes 1638400 | tf_op jit(solution)/shard_map/send_tokens/all_to_all | solution.py:346
  32.5 10.8 %collective-permute-start.3 = (bf16[128,1024]{1,0:T(8,128)(2,1)S(1)}, bf16[128,1024]{1,0:T(8,128)(2,1)S(1)}, u32[]{:S(2)}, u32[]{:S(2)}) collective-permute-start(bf16[128,1024]{1,0:T(8,128)(2,1)S(1)} %get-tuple-element.40), channel_id=1, source_target_pairs={{0,2},{1,3},{2,0},{3,1},{4,6},{5,7},{6,4},{7,5},{8,10},{9,11},{10,... | collective-permute-start | bytes 786440 | tf_op jit(solution)/shard_map/group_exchange/ppermute | solution.py:320
  33.4 12.8 %collective-permute-start.4 = (bf16[128,1024]{1,0:T(8,128)(2,1)S(1)}, bf16[128,1024]{1,0:T(8,128)(2,1)S(1)}, u32[]{:S(2)}, u32[]{:S(2)}) collective-permute-start(bf16[128,1024]{1,0:T(8,128)(2,1)S(1)} %get-tuple-element.41), channel_id=1, source_target_pairs={{0,3},{1,0},{2,1},{3,2},{4,7},{5,4},{6,5},{7,6},{8,11},{9,8},{10,9... | collective-permute-start | bytes 786440 | tf_op jit(solution)/shard_map/group_exchange/ppermute | solution.py:320
  35.0 13.1 %collective-permute-start.5 = (bf16[128,1024]{1,0:T(8,128)(2,1)S(1)}, bf16[128,1024]{1,0:T(8,128)(2,1)S(1)}, u32[]{:S(2)}, u32[]{:S(2)}) collective-permute-start(bf16[128,1024]{1,0:T(8,128)(2,1)S(1)} %get-tuple-element.42), channel_id=1, source_target_pairs={{0,1},{1,2},{2,3},{3,0},{4,5},{5,6},{6,7},{7,4},{8,9},{9,10},{10,1... | collective-permute-start | bytes 786440 | tf_op jit(solution)/shard_map/group_exchange/ppermute | solution.py:320
  55.1 19.4 %collective-permute-start.7 = (bf16[640,640]{1,0:T(8,128)(2,1)S(1)}, bf16[640,640]{1,0:T(8,128)(2,1)S(1)}, u32[]{:S(2)}, u32[]{:S(2)}) collective-permute-start(bf16[640,640]{1,0:T(8,128)(2,1)S(1)} %reshape.29.refs_0_), channel_id=1, source_target_pairs={{0,3},{1,0},{2,1},{3,2},{4,7},{5,4},{6,5},{7,6},{8,11},{9,8},{10,9... | collective-permute-start | bytes 2457608 | tf_op jit(solution)/shard_map/gather_width/ppermute | solution.py:320
  56.0 20.4 %collective-permute-start.6 = (bf16[640,640]{1,0:T(8,128)(2,1)S(1)}, bf16[640,640]{1,0:T(8,128)(2,1)}, u32[]{:S(2)}, u32[]{:S(2)}) collective-permute-start(bf16[640,640]{1,0:T(8,128)(2,1)S(1)} %reshape.29.refs_0_), channel_id=1, source_target_pairs={{0,1},{1,2},{2,3},{3,0},{4,5},{5,6},{6,7},{7,4},{8,9},{9,10},{10,1... | collective-permute-start | bytes 2457608 | tf_op jit(solution)/shard_map/gather_width/ppermute | solution.py:323
  57.2 40.3 %all-to-all-start.1 = ((bf16[64,80,128]{2,1,0:T(8,128)(2,1)}), bf16[64,80,128]{2,1,0:T(8,128)(2,1)S(1)}, u32[]{:S(2)}, u32[]{:S(2)}) async-start(bf16[64,80,128]{2,1,0:T(8,128)(2,1)} %reshape.27), calls=%async_computation.1 | async-start | bytes 2621440 | tf_op jit(solution)/shard_map/send_hidden/all_to_all | solution.py:346
  74.5 5.2 %copy-start = (bf16[640,640]{1,0:T(8,128)(2,1)}, bf16[640,640]{1,0:T(8,128)(2,1)S(1)}, u32[]{:S(2)}) copy-start(bf16[640,640]{1,0:T(8,128)(2,1)S(1)} %collective-permute-done.7.refs_0_) | copy-start | bytes 2457604
  77.4 10.2 %collective-permute-start.9 = (bf16[320,640]{1,0:T(8,128)(2,1)S(1)}, bf16[320,640]{1,0:T(8,128)(2,1)S(1)}, u32[]{:S(2)}, u32[]{:S(2)}) collective-permute-start(bf16[320,640]{1,0:T(8,128)(2,1)S(1)} %slice.19), channel_id=1, source_target_pairs={{0,3},{1,0},{2,1},{3,2},{4,7},{5,4},{6,5},{7,6},{8,11},{9,8},{10,9... | collective-permute-start | bytes 1228808 | tf_op jit(solution)/shard_map/gather_width/ppermute | solution.py:320
  78.2 10.6 %collective-permute-start.8 = (bf16[320,640]{1,0:T(8,128)(2,1)S(1)}, bf16[320,640]{1,0:T(8,128)(2,1)S(1)}, u32[]{:S(2)}, u32[]{:S(2)}) collective-permute-start(bf16[320,640]{1,0:T(8,128)(2,1)S(1)} %slice.18), channel_id=1, source_target_pairs={{0,1},{1,2},{2,3},{3,0},{4,5},{5,6},{6,7},{7,4},{8,9},{9,10},{10,1... | collective-permute-start | bytes 1228808 | tf_op jit(solution)/shard_map/gather_width/ppermute | solution.py:323
  102.8 13.9 %collective-permute-start.14 = (bf16[320,640]{1,0:T(8,128)(2,1)S(1)}, bf16[320,640]{1,0:T(8,128)(2,1)S(1)}, u32[]{:S(2)}, u32[]{:S(2)}) collective-permute-start(bf16[320,640]{1,0:T(8,128)(2,1)S(1)} %get-tuple-element.64), channel_id=1, source_target_pairs={{0,3},{1,0},{2,1},{3,2},{4,7},{5,4},{6,5},{7,6},{8,11},{9,8},{10,9... | collective-permute-start | bytes 1228808 | tf_op jit(solution)/shard_map/sum_quarters/ppermute | solution.py:320
  104.9 15.2 %collective-permute-start.10 = (bf16[320,640]{1,0:T(8,128)(2,1)S(1)}, bf16[320,640]{1,0:T(8,128)(2,1)S(1)}, u32[]{:S(2)}, u32[]{:S(2)}) collective-permute-start(bf16[320,640]{1,0:T(8,128)(2,1)S(1)} %get-tuple-element.59), channel_id=1, source_target_pairs={{0,1},{1,2},{2,3},{3,0},{4,5},{5,6},{6,7},{7,4},{8,9},{9,10},{10,1... | collective-permute-start | bytes 1228808 | tf_op jit(solution)/shard_map/sum_quarters/ppermute | solution.py:323
  109.2 15.4 %collective-permute-start.12 = (bf16[320,640]{1,0:T(8,128)(2,1)S(1)}, bf16[320,640]{1,0:T(8,128)(2,1)S(1)}, u32[]{:S(2)}, u32[]{:S(2)}) collective-permute-start(bf16[320,640]{1,0:T(8,128)(2,1)S(1)} %get-tuple-element.60), channel_id=1, source_target_pairs={{0,3},{1,0},{2,1},{3,2},{4,7},{5,4},{6,5},{7,6},{8,11},{9,8},{10,9... | collective-permute-start | bytes 1228808 | tf_op jit(solution)/shard_map/sum_quarters/ppermute | solution.py:320
  112.5 13.9 %collective-permute-start.13 = (bf16[320,640]{1,0:T(8,128)(2,1)S(1)}, bf16[320,640]{1,0:T(8,128)(2,1)S(1)}, u32[]{:S(2)}, u32[]{:S(2)}) collective-permute-start(bf16[320,640]{1,0:T(8,128)(2,1)S(1)} %get-tuple-element.62), channel_id=1, source_target_pairs={{0,1},{1,2},{2,3},{3,0},{4,5},{5,6},{6,7},{7,4},{8,9},{9,10},{10,1... | collective-permute-start | bytes 1228808 | tf_op jit(solution)/shard_map/sum_quarters/ppermute | solution.py:323
  116.8 13.7 %collective-permute-start.15 = (bf16[320,640]{1,0:T(8,128)(2,1)S(1)}, bf16[320,640]{1,0:T(8,128)(2,1)S(1)}, u32[]{:S(2)}, u32[]{:S(2)}) collective-permute-start(bf16[320,640]{1,0:T(8,128)(2,1)S(1)} %add_convert_fusion), channel_id=1, source_target_pairs={{0,3},{1,0},{2,1},{3,2},{4,7},{5,4},{6,5},{7,6},{8,11},{9,8},{10,9... | collective-permute-start | bytes 1228808 | tf_op jit(solution)/shard_map/sum_quarters/ppermute | solution.py:320
  120.2 13.2 %collective-permute-start.11 = (bf16[320,640]{1,0:T(8,128)(2,1)S(1)}, bf16[320,640]{1,0:T(8,128)(2,1)S(1)}, u32[]{:S(2)}, u32[]{:S(2)}) collective-permute-start(bf16[320,640]{1,0:T(8,128)(2,1)S(1)} %add_convert_fusion.1), channel_id=1, source_target_pairs={{0,1},{1,2},{2,3},{3,0},{4,5},{5,6},{6,7},{7,4},{8,9},{9,10},{10,1... | collective-permute-start | bytes 1228808 | tf_op jit(solution)/shard_map/sum_quarters/ppermute | solution.py:323
  165.4 7.1 %collective-permute-start.18 = (bf16[128,640]{1,0:T(8,128)(2,1)S(1)}, bf16[128,640]{1,0:T(8,128)(2,1)S(1)}, u32[]{:S(2)}, u32[]{:S(2)}) collective-permute-start(bf16[128,640]{1,0:T(8,128)(2,1)S(1)} %get-tuple-element.65), channel_id=1, source_target_pairs={{0,3},{1,0},{2,1},{3,2},{4,7},{5,4},{6,5},{7,6},{8,11},{9,8},{10,9... | collective-permute-start | bytes 491528 | tf_op jit(solution)/shard_map/return_tokens/ppermute | solution.py:323
  165.8 9.9 %collective-permute-start.17 = (bf16[128,640]{1,0:T(8,128)(2,1)S(1)}, bf16[128,640]{1,0:T(8,128)(2,1)S(1)}, u32[]{:S(2)}, u32[]{:S(2)}) collective-permute-start(bf16[128,640]{1,0:T(8,128)(2,1)S(1)} %get-tuple-element.66), channel_id=1, source_target_pairs={{0,1},{1,2},{2,3},{3,0},{4,5},{5,6},{6,7},{7,4},{8,9},{9,10},{10,1... | collective-permute-start | bytes 491528 | tf_op jit(solution)/shard_map/return_tokens/ppermute | solution.py:323
  167.5 8.2 %collective-permute-start.16 = (bf16[128,640]{1,0:T(8,128)(2,1)S(1)}, bf16[128,640]{1,0:T(8,128)(2,1)S(1)}, u32[]{:S(2)}, u32[]{:S(2)}) collective-permute-start(bf16[128,640]{1,0:T(8,128)(2,1)S(1)} %get-tuple-element.67), channel_id=1, source_target_pairs={{0,2},{1,3},{2,0},{3,1},{4,6},{5,7},{6,4},{7,5},{8,10},{9,11},{10,... | collective-permute-start | bytes 491528 | tf_op jit(solution)/shard_map/return_tokens/ppermute | solution.py:323

commit v8 on v7

--- a/solution.py
+++ b/solution.py
@@ -392,8 +392,9 @@
             select, rows, (((0,), (0,)), ((), ())), preferred_element_type=F32
         ).astype(BF)
         parts = [group_rows[k * own_rows : (k + 1) * own_rows] for k in range(4)]
-        blocks = [parts[0]] + [forward(parts[k], ahead[k]) for k in (1, 2, 3)]
-        return join_columns(blocks, x, [-r for r in ahead])
+        order = (0, 2, 3, 1)
+        blocks = [forward(parts[k], ahead[k]) if k else parts[0] for k in order]
+        return join_columns(blocks, x, [-ahead[k] for k in order])
 
 
 def solution(mesh):

time: 177 us -> 178 us (level)
  no operation moved by 1% of the time
where the time goes in v8:
time: 178 us; the launch traced here: 177 us
  waiting for transfers between devices  47.4 us (27%)
  starting transfers between devices  41.5 us (23%)
  blocking collectives  40.4 us (23%)
  Pallas kernels  39.3 us (22%)
  local copies, waits for them, and re-layouts  5.4 us (3%)
  matrix products  2.36 us (1%)
    all_to_all x1, blocking collectives, to_experts(): lax.all_to_all(array, 'expert', split_axis=0, concat_axis=0, tiled=True)  30.2 us
    ppermute x11, waiting for transfers between devices, back(): return lax.ppermute(array, 'etp', [(i, (i - r) % etp) for i in range(etp)])  24.1 us
    ppermute x11, starting transfers between devices, back(): return lax.ppermute(array, 'etp', [(i, (i - r) % etp) for i in range(etp)])  18.5 us
    all_to_all x2, starting transfers between devices, to_experts(): lax.all_to_all(array, 'expert', split_axis=0, concat_axis=0, tiled=True)  17.9 us
    ppermute x8, waiting for transfers between devices, forward(): return lax.ppermute(array, 'etp', [(i, (i + r) % etp) for i in range(etp)])  15.9 us
    pallas_call x3, Pallas kernels, down_halves(): pl.pallas_call(kernel, grid_spec=pltpu.PrefetchScalarGridSpec(num_scalar_...  12.7 us
    pallas_call x2, Pallas kernels, up_sums(): pl.pallas_call(kernel, grid_spec=pltpu.PrefetchScalarGridSpec(num_scalar_...  11.9 us
    all_gather x1, blocking collectives, on_device(): lax.all_gather(routes.reshape(1, own_rows), 'etp', axis=0, tiled=True)  10.2 us
  transfers between devices with their start and end apart: 21, of which 13 were waited for; matrix products, arithmetic and copies ran while one was open for 2% of the time, Pallas kernels for 18%

profile of v8, /device:TPU:8, one launch (start us, length us, event | category | flops | bytes accessed | tf_op | source)
XLA Modules:
  0.0 176.7 jit_solution(1092669066064600963)
XLA Ops:
  0.0 1.2 split_columns.2
  1.2 3.1 %collective-permute-start = (bf16[128,640]{1,0:T(8,128)(2,1)S(1)}, bf16[128,640]{1,0:T(8,128)(2,1)S(1)}, u32[]{:S(2)}, u32[]{:S(2)}) collective-permute-start(bf16[128,640]{1,0:T(8,128)(2,1)S(1)} %get-tuple-element.36), channel_id=1, source_target_pairs={{0,2},{1,3},{2,0},{3,1},{4,6},{5,7},{6,4},{7,5},{8,10},{9,11},{10,... | collective-permute-start | bytes 491528 | tf_op jit(solution)/shard_map/group_exchange/ppermute | solution.py:320
  4.3 1.1 collective-permute-start.1
  5.5 0.9 collective-permute-start.2
  6.4 10.2 %all-gather = s32[512,1]{0,1:T(1,128)S(1)} all-gather(s32[128,1]{0,1:T(1,128)S(1)} %copy-done.1), channel_id=2, replica_groups=mesh['expert'=64,'etp'=4] {'etp'}, dimensions={0}, use_global_device_ids=true | all-gather | bytes 2560 | tf_op jit(solution)/shard_map/group_exchange/all_gather | solution.py:331
  16.6 0.2 slot_index.1
  16.9 0.0 collective-permute-done.1
  16.9 0.0 collective-permute-done.2
  16.9 0.7 convolution_convert_fusion.1
  17.6 0.0 copy-start.2
  17.6 1.2 reshape.26
  18.8 12.1 %all-to-all-start = ((bf16[64,5,2,640]{3,2,1,0:T(2,128)(2,1)}), bf16[64,5,2,640]{3,2,1,0:T(2,128)(2,1)S(1)}, u32[]{:S(2)}, u32[]{:S(2)}) async-start(bf16[64,5,2,640]{3,2,1,0:T(2,128)(2,1)} %reshape.26), calls=%async_computation | async-start | bytes 1638400 | tf_op jit(solution)/shard_map/send_tokens/all_to_all | solution.py:346
  30.9 0.1 copy.7.refs_4_
  31.0 1.4 split_columns.3
  32.5 0.9 collective-permute-start.3
  33.4 1.6 collective-permute-start.4
  35.0 0.5 collective-permute-start.5
  35.5 7.8 %collective-permute-done.3 = bf16[128,1024]{1,0:T(8,128)(2,1)S(1)} collective-permute-done((bf16[128,1024]{1,0:T(8,128)(2,1)S(1)}, bf16[128,1024]{1,0:T(8,128)(2,1)S(1)}, u32[]{:S(2)}, u32[]{:S(2)}) %collective-permute-start.3) | collective-permute-done | bytes 262176 | tf_op jit(solution)/shard_map/group_exchange/ppermute | solution.py:320
  43.3 3.0 %collective-permute-done.4 = bf16[128,1024]{1,0:T(8,128)(2,1)S(1)} collective-permute-done((bf16[128,1024]{1,0:T(8,128)(2,1)S(1)}, bf16[128,1024]{1,0:T(8,128)(2,1)S(1)}, u32[]{:S(2)}, u32[]{:S(2)}) %collective-permute-start.4) | collective-permute-done | bytes 262176 | tf_op jit(solution)/shard_map/group_exchange/ppermute | solution.py:320
  46.2 1.8 %collective-permute-done.5 = bf16[128,1024]{1,0:T(8,128)(2,1)S(1)} collective-permute-done((bf16[128,1024]{1,0:T(8,128)(2,1)S(1)}, bf16[128,1024]{1,0:T(8,128)(2,1)S(1)}, u32[]{:S(2)}, u32[]{:S(2)}) %collective-permute-start.5) | collective-permute-done | bytes 262176 | tf_op jit(solution)/shard_map/group_exchange/ppermute | solution.py:320
  48.0 0.8 convolution_convert_fusion
  48.9 1.4 reshape.27
  50.3 4.5 %all-to-all-done = bf16[64,5,2,640]{3,2,1,0:T(2,128)(2,1)S(1)} async-done(((bf16[64,5,2,640]{3,2,1,0:T(2,128)(2,1)}), bf16[64,5,2,640]{3,2,1,0:T(2,128)(2,1)S(1)}, u32[]{:S(2)}, u32[]{:S(2)}) %all-to-all-start) | async-done | bytes 819232 | tf_op jit(solution)/shard_map/send_tokens/all_to_all | solution.py:346
  54.8 0.3 reshape.29.refs_0_
  55.1 0.9 collective-permute-start.7
  56.0 1.2 collective-permute-start.6
  57.2 5.8 %all-to-all-start.1 = ((bf16[64,80,128]{2,1,0:T(8,128)(2,1)}), bf16[64,80,128]{2,1,0:T(8,128)(2,1)S(1)}, u32[]{:S(2)}, u32[]{:S(2)}) async-start(bf16[64,80,128]{2,1,0:T(8,128)(2,1)} %reshape.27), calls=%async_computation.1 | async-start | bytes 2621440 | tf_op jit(solution)/shard_map/send_hidden/all_to_all | solution.py:346
  63.0 4.0 %up_sums.2 = (f32[640,1024]{1,0:T(8,128)S(1)}, f32[640,1024]{1,0:T(8,128)S(1)}) custom-call(s32[1]{0:T(128)} %bitcast.x_ref, bf16[640,640]{1,0:T(8,128)(2,1)S(1)} %reshape.29.refs_0_, bf16[2560,1024]{1,0:T(8,128)(2,1)} %bitcast.12, bf16[2560,1024]{1,0:T(8,128)(2,1)} %bitcast.20), custom_call_target="tpu_custom_call" | custom-call | flops 10066329600 | bytes 13107200 | tf_op jit(solution)/shard_map/gather_width/up_sums/pallas_call | solution.py:152
  67.1 7.4 %collective-permute-done.7.refs_0_ = bf16[640,640]{1,0:T(8,128)(2,1)S(1)} collective-permute-done((bf16[640,640]{1,0:T(8,128)(2,1)S(1)}, bf16[640,640]{1,0:T(8,128)(2,1)S(1)}, u32[]{:S(2)}, u32[]{:S(2)}) %collective-permute-start.7) | collective-permute-done | bytes 819232 | tf_op jit(solution)/shard_map/gather_width/ppermute | solution.py:320
  74.5 1.9 %collective-permute-done.6.refs_1_ = bf16[640,640]{1,0:T(8,128)(2,1)} collective-permute-done((bf16[640,640]{1,0:T(8,128)(2,1)S(1)}, bf16[640,640]{1,0:T(8,128)(2,1)}, u32[]{:S(2)}, u32[]{:S(2)}) %collective-permute-start.6) | collective-permute-done | bytes 819232 | tf_op jit(solution)/shard_map/gather_width/ppermute | solution.py:323
  76.4 1.0 slice.18
  77.4 0.7 collective-permute-start.9
  78.2 1.6 collective-permute-start.8
  79.7 7.9 %up_sums.3 = (f32[640,1024]{1,0:T(8,128)}, f32[640,1024]{1,0:T(8,128)}) custom-call(s32[1]{0:T(128)} %bitcast.x_ref, bf16[640,640]{1,0:T(8,128)(2,1)} %copy-done, bf16[640,640]{1,0:T(8,128)(2,1)} %collective-permute-done.6.refs_1_, bf16[2560,1024]{1,0:T(8,128)(2,1)} %bitcast.13, bf16[2560,1024]{1,0:T(8,128)(2,1)} %bitcast.14, bf16[2560,1024]{1,0:T(8,128)(2,1)} %bitcast.21, ...), custom_call_target="tpu_custom_call" | custom-call | flops 20132659200 | bytes 15728640 | tf_op jit(solution)/shard_map/pre_activations/up_sums/pallas_call | solution.py:152
  87.6 1.1 collective-permute-done.8.top
  88.7 5.9 %up_last.1 = (bf16[640,1024]{1,0:T(8,128)(2,1)}, bf16[640,1024]{1,0:T(8,128)(2,1)}) custom-call(s32[1]{0:T(128)} %bitcast.x_ref, bf16[320,640]{1,0:T(8,128)(2,1)S(1)} %collective-permute-done.8.top, bf16[320,640]{1,0:T(8,128)(2,1)S(1)} %collective-permute-done.9.bottom, f32[640,1024]{1,0:T(8,128)} %get-tuple-element.51.g_in, ...), custom_call_target="tpu_custom_call" | custom-call | flops 1677721600 | bytes 10485760 | tf_op jit(solution)/shard_map/pre_activations/up_last/pallas_call | solution.py:195
  94.6 2.9 %all-to-all-done.1 = bf16[64,80,128]{2,1,0:T(8,128)(2,1)S(1)} async-done(((bf16[64,80,128]{2,1,0:T(8,128)(2,1)}), bf16[64,80,128]{2,1,0:T(8,128)(2,1)S(1)}, u32[]{:S(2)}, u32[]{:S(2)}) %all-to-all-start.1) | async-done | bytes 1310752 | tf_op jit(solution)/shard_map/send_hidden/all_to_all | solution.py:346
  97.5 0.6 reshape.28.h
  98.1 4.7 %down_first.1 = (bf16[640,1024]{1,0:T(8,128)(2,1)S(1)}, bf16[640,1024]{1,0:T(8,128)(2,1)S(1)}, bf16[320,640]{1,0:T(8,128)(2,1)S(1)}, bf16[320,640]{1,0:T(8,128)(2,1)S(1)}) custom-call(s32[1]{0:T(128)} %bitcast.x_ref, bf16[640,1024]{1,0:T(8,128)(2,1)S(1)} %reshape.28.h, bf16[640,1024]{1,0:T(8,128)(2,1)} %get-tuple-element.53.a, ...), custom_call_target="tpu_custom_call" | custom-call | flops 1677721600 | bytes 9175040 | tf_op jit(solution)/shard_map/input_partials/down_first/pallas_call | solution.py:230
  102.8 2.1 %collective-permute-start.14 = (bf16[320,640]{1,0:T(8,128)(2,1)S(1)}, bf16[320,640]{1,0:T(8,128)(2,1)S(1)}, u32[]{:S(2)}, u32[]{:S(2)}) collective-permute-start(bf16[320,640]{1,0:T(8,128)(2,1)S(1)} %get-tuple-element.64), channel_id=1, source_target_pairs={{0,3},{1,0},{2,1},{3,2},{4,7},{5,4},{6,5},{7,6},{8,11},{9,8},{10,9... | collective-permute-start | bytes 1228808 | tf_op jit(solution)/shard_map/sum_quarters/ppermute | solution.py:320
  104.9 4.2 %down_halves.5 = (bf16[320,640]{1,0:T(8,128)(2,1)S(1)}, bf16[320,640]{1,0:T(8,128)(2,1)S(1)}) custom-call(s32[1]{0:T(128)} %bitcast.x_ref, bf16[640,1024]{1,0:T(8,128)(2,1)S(1)} %get-tuple-element.55.gg, bf16[640,1024]{1,0:T(8,128)(2,1)S(1)} %get-tuple-element.56.gu, bf16[2560,1024]{1,0:T(8,128)(2,1)} %bitcast.17, bf16[2560,1024]{1,0:T(8,128)(2,1)} %bitcast.25), custom_call_target="tpu_custom_call" | custom-call | flops 419430400 | bytes 7864320 | tf_op jit(solution)/shard_map/input_partials/down_halves/pallas_call | solution.py:270
  109.2 3.3 %collective-permute-start.12 = (bf16[320,640]{1,0:T(8,128)(2,1)S(1)}, bf16[320,640]{1,0:T(8,128)(2,1)S(1)}, u32[]{:S(2)}, u32[]{:S(2)}) collective-permute-start(bf16[320,640]{1,0:T(8,128)(2,1)S(1)} %get-tuple-element.60), channel_id=1, source_target_pairs={{0,3},{1,0},{2,1},{3,2},{4,7},{5,4},{6,5},{7,6},{8,11},{9,8},{10,9... | collective-permute-start | bytes 1228808 | tf_op jit(solution)/shard_map/sum_quarters/ppermute | solution.py:320
  112.5 0.0 collective-permute-start.13
  112.5 4.2 %down_halves.4 = (f32[320,640]{1,0:T(8,128)S(1)}, f32[320,640]{1,0:T(8,128)S(1)}) custom-call(s32[1]{0:T(128)} %bitcast.x_ref, bf16[640,1024]{1,0:T(8,128)(2,1)S(1)} %get-tuple-element.55.gg, bf16[640,1024]{1,0:T(8,128)(2,1)S(1)} %get-tuple-element.56.gu, bf16[2560,1024]{1,0:T(8,128)(2,1)} %bitcast.18, bf16[2560,1024]{1,0:T(8,128)(2,1)} %bitcast.26), custom_call_target="tpu_custom_call" | custom-call | flops 419430400 | bytes 7864320 | tf_op jit(solution)/shard_map/input_partials/down_halves/pallas_call | solution.py:270
  116.7 0.1 add_convert_fusion
  116.8 3.3 %collective-permute-start.15 = (bf16[320,640]{1,0:T(8,128)(2,1)S(1)}, bf16[320,640]{1,0:T(8,128)(2,1)S(1)}, u32[]{:S(2)}, u32[]{:S(2)}) collective-permute-start(bf16[320,640]{1,0:T(8,128)(2,1)S(1)} %add_convert_fusion), channel_id=1, source_target_pairs={{0,3},{1,0},{2,1},{3,2},{4,7},{5,4},{6,5},{7,6},{8,11},{9,8},{10,9... | collective-permute-start | bytes 1228808 | tf_op jit(solution)/shard_map/sum_quarters/ppermute | solution.py:320
  120.1 0.1 add_convert_fusion.1
  120.2 0.1 collective-permute-start.11
  120.3 4.2 %down_halves.3 = (f32[320,640]{1,0:T(8,128)S(1)}, f32[320,640]{1,0:T(8,128)S(1)}) custom-call(s32[1]{0:T(128)} %bitcast.x_ref, bf16[640,1024]{1,0:T(8,128)(2,1)S(1)} %get-tuple-element.55.gg, bf16[640,1024]{1,0:T(8,128)(2,1)S(1)} %get-tuple-element.56.gu, bf16[2560,1024]{1,0:T(8,128)(2,1)} %bitcast.19, bf16[2560,1024]{1,0:T(8,128)(2,1)} %bitcast.27), custom_call_target="tpu_custom_call" | custom-call | flops 419430400 | bytes 7864320 | tf_op jit(solution)/shard_map/input_partials/down_halves/pallas_call | solution.py:270
  124.6 1.8 %collective-permute-done.13.refs_4_ = bf16[320,640]{1,0:T(8,128)(2,1)S(1)} collective-permute-done((bf16[320,640]{1,0:T(8,128)(2,1)S(1)}, bf16[320,640]{1,0:T(8,128)(2,1)S(1)}, u32[]{:S(2)}, u32[]{:S(2)}) %collective-permute-start.13) | collective-permute-done | bytes 409632 | tf_op jit(solution)/shard_map/sum_quarters/ppermute | solution.py:323
  126.4 4.1 %collective-permute-done.15.refs_5_ = bf16[320,640]{1,0:T(8,128)(2,1)S(1)} collective-permute-done((bf16[320,640]{1,0:T(8,128)(2,1)S(1)}, bf16[320,640]{1,0:T(8,128)(2,1)S(1)}, u32[]{:S(2)}, u32[]{:S(2)}) %collective-permute-start.15) | collective-permute-done | bytes 409632 | tf_op jit(solution)/shard_map/sum_quarters/ppermute | solution.py:320
  130.5 3.0 %collective-permute-done.11.refs_1_ = bf16[320,640]{1,0:T(8,128)(2,1)S(1)} collective-permute-done((bf16[320,640]{1,0:T(8,128)(2,1)S(1)}, bf16[320,640]{1,0:T(8,128)(2,1)S(1)}, u32[]{:S(2)}, u32[]{:S(2)}) %collective-permute-start.11) | collective-permute-done | bytes 409632 | tf_op jit(solution)/shard_map/sum_quarters/ppermute | solution.py:323
  133.5 0.3 sum_halves.1
  133.7 0.3 reshape.30
  134.1 30.2 %all_to_all.15 = bf16[64,5,2,640]{3,2,1,0:T(2,128)(2,1)S(1)} all-to-all(bf16[64,5,2,640]{3,2,1,0:T(2,128)(2,1)S(1)} %reshape.30), channel_id=1, replica_groups=mesh['expert'=64,'etp'=4] {'expert'}, dimensions={0} | all-to-all | bytes 1638400 | tf_op jit(solution)/shard_map/return_tokens/all_to_all | solution.py:346
  164.2 0.3 reshape.31
  164.5 0.8 convolution_convert_fusion.2
  165.4 0.1 fusion.19
  165.4 0.1 collective-permute-start.18
  165.5 1.7 collective-permute-start.17
  167.3 0.4 collective-permute-start.16
  167.6 6.4 %collective-permute-done.18.b3 = bf16[128,640]{1,0:T(8,128)(2,1)S(1)} collective-permute-done((bf16[128,640]{1,0:T(8,128)(2,1)S(1)}, bf16[128,640]{1,0:T(8,128)(2,1)S(1)}, u32[]{:S(2)}, u32[]{:S(2)}) %collective-permute-start.18) | collective-permute-done | bytes 163872 | tf_op jit(solution)/shard_map/return_tokens/ppermute | solution.py:323
  174.1 1.7 collective-permute-done.16.b1
  175.8 0.9 join_columns.1
  (14 shorter events, 0.1 us)
Async XLA Ops:
  0.0 6.4 %copy-start.1 = (s32[128,1]{0,1:T(1,128)S(1)}, s32[128,1]{0,1:T(1,128)}, u32[]{:S(2)}) copy-start(s32[128,1]{0,1:T(1,128)} %param.8) | copy-start | bytes 1540
  1.2 15.6 %collective-permute-start = (bf16[128,640]{1,0:T(8,128)(2,1)S(1)}, bf16[128,640]{1,0:T(8,128)(2,1)S(1)}, u32[]{:S(2)}, u32[]{:S(2)}) collective-permute-start(bf16[128,640]{1,0:T(8,128)(2,1)S(1)} %get-tuple-element.36), channel_id=1, source_target_pairs={{0,2},{1,3},{2,0},{3,1},{4,6},{5,7},{6,4},{7,5},{8,10},{9,11},{10,... | collective-permute-start | bytes 491528 | tf_op jit(solution)/shard_map/group_exchange/ppermute | solution.py:320
  4.3 12.5 %collective-permute-start.1 = (bf16[128,640]{1,0:T(8,128)(2,1)S(1)}, bf16[128,640]{1,0:T(8,128)(2,1)S(1)}, u32[]{:S(2)}, u32[]{:S(2)}) collective-permute-start(bf16[128,640]{1,0:T(8,128)(2,1)S(1)} %get-tuple-element.37), channel_id=1, source_target_pairs={{0,3},{1,0},{2,1},{3,2},{4,7},{5,4},{6,5},{7,6},{8,11},{9,8},{10,9... | collective-permute-start | bytes 491528 | tf_op jit(solution)/shard_map/group_exchange/ppermute | solution.py:320
  5.5 11.4 %collective-permute-start.2 = (bf16[128,640]{1,0:T(8,128)(2,1)S(1)}, bf16[128,640]{1,0:T(8,128)(2,1)S(1)}, u32[]{:S(2)}, u32[]{:S(2)}) collective-permute-start(bf16[128,640]{1,0:T(8,128)(2,1)S(1)} %get-tuple-element.38), channel_id=1, source_target_pairs={{0,1},{1,2},{2,3},{3,0},{4,5},{5,6},{6,7},{7,4},{8,9},{9,10},{10,1... | collective-permute-start | bytes 491528 | tf_op jit(solution)/shard_map/group_exchange/ppermute | solution.py:320
  17.6 13.3 %copy-start.2 = (s32[128]{0:T(128)S(1)}, s32[128]{0:T(128)}, u32[]{:S(2)}) copy-start(s32[128]{0:T(128)} %param.9) | copy-start | bytes 1540
  18.8 36.0 %all-to-all-start = ((bf16[64,5,2,640]{3,2,1,0:T(2,128)(2,1)}), bf16[64,5,2,640]{3,2,1,0:T(2,128)(2,1)S(1)}, u32[]{:S(2)}, u32[]{:S(2)}) async-start(bf16[64,5,2,640]{3,2,1,0:T(2,128)(2,1)} %reshape.26), calls=%async_computation | async-start | bytes 1638400 | tf_op jit(solution)/shard_map/send_tokens/all_to_all | solution.py:346
  32.5 10.8 %collective-permute-start.3 = (bf16[128,1024]{1,0:T(8,128)(2,1)S(1)}, bf16[128,1024]{1,0:T(8,128)(2,1)S(1)}, u32[]{:S(2)}, u32[]{:S(2)}) collective-permute-start(bf16[128,1024]{1,0:T(8,128)(2,1)S(1)} %get-tuple-element.40), channel_id=1, source_target_pairs={{0,2},{1,3},{2,0},{3,1},{4,6},{5,7},{6,4},{7,5},{8,10},{9,11},{10,... | collective-permute-start | bytes 786440 | tf_op jit(solution)/shard_map/group_exchange/ppermute | solution.py:320
  33.4 12.8 %collective-permute-start.4 = (bf16[128,1024]{1,0:T(8,128)(2,1)S(1)}, bf16[128,1024]{1,0:T(8,128)(2,1)S(1)}, u32[]{:S(2)}, u32[]{:S(2)}) collective-permute-start(bf16[128,1024]{1,0:T(8,128)(2,1)S(1)} %get-tuple-element.41), channel_id=1, source_target_pairs={{0,3},{1,0},{2,1},{3,2},{4,7},{5,4},{6,5},{7,6},{8,11},{9,8},{10,9... | collective-permute-start | bytes 786440 | tf_op jit(solution)/shard_map/group_exchange/ppermute | solution.py:320
  35.0 13.1 %collective-permute-start.5 = (bf16[128,1024]{1,0:T(8,128)(2,1)S(1)}, bf16[128,1024]{1,0:T(8,128)(2,1)S(1)}, u32[]{:S(2)}, u32[]{:S(2)}) collective-permute-start(bf16[128,1024]{1,0:T(8,128)(2,1)S(1)} %get-tuple-element.42), channel_id=1, source_target_pairs={{0,1},{1,2},{2,3},{3,0},{4,5},{5,6},{6,7},{7,4},{8,9},{9,10},{10,1... | collective-permute-start | bytes 786440 | tf_op jit(solution)/shard_map/group_exchange/ppermute | solution.py:320
  55.1 19.4 %collective-permute-start.7 = (bf16[640,640]{1,0:T(8,128)(2,1)S(1)}, bf16[640,640]{1,0:T(8,128)(2,1)S(1)}, u32[]{:S(2)}, u32[]{:S(2)}) collective-permute-start(bf16[640,640]{1,0:T(8,128)(2,1)S(1)} %reshape.29.refs_0_), channel_id=1, source_target_pairs={{0,3},{1,0},{2,1},{3,2},{4,7},{5,4},{6,5},{7,6},{8,11},{9,8},{10,9... | collective-permute-start | bytes 2457608 | tf_op jit(solution)/shard_map/gather_width/ppermute | solution.py:320
  56.0 20.4 %collective-permute-start.6 = (bf16[640,640]{1,0:T(8,128)(2,1)S(1)}, bf16[640,640]{1,0:T(8,128)(2,1)}, u32[]{:S(2)}, u32[]{:S(2)}) collective-permute-start(bf16[640,640]{1,0:T(8,128)(2,1)S(1)} %reshape.29.refs_0_), channel_id=1, source_target_pairs={{0,1},{1,2},{2,3},{3,0},{4,5},{5,6},{6,7},{7,4},{8,9},{9,10},{10,1... | collective-permute-start | bytes 2457608 | tf_op jit(solution)/shard_map/gather_width/ppermute | solution.py:323
  57.2 40.3 %all-to-all-start.1 = ((bf16[64,80,128]{2,1,0:T(8,128)(2,1)}), bf16[64,80,128]{2,1,0:T(8,128)(2,1)S(1)}, u32[]{:S(2)}, u32[]{:S(2)}) async-start(bf16[64,80,128]{2,1,0:T(8,128)(2,1)} %reshape.27), calls=%async_computation.1 | async-start | bytes 2621440 | tf_op jit(solution)/shard_map/send_hidden/all_to_all | solution.py:346
  74.5 5.2 %copy-start = (bf16[640,640]{1,0:T(8,128)(2,1)}, bf16[640,640]{1,0:T(8,128)(2,1)S(1)}, u32[]{:S(2)}) copy-start(bf16[640,640]{1,0:T(8,128)(2,1)S(1)} %collective-permute-done.7.refs_0_) | copy-start | bytes 2457604
  77.4 10.2 %collective-permute-start.9 = (bf16[320,640]{1,0:T(8,128)(2,1)S(1)}, bf16[320,640]{1,0:T(8,128)(2,1)S(1)}, u32[]{:S(2)}, u32[]{:S(2)}) collective-permute-start(bf16[320,640]{1,0:T(8,128)(2,1)S(1)} %slice.19), channel_id=1, source_target_pairs={{0,3},{1,0},{2,1},{3,2},{4,7},{5,4},{6,5},{7,6},{8,11},{9,8},{10,9... | collective-permute-start | bytes 1228808 | tf_op jit(solution)/shard_map/gather_width/ppermute | solution.py:320
  78.2 10.6 %collective-permute-start.8 = (bf16[320,640]{1,0:T(8,128)(2,1)S(1)}, bf16[320,640]{1,0:T(8,128)(2,1)S(1)}, u32[]{:S(2)}, u32[]{:S(2)}) collective-permute-start(bf16[320,640]{1,0:T(8,128)(2,1)S(1)} %slice.18), channel_id=1, source_target_pairs={{0,1},{1,2},{2,3},{3,0},{4,5},{5,6},{6,7},{7,4},{8,9},{9,10},{10,1... | collective-permute-start | bytes 1228808 | tf_op jit(solution)/shard_map/gather_width/ppermute | solution.py:323
  102.8 13.9 %collective-permute-start.14 = (bf16[320,640]{1,0:T(8,128)(2,1)S(1)}, bf16[320,640]{1,0:T(8,128)(2,1)S(1)}, u32[]{:S(2)}, u32[]{:S(2)}) collective-permute-start(bf16[320,640]{1,0:T(8,128)(2,1)S(1)} %get-tuple-element.64), channel_id=1, source_target_pairs={{0,3},{1,0},{2,1},{3,2},{4,7},{5,4},{6,5},{7,6},{8,11},{9,8},{10,9... | collective-permute-start | bytes 1228808 | tf_op jit(solution)/shard_map/sum_quarters/ppermute | solution.py:320
  104.9 15.2 %collective-permute-start.10 = (bf16[320,640]{1,0:T(8,128)(2,1)S(1)}, bf16[320,640]{1,0:T(8,128)(2,1)S(1)}, u32[]{:S(2)}, u32[]{:S(2)}) collective-permute-start(bf16[320,640]{1,0:T(8,128)(2,1)S(1)} %get-tuple-element.59), channel_id=1, source_target_pairs={{0,1},{1,2},{2,3},{3,0},{4,5},{5,6},{6,7},{7,4},{8,9},{9,10},{10,1... | collective-permute-start | bytes 1228808 | tf_op jit(solution)/shard_map/sum_quarters/ppermute | solution.py:323
  109.2 15.4 %collective-permute-start.12 = (bf16[320,640]{1,0:T(8,128)(2,1)S(1)}, bf16[320,640]{1,0:T(8,128)(2,1)S(1)}, u32[]{:S(2)}, u32[]{:S(2)}) collective-permute-start(bf16[320,640]{1,0:T(8,128)(2,1)S(1)} %get-tuple-element.60), channel_id=1, source_target_pairs={{0,3},{1,0},{2,1},{3,2},{4,7},{5,4},{6,5},{7,6},{8,11},{9,8},{10,9... | collective-permute-start | bytes 1228808 | tf_op jit(solution)/shard_map/sum_quarters/ppermute | solution.py:320
  112.5 13.9 %collective-permute-start.13 = (bf16[320,640]{1,0:T(8,128)(2,1)S(1)}, bf16[320,640]{1,0:T(8,128)(2,1)S(1)}, u32[]{:S(2)}, u32[]{:S(2)}) collective-permute-start(bf16[320,640]{1,0:T(8,128)(2,1)S(1)} %get-tuple-element.62), channel_id=1, source_target_pairs={{0,1},{1,2},{2,3},{3,0},{4,5},{5,6},{6,7},{7,4},{8,9},{9,10},{10,1... | collective-permute-start | bytes 1228808 | tf_op jit(solution)/shard_map/sum_quarters/ppermute | solution.py:323
  116.8 13.7 %collective-permute-start.15 = (bf16[320,640]{1,0:T(8,128)(2,1)S(1)}, bf16[320,640]{1,0:T(8,128)(2,1)S(1)}, u32[]{:S(2)}, u32[]{:S(2)}) collective-permute-start(bf16[320,640]{1,0:T(8,128)(2,1)S(1)} %add_convert_fusion), channel_id=1, source_target_pairs={{0,3},{1,0},{2,1},{3,2},{4,7},{5,4},{6,5},{7,6},{8,11},{9,8},{10,9... | collective-permute-start | bytes 1228808 | tf_op jit(solution)/shard_map/sum_quarters/ppermute | solution.py:320
  120.2 13.2 %collective-permute-start.11 = (bf16[320,640]{1,0:T(8,128)(2,1)S(1)}, bf16[320,640]{1,0:T(8,128)(2,1)S(1)}, u32[]{:S(2)}, u32[]{:S(2)}) collective-permute-start(bf16[320,640]{1,0:T(8,128)(2,1)S(1)} %add_convert_fusion.1), channel_id=1, source_target_pairs={{0,1},{1,2},{2,3},{3,0},{4,5},{5,6},{6,7},{7,4},{8,9},{9,10},{10,1... | collective-permute-start | bytes 1228808 | tf_op jit(solution)/shard_map/sum_quarters/ppermute | solution.py:323
  165.4 8.6 %collective-permute-start.18 = (bf16[128,640]{1,0:T(8,128)(2,1)S(1)}, bf16[128,640]{1,0:T(8,128)(2,1)S(1)}, u32[]{:S(2)}, u32[]{:S(2)}) collective-permute-start(bf16[128,640]{1,0:T(8,128)(2,1)S(1)} %get-tuple-element.65), channel_id=1, source_target_pairs={{0,2},{1,3},{2,0},{3,1},{4,6},{5,7},{6,4},{7,5},{8,10},{9,11},{10,... | collective-permute-start | bytes 491528 | tf_op jit(solution)/shard_map/return_tokens/ppermute | solution.py:323
  165.5 8.5 %collective-permute-start.17 = (bf16[128,640]{1,0:T(8,128)(2,1)S(1)}, bf16[128,640]{1,0:T(8,128)(2,1)S(1)}, u32[]{:S(2)}, u32[]{:S(2)}) collective-permute-start(bf16[128,640]{1,0:T(8,128)(2,1)S(1)} %get-tuple-element.66), channel_id=1, source_target_pairs={{0,3},{1,0},{2,1},{3,2},{4,7},{5,4},{6,5},{7,6},{8,11},{9,8},{10,9... | collective-permute-start | bytes 491528 | tf_op jit(solution)/shard_map/return_tokens/ppermute | solution.py:323
  167.3 8.6 %collective-permute-start.16 = (bf16[128,640]{1,0:T(8,128)(2,1)S(1)}, bf16[128,640]{1,0:T(8,128)(2,1)S(1)}, u32[]{:S(2)}, u32[]{:S(2)}) collective-permute-start(bf16[128,640]{1,0:T(8,128)(2,1)S(1)} %get-tuple-element.67), channel_id=1, source_target_pairs={{0,1},{1,2},{2,3},{3,0},{4,5},{5,6},{6,7},{7,4},{8,9},{9,10},{10,1... | collective-permute-start | bytes 491528 | tf_op jit(solution)/shard_map/return_tokens/ppermute | solution.py:323
